TPU v7x, 32 devices: a whole 2x2x4 slice. The times are simulated.
32 devices in a mesh: fsdp: 16 (over z, x, core), dp: 2 (over y).
Axes of the slice: x: 2, y: 2, z: 4, core: 2. Of those that a mesh axis runs over, the one named last changes fastest.
Arguments:
- tokens: bfloat16 [24576, 1024], P(('fsdp', 'dp')), may hold values from -6 to 6
- cotangent: bfloat16 [24576, 1024], P(('fsdp', 'dp')), may hold values from -6 to 6
- segments: int32 [24576], replicated, may hold values from 0 to 47, never falling along the last dimension, each value on 1 to 577 neighbouring positions
- adapter_ids: int32 [48], replicated, may hold values from 0 to 7
- ln1_gain: float32 [1024], replicated, may hold values from 0.5 to 1.5
- ln1_bias: float32 [1024], replicated, may hold values from -1.5 to 1.5
- w_query: bfloat16 [1024, 1024], P(('fsdp', 'dp')), may hold values from -0.1875 to 0.1875
- b_query: float32 [1024], replicated, may hold values from -2.5 to 2.5
- w_key: bfloat16 [1024, 1024], P(('fsdp', 'dp')), may hold values from -0.1875 to 0.1875
- w_value: bfloat16 [1024, 1024], P(('fsdp', 'dp')), may hold values from -0.1875 to 0.1875
- b_value: float32 [1024], replicated, may hold values from -2.5 to 2.5
- w_out: bfloat16 [1024, 1024], P(('fsdp', 'dp')), may hold values from -4 to 4
- b_out: float32 [1024], replicated, may hold values from -2.5 to 2.5
- ln2_gain: float32 [1024], replicated, may hold values from 0.5 to 1.5
- ln2_bias: float32 [1024], replicated, may hold values from -1.5 to 1.5
- w_up: bfloat16 [1024, 4096], P(('fsdp', 'dp')), may hold values from -0.1875 to 0.1875
- b_up: float32 [4096], replicated, may hold values from -2.5 to 2.5
- w_down: bfloat16 [4096, 1024], P(('fsdp', 'dp')), may hold values from -0.1875 to 0.1875
- b_down: float32 [1024], replicated, may hold values from -2.5 to 2.5
- query_in: bfloat16 [1024, 128], P(('fsdp', 'dp')), may hold values from -0.1875 to 0.1875
- query_out: bfloat16 [1024, 128], P(('fsdp', 'dp')), may hold values from -0.75 to 0.75
- value_in: bfloat16 [1024, 128], P(('fsdp', 'dp')), may hold values from -0.1875 to 0.1875
- value_out: bfloat16 [1024, 128], P(('fsdp', 'dp')), may hold values from -0.75 to 0.75
- up_in: bfloat16 [1024, 128], P(('fsdp', 'dp')), may hold values from -0.1875 to 0.1875
- up_out: bfloat16 [4096, 128], P(('fsdp', 'dp')), may hold values from -0.75 to 0.75
- down_in: bfloat16 [4096, 128], P(('fsdp', 'dp')), may hold values from -0.1875 to 0.1875
- down_out: bfloat16 [1024, 128], P(('fsdp', 'dp')), may hold values from -0.75 to 0.75
Outputs:
- block_out: bfloat16 [24576, 1024], P(('fsdp', 'dp'))
- grad_input: bfloat16 [24576, 1024], P(('fsdp', 'dp'))
- grad_query_in: float32 [1024, 128], P(('fsdp', 'dp'))
- grad_query_out: float32 [1024, 128], P(('fsdp', 'dp'))
- grad_value_in: float32 [1024, 128], P(('fsdp', 'dp'))
- grad_value_out: float32 [1024, 128], P(('fsdp', 'dp'))
- grad_up_in: float32 [1024, 128], P(('fsdp', 'dp'))
- grad_up_out: float32 [4096, 128], P(('fsdp', 'dp'))
- grad_down_in: float32 [4096, 128], P(('fsdp', 'dp'))
- grad_down_out: float32 [1024, 128], P(('fsdp', 'dp'))
Inputs may be any that keep to these rules, and one draw needn't show every extreme that they name: `segments`: image numbers never fall along the packed order; each image holds 1 to 577 consecutive tokens, and one holds exactly 577.
All inputs are finite; a program needn't handle non-finite values.
Results may differ from a plain program's by a relative error of at most 0.014.
Values may be sent and summed in bfloat16 or wider, within the bound.
No kernel may reach another device: no remote copies, remote signals or barrier semaphores. Data moves between devices by JAX's collectives and lax.ppermute only.
A program may use at most 384 MiB of HBM per device.

v0:
```python
import jax
import jax.numpy as jnp
from jax import lax
from jax.sharding import PartitionSpec as P

HEADS = 16
HALO = 576
RANK = 16
ADAPTERS = 8


epsilon = 1e-05
gelu_slope = 1.702


def extended(array, sides, width):
    for axis, dim in sides:
        devices, length = (lax.axis_size(axis), array.shape[dim])
        up = [(i, (i + 1) % devices) for i in range(devices - 1)]
        down = [(j, i) for i, j in up]
        last = lax.slice_in_dim(array, length - width, length, axis=dim)
        first = lax.slice_in_dim(array, 0, width, axis=dim)
        before = lax.ppermute(last, axis, up)
        after = lax.ppermute(first, axis, down)
        array = jnp.concatenate([before, array, after], axis=dim)
    return array


def from_behind(value, axis, steps):
    count = lax.axis_size(axis)
    first, last = (max(0, -steps), min(count, count - steps))
    return lax.ppermute(value, axis, [(source, source + steps) for source in range(first, last)])


def product(left, right):
    return jnp.dot(left, right, preferred_element_type=jnp.float32)


def times_transposed(left, right):
    return lax.dot_general(
        left, right, (((1,), (1,)), ((), ())), preferred_element_type=jnp.float32
    )


def transposed_times(left, right):
    return lax.dot_general(
        left, right, (((0,), (0,)), ((), ())), preferred_element_type=jnp.float32
    )


def norm_forward(values, gain, shift):
    mean = jnp.mean(values, axis=1, keepdims=True)
    centered = values - mean
    inverse = lax.rsqrt(jnp.mean(centered * centered, axis=1, keepdims=True) + epsilon)
    normed = centered * inverse
    return (normed * gain + shift, normed, inverse)


def norm_backward(grad, normed, inverse, gain):
    scaled = grad * gain
    return inverse * (
        scaled
        - jnp.mean(scaled, axis=1, keepdims=True)
        - normed * jnp.mean(scaled * normed, axis=1, keepdims=True)
    )


def split_heads(block, head_dim):
    return block.reshape(block.shape[0], block.shape[1] // head_dim, head_dim)


def group_scores(query3, key3, same_image, score_scale):
    raw = jnp.einsum("qhd,khd->hqk", query3, key3, preferred_element_type=jnp.float32) * score_scale
    return jnp.where(same_image[None], raw, -1000000000.0)


def local(
    tokens,
    cotangent,
    segments,
    adapter_ids,
    ln1_gain,
    ln1_bias,
    w_query,
    b_query,
    w_key,
    w_value,
    b_value,
    w_out,
    b_out,
    ln2_gain,
    ln2_bias,
    w_up,
    b_up,
    w_down,
    b_down,
    query_in,
    query_out,
    value_in,
    value_out,
    up_in,
    up_out,
    down_in,
    down_out,
):
    row_count, model_width = tokens.shape
    head_dim = model_width // HEADS
    score_scale = head_dim ** (-0.5)
    group_count = max(1, HEADS // 4)
    group_width = model_width // group_count
    gathered = (
        lax.all_gather(w_query, ("fsdp", "dp"), axis=0, tiled=True),
        lax.all_gather(w_key, ("fsdp", "dp"), axis=0, tiled=True),
        lax.all_gather(w_value, ("fsdp", "dp"), axis=0, tiled=True),
        lax.all_gather(w_out, ("fsdp", "dp"), axis=0, tiled=True),
        lax.all_gather(w_up, ("fsdp", "dp"), axis=0, tiled=True),
        lax.all_gather(w_down, ("fsdp", "dp"), axis=0, tiled=True),
        lax.all_gather(query_in, ("fsdp", "dp"), axis=0, tiled=True),
        lax.all_gather(query_out, ("fsdp", "dp"), axis=0, tiled=True),
        lax.all_gather(value_in, ("fsdp", "dp"), axis=0, tiled=True),
        lax.all_gather(value_out, ("fsdp", "dp"), axis=0, tiled=True),
        lax.all_gather(up_in, ("fsdp", "dp"), axis=0, tiled=True),
        lax.all_gather(up_out, ("fsdp", "dp"), axis=0, tiled=True),
        lax.all_gather(down_in, ("fsdp", "dp"), axis=0, tiled=True),
        lax.all_gather(down_out, ("fsdp", "dp"), axis=0, tiled=True),
    )
    (
        full_wq,
        full_wk,
        full_wv,
        full_wo,
        full_wup,
        full_wdown,
        full_qin,
        full_qout,
        full_vin,
        full_vout,
        full_uin,
        full_uout,
        full_din,
        full_dout,
    ) = gathered
    position = lax.axis_index(("fsdp", "dp"))
    padded_seg = jnp.pad(segments, HALO, constant_values=-1)
    seg_window = lax.dynamic_slice_in_dim(padded_seg, position * row_count, row_count + 2 * HALO, 0)
    seg_own = lax.dynamic_slice_in_dim(segments, position * row_count, row_count, 0)
    same_image = seg_own[:, None] == seg_window[None, :]
    image_hot = (
        seg_own[:, None] == jnp.arange(adapter_ids.shape[0], dtype=jnp.int32)[None, :]
    ).astype(jnp.bfloat16)
    adapter_hot = (adapter_ids[:, None] == jnp.arange(ADAPTERS, dtype=jnp.int32)[None, :]).astype(
        jnp.bfloat16
    )
    select = jnp.repeat(product(image_hot, adapter_hot), RANK, axis=1).astype(jnp.bfloat16)
    tokens_f = tokens.astype(jnp.float32)
    normal1, hat_one, inv_one = norm_forward(tokens_f, ln1_gain, ln1_bias)
    normed1 = normal1.astype(jnp.bfloat16)
    low_q = product(normed1, full_qin).astype(jnp.bfloat16) * select
    low_v = product(normed1, full_vin).astype(jnp.bfloat16) * select
    query = (product(normed1, full_wq) + b_query + times_transposed(low_q, full_qout)).astype(
        jnp.bfloat16
    )
    keys = product(normed1, full_wk).astype(jnp.bfloat16)
    values = (product(normed1, full_wv) + b_value + times_transposed(low_v, full_vout)).astype(
        jnp.bfloat16
    )
    window = extended(jnp.concatenate([keys, values], axis=1), ((("fsdp", "dp"), 0),), HALO)
    key_window = window[:, :model_width]
    value_window = window[:, model_width:]
    mixed_parts = []
    log_totals = []
    for head_group in range(group_count):
        first = head_group * group_width
        query3 = split_heads(query[:, first : first + group_width], head_dim)
        key3 = split_heads(key_window[:, first : first + group_width], head_dim)
        value3 = split_heads(value_window[:, first : first + group_width], head_dim)
        scores = group_scores(query3, key3, same_image, score_scale)
        row_max = jnp.max(scores, axis=2, keepdims=True)
        exp_scores = jnp.exp(scores - row_max)
        row_total = jnp.sum(exp_scores, axis=2, keepdims=True)
        softmax_w = (exp_scores / row_total).astype(jnp.bfloat16)
        log_totals.append(row_max + jnp.log(row_total))
        attended = jnp.einsum("hqk,khd->qhd", softmax_w, value3, preferred_element_type=jnp.float32)
        mixed_parts.append(attended.reshape(row_count, group_width))
    mixed = jnp.concatenate(mixed_parts, axis=1).astype(jnp.bfloat16)
    resid = tokens_f + product(mixed, full_wo) + b_out
    normal2, hat_two, inv_two = norm_forward(resid, ln2_gain, ln2_bias)
    normed2 = normal2.astype(jnp.bfloat16)
    low_u = product(normed2, full_uin).astype(jnp.bfloat16) * select
    pre_act = product(normed2, full_wup) + b_up + times_transposed(low_u, full_uout)
    gate_value = 1.0 / (1.0 + jnp.exp(-gelu_slope * pre_act))
    act = (pre_act * gate_value).astype(jnp.bfloat16)
    low_d = product(act, full_din).astype(jnp.bfloat16) * select
    result = resid + product(act, full_wdown) + b_down + times_transposed(low_d, full_dout)
    block_out = result.astype(jnp.bfloat16)
    again = (
        lax.all_gather(w_query, ("fsdp", "dp"), axis=0, tiled=True),
        lax.all_gather(w_key, ("fsdp", "dp"), axis=0, tiled=True),
        lax.all_gather(w_value, ("fsdp", "dp"), axis=0, tiled=True),
        lax.all_gather(w_out, ("fsdp", "dp"), axis=0, tiled=True),
        lax.all_gather(w_up, ("fsdp", "dp"), axis=0, tiled=True),
        lax.all_gather(w_down, ("fsdp", "dp"), axis=0, tiled=True),
        lax.all_gather(query_in, ("fsdp", "dp"), axis=0, tiled=True),
        lax.all_gather(query_out, ("fsdp", "dp"), axis=0, tiled=True),
        lax.all_gather(value_in, ("fsdp", "dp"), axis=0, tiled=True),
        lax.all_gather(value_out, ("fsdp", "dp"), axis=0, tiled=True),
        lax.all_gather(up_in, ("fsdp", "dp"), axis=0, tiled=True),
        lax.all_gather(up_out, ("fsdp", "dp"), axis=0, tiled=True),
        lax.all_gather(down_in, ("fsdp", "dp"), axis=0, tiled=True),
        lax.all_gather(down_out, ("fsdp", "dp"), axis=0, tiled=True),
    )
    (
        back_wq,
        back_wk,
        back_wv,
        back_wo,
        back_wup,
        back_wdown,
        back_qin,
        back_qout,
        back_vin,
        back_vout,
        back_uin,
        back_uout,
        back_din,
        back_dout,
    ) = again
    grad_down_out = transposed_times(cotangent, low_d)
    d_low_d = product(cotangent, back_dout).astype(jnp.bfloat16) * select
    grad_down_in = transposed_times(act, d_low_d)
    d_act = times_transposed(cotangent, back_wdown) + times_transposed(d_low_d, back_din)
    d_pre = (d_act * (gate_value + gelu_slope * pre_act * gate_value * (1.0 - gate_value))).astype(
        jnp.bfloat16
    )
    grad_up_out = transposed_times(d_pre, low_u)
    d_low_u = product(d_pre, back_uout).astype(jnp.bfloat16) * select
    grad_up_in = transposed_times(normed2, d_low_u)
    d_normed2 = times_transposed(d_pre, back_wup) + times_transposed(d_low_u, back_uin)
    d_resid = cotangent.astype(jnp.float32) + norm_backward(d_normed2, hat_two, inv_two, ln2_gain)
    d_attn = d_resid.astype(jnp.bfloat16)
    d_mixed = times_transposed(d_attn, back_wo).astype(jnp.bfloat16)
    query_grads = []
    key_grads = []
    value_grads = []
    for head_group in range(group_count):
        first = head_group * group_width
        query3 = split_heads(query[:, first : first + group_width], head_dim)
        key3 = split_heads(key_window[:, first : first + group_width], head_dim)
        value3 = split_heads(value_window[:, first : first + group_width], head_dim)
        d_out3 = split_heads(d_mixed[:, first : first + group_width], head_dim)
        scores = group_scores(query3, key3, same_image, score_scale)
        exact_probs = jnp.exp(scores - log_totals[head_group])
        softmax_w = exact_probs.astype(jnp.bfloat16)
        d_probs = jnp.einsum("qhd,khd->hqk", d_out3, value3, preferred_element_type=jnp.float32)
        row_delta = jnp.sum(exact_probs * d_probs, axis=2, keepdims=True)
        d_scores = (exact_probs * (d_probs - row_delta)).astype(jnp.bfloat16)
        grad_q3 = (
            jnp.einsum("hqk,khd->qhd", d_scores, key3, preferred_element_type=jnp.float32)
            * score_scale
        )
        grad_k3 = (
            jnp.einsum("hqk,qhd->khd", d_scores, query3, preferred_element_type=jnp.float32)
            * score_scale
        )
        grad_v3 = jnp.einsum("hqk,qhd->khd", softmax_w, d_out3, preferred_element_type=jnp.float32)
        query_grads.append(grad_q3.reshape(row_count, group_width))
        key_grads.append(grad_k3.reshape(grad_k3.shape[0], group_width))
        value_grads.append(grad_v3.reshape(grad_v3.shape[0], group_width))
    d_query = jnp.concatenate(query_grads, axis=1).astype(jnp.bfloat16)
    d_kv_window = jnp.concatenate(key_grads + value_grads, axis=1)
    from_right = from_behind(d_kv_window[:HALO].astype(jnp.bfloat16), ("fsdp", "dp"), -1).astype(
        jnp.float32
    )
    from_left = from_behind(
        d_kv_window[row_count + HALO :].astype(jnp.bfloat16), ("fsdp", "dp"), 1
    ).astype(jnp.float32)
    d_kv_own = d_kv_window[HALO : HALO + row_count]
    d_kv_own = (
        d_kv_own
        + jnp.pad(from_left, ((0, row_count - HALO), (0, 0)))
        + jnp.pad(from_right, ((row_count - HALO, 0), (0, 0)))
    )
    d_keys = d_kv_own[:, :model_width].astype(jnp.bfloat16)
    d_values = d_kv_own[:, model_width:].astype(jnp.bfloat16)
    grad_query_out = transposed_times(d_query, low_q)
    grad_value_out = transposed_times(d_values, low_v)
    d_low_q = product(d_query, back_qout).astype(jnp.bfloat16) * select
    d_low_v = product(d_values, back_vout).astype(jnp.bfloat16) * select
    grad_query_in = transposed_times(normed1, d_low_q)
    grad_value_in = transposed_times(normed1, d_low_v)
    d_normed1 = (
        times_transposed(d_query, back_wq)
        + times_transposed(d_keys, back_wk)
        + times_transposed(d_values, back_wv)
    )
    d_normed1 = (
        d_normed1 + times_transposed(d_low_q, back_qin) + times_transposed(d_low_v, back_vin)
    )
    grad_input = (d_resid + norm_backward(d_normed1, hat_one, inv_one, ln1_gain)).astype(
        jnp.bfloat16
    )
    summed = (
        lax.psum_scatter(grad_query_in, ("fsdp", "dp"), scatter_dimension=0, tiled=True),
        lax.psum_scatter(grad_query_out, ("fsdp", "dp"), scatter_dimension=0, tiled=True),
        lax.psum_scatter(grad_value_in, ("fsdp", "dp"), scatter_dimension=0, tiled=True),
        lax.psum_scatter(grad_value_out, ("fsdp", "dp"), scatter_dimension=0, tiled=True),
        lax.psum_scatter(grad_up_in, ("fsdp", "dp"), scatter_dimension=0, tiled=True),
        lax.psum_scatter(grad_up_out, ("fsdp", "dp"), scatter_dimension=0, tiled=True),
        lax.psum_scatter(grad_down_in, ("fsdp", "dp"), scatter_dimension=0, tiled=True),
        lax.psum_scatter(grad_down_out, ("fsdp", "dp"), scatter_dimension=0, tiled=True),
    )
    return (
        block_out,
        grad_input,
        summed[0],
        summed[1],
        summed[2],
        summed[3],
        summed[4],
        summed[5],
        summed[6],
        summed[7],
    )


def solution(mesh):
    return jax.shard_map(
        local,
        mesh=mesh,
        in_specs=(
            P(("fsdp", "dp"), None),
            P(("fsdp", "dp"), None),
            P(),
            P(),
            P(),
            P(),
            P(("fsdp", "dp"), None),
            P(),
            P(("fsdp", "dp"), None),
            P(("fsdp", "dp"), None),
            P(),
            P(("fsdp", "dp"), None),
            P(),
            P(),
            P(),
            P(("fsdp", "dp"), None),
            P(),
            P(("fsdp", "dp"), None),
            P(),
            P(("fsdp", "dp"), None),
            P(("fsdp", "dp"), None),
            P(("fsdp", "dp"), None),
            P(("fsdp", "dp"), None),
            P(("fsdp", "dp"), None),
            P(("fsdp", "dp"), None),
            P(("fsdp", "dp"), None),
            P(("fsdp", "dp"), None),
        ),
        out_specs=(
            P(("fsdp", "dp"), None),
            P(("fsdp", "dp"), None),
            P(("fsdp", "dp"), None),
            P(("fsdp", "dp"), None),
            P(("fsdp", "dp"), None),
            P(("fsdp", "dp"), None),
            P(("fsdp", "dp"), None),
            P(("fsdp", "dp"), None),
            P(("fsdp", "dp"), None),
            P(("fsdp", "dp"), None),
        ),
        check_vma=False,
    )
```

profile of v0, /device:TPU:0, one launch (start us, length us, event | category | flops | bytes accessed | tf_op | source)
XLA Modules:
  0.0 2053.9 jit_solution(11524287528089910341)
XLA Ops:
  16.4 76.2 %all_gather.61 = bf16[1024,128]{1,0:T(8,128)(2,1)} all-gather(bf16[32,128]{1,0:T(8,128)(2,1)S(1)} %copy-done.96), channel_id=1, replica_groups=mesh['fsdp'=16,'dp'=2] {'fsdp','dp'}, dimensions={0}, use_global_device_ids=true | all-gather | bytes 270336 | tf_op jit(solution)/shard_map/all_gather | solution.py:118
  92.6 70.0 %all_gather.62 = bf16[1024,128]{1,0:T(8,128)(2,1)} all-gather(bf16[32,128]{1,0:T(8,128)(2,1)S(1)} %copy-done.97), channel_id=1, replica_groups=mesh['fsdp'=16,'dp'=2] {'fsdp','dp'}, dimensions={0}, use_global_device_ids=true | all-gather | bytes 270336 | tf_op jit(solution)/shard_map/all_gather | solution.py:119
  162.6 67.6 %all_gather.58 = bf16[1024,128]{1,0:T(8,128)(2,1)S(1)} all-gather(bf16[32,128]{1,0:T(8,128)(2,1)S(1)} %copy-done.98), channel_id=1, replica_groups=mesh['fsdp'=16,'dp'=2] {'fsdp','dp'}, dimensions={0}, use_global_device_ids=true | all-gather | bytes 270336 | tf_op jit(solution)/shard_map/all_gather | solution.py:120
  230.2 70.7 %all_gather.59 = bf16[1024,128]{1,0:T(8,128)(2,1)} all-gather(bf16[32,128]{1,0:T(8,128)(2,1)S(1)} %copy-done.99), channel_id=1, replica_groups=mesh['fsdp'=16,'dp'=2] {'fsdp','dp'}, dimensions={0}, use_global_device_ids=true | all-gather | bytes 270336 | tf_op jit(solution)/shard_map/all_gather | solution.py:121
  300.9 73.3 %all_gather.65 = bf16[1024,128]{1,0:T(8,128)(2,1)} all-gather(bf16[32,128]{1,0:T(8,128)(2,1)S(1)} %copy-done.100), channel_id=1, replica_groups=mesh['fsdp'=16,'dp'=2] {'fsdp','dp'}, dimensions={0}, use_global_device_ids=true | all-gather | bytes 270336 | tf_op jit(solution)/shard_map/all_gather | solution.py:122
  394.6 160.8 %all_gather.69 = bf16[1024,128]{1,0:T(8,128)(2,1)S(1)} all-gather(bf16[32,128]{1,0:T(8,128)(2,1)S(1)} %copy-done.101), channel_id=1, replica_groups=mesh['fsdp'=16,'dp'=2] {'fsdp','dp'}, dimensions={0}, use_global_device_ids=true | all-gather | bytes 270336 | tf_op jit(solution)/shard_map/all_gather | solution.py:125
  732.0 12.3 fusion.97
  756.5 13.5 multiply_convert_fusion.5
  813.0 18.6 multiply_reduce_fusion
  831.5 15.7 multiply_convert_fusion
  865.0 18.8 multiply_reduce_fusion.1
  895.1 18.6 multiply_reduce_fusion.2
  925.1 18.6 multiply_reduce_fusion.3
  957.4 15.7 multiply_convert_fusion.1
  979.3 15.7 multiply_convert_fusion.2
  1001.1 15.8 multiply_convert_fusion.3
  1093.9 48.1 %collective-permute-done.2 = bf16[576,2048]{1,0:T(8,128)(2,1)} collective-permute-done((bf16[576,2048]{1,0:T(8,128)(2,1)}, bf16[576,2048]{1,0:T(8,128)(2,1)}, u32[]{:S(2)}, u32[]{:S(2)}) %collective-permute-start.2) | collective-permute-done | bytes 2359328 | tf_op jit(solution)/shard_map/ppermute | solution.py:32
  1193.1 41.3 %reduce-scatter.25.cloned.1.call-done = f32[32,128]{1,0:T(8,128)} async-done(((f32[1024,128]{1,0:T(8,128)}), f32[32,128]{1,0:T(8,128)}) %reduce-scatter.25.cloned.1.call-update) | async-done | bytes 16400
  1234.4 134.7 %reduce-scatter.13.cloned.1.call-done = f32[32,128]{1,0:T(8,128)} async-done(((f32[1024,128]{1,0:T(8,128)}), f32[32,128]{1,0:T(8,128)}) %reduce-scatter.13.cloned.1.call-update) | async-done | bytes 16400 | tf_op jit(solution)/shard_map/reduce_scatter | solution.py:304
  1369.1 134.3 %reduce-scatter.11.cloned.1.call-done = f32[32,128]{1,0:T(8,128)} async-done(((f32[1024,128]{1,0:T(8,128)}), f32[32,128]{1,0:T(8,128)}) %reduce-scatter.11.cloned.1.call-update) | async-done | bytes 16400 | tf_op jit(solution)/shard_map/reduce_scatter | solution.py:303
  1503.4 134.5 %reduce-scatter.15.cloned.1.call-done = f32[32,128]{1,0:T(8,128)} async-done(((f32[1024,128]{1,0:T(8,128)}), f32[32,128]{1,0:T(8,128)}) %reduce-scatter.15.cloned.1.call-update) | async-done | bytes 16400 | tf_op jit(solution)/shard_map/reduce_scatter | solution.py:305
  1637.9 134.3 %reduce-scatter.17.cloned.1.call-done = f32[32,128]{1,0:T(8,128)} async-done(((f32[1024,128]{1,0:T(8,128)}), f32[32,128]{1,0:T(8,128)}) %reduce-scatter.17.cloned.1.call-update) | async-done | bytes 16400 | tf_op jit(solution)/shard_map/reduce_scatter | solution.py:306
  1772.2 137.1 %reduce-scatter.21.cloned.1.call-done = f32[128,128]{1,0:T(8,128)} async-done(((f32[4096,128]{1,0:T(8,128)}), f32[128,128]{1,0:T(8,128)}) %reduce-scatter.21.cloned.1.call-update) | async-done | bytes 65552 | tf_op jit(solution)/shard_map/reduce_scatter | solution.py:308
  1909.3 137.8 %reduce-scatter.23.cloned.1.call-done = f32[128,128]{1,0:T(8,128)} async-done(((f32[4096,128]{1,0:T(8,128)}), f32[128,128]{1,0:T(8,128)}) %reduce-scatter.23.cloned.1.call-update) | async-done | bytes 65552 | tf_op jit(solution)/shard_map/reduce_scatter | solution.py:309
  (399 shorter events, 454.2 us)
Async XLA Ops:
  7.2 367.0 %copy-start.94 = (f32[1024]{0:T(1024)S(1)}, f32[1024]{0:T(1024)}, u32[]{:S(2)}) copy-start(f32[1024]{0:T(1024)} %param.31) | copy-start | bytes 12292
  7.3 366.9 %copy-start.102 = (f32[1024]{0:T(1024)S(1)}, f32[1024]{0:T(1024)}, u32[]{:S(2)}) copy-start(f32[1024]{0:T(1024)} %param.32) | copy-start | bytes 12292
  7.3 368.2 %all-gather.11.cloned.1.call-start = ((), (), s32[]{:S(2)}) async-start(), calls=%async_computation.9 | async-start | bytes 2162688 | tf_op jit(solution)/shard_map/all_gather | solution.py:114
  8.0 372.3 %all-gather.9.cloned.1.call-start = ((), (), s32[]{:S(2)}) async-start(), calls=%async_computation.8 | async-start | bytes 2162688 | tf_op jit(solution)/shard_map/all_gather | solution.py:113
  8.8 550.1 %all-gather.13.cloned.1.call-start = ((), (), s32[]{:S(2)}) async-start(), calls=%async_computation.10 | async-start | bytes 2162688 | tf_op jit(solution)/shard_map/all_gather | solution.py:112
  9.5 714.4 %all-gather.15.cloned.1.call-start = ((), (), s32[]{:S(2)}) async-start(), calls=%async_computation.11 | async-start | bytes 2162688 | tf_op jit(solution)/shard_map/all_gather | solution.py:115
  10.1 722.0 %all-gather.21.cloned.1.call-start = ((), (), s32[]{:S(2)}) async-start(), calls=%async_computation.14 | async-start | bytes 8650752 | tf_op jit(solution)/shard_map/all_gather | solution.py:117
  10.7 733.7 %all-gather.17.cloned.1.call-start = ((), (), s32[]{:S(2)}) async-start(), calls=%async_computation.12 | async-start | bytes 8650752 | tf_op jit(solution)/shard_map/all_gather | solution.py:116
  11.2 745.2 %all-gather.19.cloned.1.call-start = ((), (), s32[]{:S(2)}) async-start(), calls=%async_computation.13 | async-start | bytes 1081344 | tf_op jit(solution)/shard_map/all_gather | solution.py:123
  12.0 758.0 %all-gather.23.cloned.1.call-start = ((), (), s32[]{:S(2)}) async-start(), calls=%async_computation.15 | async-start | bytes 1081344 | tf_op jit(solution)/shard_map/all_gather | solution.py:124
  12.7 1180.4 %reduce-scatter.19.cloned.1.call-start = ((), (), s32[]{:S(2)}) async-start(), calls=%async_computation.20 | async-start | bytes 540672 | tf_op jit(solution)/shard_map/reduce_scatter | solution.py:307
  14.5 359.7 %copy-start.89 = (f32[768]{0:T(1024)}, f32[768]{0:T(1024)S(1)}, u32[]{:S(2)}) copy-start(f32[768]{0:T(1024)S(1)} %broadcast_multiply_fusion.5) | copy-start | bytes 9220
  16.4 540.3 %copy-start.45 = (bf16[768,128]{1,0:T(8,128)(2,1)}, bf16[768,128]{1,0:T(8,128)(2,1)S(1)}, u32[]{:S(2)}) copy-start(bf16[768,128]{1,0:T(8,128)(2,1)S(1)} %copy.96) | copy-start | bytes 589828
  390.5 180.3 %collective-permute-start = (bf16[576,2048]{1,0:T(8,128)(2,1)}, bf16[576,2048]{1,0:T(8,128)(2,1)}, u32[]{:S(2)}, u32[]{:S(2)}) collective-permute-start(bf16[576,2048]{1,0:T(8,128)(2,1)} %get-tuple-element.54), channel_id=1, source_target_pairs={{0,1},{1,2},{2,3},{3,4},{4,5},{5,6},{6,7},{7,8},{8,9},{9,10},{10,1... | collective-permute-start | bytes 7077896 | tf_op jit(solution)/shard_map/ppermute | solution.py:23
  393.2 177.6 %collective-permute-start.1 = (bf16[576,2048]{1,0:T(8,128)(2,1)}, bf16[576,2048]{1,0:T(8,128)(2,1)}, u32[]{:S(2)}, u32[]{:S(2)}) collective-permute-start(bf16[576,2048]{1,0:T(8,128)(2,1)} %get-tuple-element.55), channel_id=1, source_target_pairs={{1,0},{2,1},{3,2},{4,3},{5,4},{6,5},{7,6},{8,7},{9,8},{10,9},{11,1... | collective-permute-start | bytes 7077896 | tf_op jit(solution)/shard_map/ppermute | solution.py:24
  943.7 290.6 %reduce-scatter.25.cloned.1.call-start = ((), (), s32[]{:S(2)}) async-start(), calls=%async_computation.23 | async-start | bytes 540672
  1058.4 83.6 %collective-permute-start.2 = (bf16[576,2048]{1,0:T(8,128)(2,1)}, bf16[576,2048]{1,0:T(8,128)(2,1)}, u32[]{:S(2)}, u32[]{:S(2)}) collective-permute-start(bf16[576,2048]{1,0:T(8,128)(2,1)} %get-tuple-element.44), channel_id=1, source_target_pairs={{0,1},{1,2},{2,3},{3,4},{4,5},{5,6},{6,7},{7,8},{8,9},{9,10},{10,1... | collective-permute-start | bytes 7077896 | tf_op jit(solution)/shard_map/ppermute | solution.py:32
  1062.7 80.0 %collective-permute-start.3 = (bf16[576,2048]{1,0:T(8,128)(2,1)}, bf16[576,2048]{1,0:T(8,128)(2,1)}, u32[]{:S(2)}, u32[]{:S(2)}) collective-permute-start(bf16[576,2048]{1,0:T(8,128)(2,1)} %get-tuple-element.45), channel_id=1, source_target_pairs={{1,0},{2,1},{3,2},{4,3},{5,4},{6,5},{7,6},{8,7},{9,8},{10,9},{11,1... | collective-permute-start | bytes 7077896 | tf_op jit(solution)/shard_map/ppermute | solution.py:32
  1072.2 296.9 %reduce-scatter.13.cloned.1.call-start = ((), (), s32[]{:S(2)}) async-start(), calls=%async_computation.17 | async-start | bytes 540672 | tf_op jit(solution)/shard_map/reduce_scatter | solution.py:304
  1089.9 413.5 %reduce-scatter.11.cloned.1.call-start = ((), (), s32[]{:S(2)}) async-start(), calls=%async_computation.16 | async-start | bytes 540672 | tf_op jit(solution)/shard_map/reduce_scatter | solution.py:303
  1093.8 544.1 %reduce-scatter.15.cloned.1.call-start = ((), (), s32[]{:S(2)}) async-start(), calls=%async_computation.18 | async-start | bytes 540672 | tf_op jit(solution)/shard_map/reduce_scatter | solution.py:305
  1152.1 620.1 %reduce-scatter.17.cloned.1.call-start = ((), (), s32[]{:S(2)}) async-start(), calls=%async_computation.19 | async-start | bytes 540672 | tf_op jit(solution)/shard_map/reduce_scatter | solution.py:306
  1155.0 754.3 %reduce-scatter.21.cloned.1.call-start = ((), (), s32[]{:S(2)}) async-start(), calls=%async_computation.21 | async-start | bytes 2162688 | tf_op jit(solution)/shard_map/reduce_scatter | solution.py:308
  1161.1 886.1 %reduce-scatter.23.cloned.1.call-start = ((), (), s32[]{:S(2)}) async-start(), calls=%async_computation.22 | async-start | bytes 2162688 | tf_op jit(solution)/shard_map/reduce_scatter | solution.py:309
  (110 other events, 2627.4 us)
Sparse Core Ops, SparseCore 0:
  11.2 59.3 all-gather.10
  73.7 55.3 all-gather.8
  132.2 55.6 all-gather.12
  190.8 55.3 all-gather.14
  249.2 77.4 all-gather.20
  329.6 112.4 all-gather.16
  445.0 55.7 all-gather.18
  503.6 52.7 all-gather.22
  943.9 150.1 reduce-scatter.18
  1096.7 137.6 reduce-scatter.24
  1237.2 131.8 reduce-scatter.12
  1371.8 131.6 reduce-scatter.10
  1506.2 131.6 reduce-scatter.14
  1640.6 131.6 reduce-scatter.16
  1774.9 134.3 reduce-scatter.20
  1912.0 135.1 reduce-scatter.22
where the time goes:
time: 2060 us; the launch traced here: 2050 us
  waiting for transfers between devices  908 us (44%)
  blocking collectives  519 us (25%)
  matrix products  376 us (18%)
  other arithmetic  140 us (7%)
  local copies, waits for them, and re-layouts  84.7 us (4%)
    all_gather x1, blocking collectives, local(): lax.all_gather(down_out, ('fsdp', 'dp'), axis=0, tiled=True)  161 us
    reduce_scatter x1, waiting for transfers between devices, local(): lax.psum_scatter(grad_down_in, ('fsdp', 'dp'), scatter_dimension=0, tiled...  138 us
    reduce_scatter x1, waiting for transfers between devices, local(): lax.psum_scatter(grad_up_out, ('fsdp', 'dp'), scatter_dimension=0, tiled=...  137 us
    reduce_scatter x1, waiting for transfers between devices, local(): lax.psum_scatter(grad_query_out, ('fsdp', 'dp'), scatter_dimension=0, til...  135 us
    reduce_scatter x1, waiting for transfers between devices, local(): lax.psum_scatter(grad_value_in, ('fsdp', 'dp'), scatter_dimension=0, tile...  135 us
    reduce_scatter x1, waiting for transfers between devices, local(): lax.psum_scatter(grad_value_out, ('fsdp', 'dp'), scatter_dimension=0, til...  134 us
    reduce_scatter x1, waiting for transfers between devices, local(): lax.psum_scatter(grad_query_in, ('fsdp', 'dp'), scatter_dimension=0, tile...  134 us
    all_gather x1, blocking collectives, local(): lax.all_gather(query_in, ('fsdp', 'dp'), axis=0, tiled=True)  76.2 us
  transfers between devices with their start and end apart: 20, of which 9 were waited for; matrix products, arithmetic and copies ran while one was open for 20% of the time, Pallas kernels for 0%

commit v1 on v0

v1 whole, which is shorter than its diff:
```python
import functools

import jax
import jax.numpy as jnp
from jax import lax
from jax.experimental import pallas as pl
from jax.experimental.pallas import tpu as pltpu
from jax.sharding import PartitionSpec as P

HEADS = 16
IMG_LEN = 577
RANK = 16
ADAPTERS = 8
EPS = 1e-05
SLOPE = 1.702
NEG = -1000000000.0
AXES = ("fsdp", "dp")
LANES = 128
TILE = 256
HALO = 640
VMEM_LIMIT = 60 * 1024 * 1024

f32 = jnp.float32
bf16 = jnp.bfloat16


def dot_nn(a, b):
    return jnp.dot(a, b, preferred_element_type=f32)


def dot_nt(a, b):
    return lax.dot_general(a, b, (((1,), (1,)), ((), ())), preferred_element_type=f32)


def dot_tn(a, b):
    return lax.dot_general(a, b, (((0,), (0,)), ((), ())), preferred_element_type=f32)


def norm_forward(values, gain, shift):
    mean = jnp.mean(values, axis=1, keepdims=True)
    centered = values - mean
    inverse = lax.rsqrt(jnp.mean(centered * centered, axis=1, keepdims=True) + EPS)
    normed = centered * inverse
    return normed * gain + shift, normed, inverse


def norm_backward(grad, normed, inverse, gain):
    scaled = grad * gain
    return inverse * (
        scaled
        - jnp.mean(scaled, axis=1, keepdims=True)
        - normed * jnp.mean(scaled * normed, axis=1, keepdims=True)
    )


def params(grid_dims):
    return pltpu.CompilerParams(
        dimension_semantics=("arbitrary",) * grid_dims, vmem_limit_bytes=VMEM_LIMIT
    )


def whole(shape):
    return pl.BlockSpec(shape, lambda *_: (0,) * len(shape), pipeline_mode=pl.Buffered(1))


def twice(x):
    return jnp.concatenate([x, x], axis=1)


def qkv_kernel(tok, sel, w, bq, bv, gain, shift, q_o, k_o, v_o):
    width = tok.shape[1]
    normal, _, _ = norm_forward(tok[...].astype(f32), gain[...], shift[...])
    n1 = normal.astype(bf16)
    select = sel[...]
    low = dot_nn(n1, w[:, 3 * width : 3 * width + 2 * LANES]).astype(bf16)
    low_q = low[:, :LANES] * select
    low_v = low[:, LANES:] * select
    q_out = w[:, 3 * width + 2 * LANES : 3 * width + 3 * LANES]
    v_out = w[:, 3 * width + 3 * LANES : 3 * width + 4 * LANES]
    scale = (width // HEADS) ** -0.5
    q = dot_nn(n1, w[:, :width]) + bq[...] + dot_nt(low_q, q_out)
    q_o[...] = (q * scale).astype(bf16)
    k_o[...] = dot_nn(n1, w[:, width : 2 * width]).astype(bf16)
    v = dot_nn(n1, w[:, 2 * width : 3 * width]) + bv[...] + dot_nt(low_v, v_out)
    v_o[...] = v.astype(bf16)


def qkv_call(tok_w, sel_w, w_a, bq, bv, gain, shift):
    rows, width = tok_w.shape
    tile = pl.BlockSpec((TILE, width), lambda i: (i, 0))
    vec = whole((1, width))
    out = jax.ShapeDtypeStruct((rows, width), bf16)
    return pl.pallas_call(
        qkv_kernel,
        grid=(rows // TILE,),
        in_specs=[
            tile,
            pl.BlockSpec((TILE, LANES), lambda i: (i, 0)),
            whole(w_a.shape),
            vec,
            vec,
            vec,
            vec,
        ],
        out_specs=[tile] * 3,
        out_shape=[out] * 3,
        compiler_params=params(1),
        name="qkv",
    )(tok_w, sel_w, w_a, bq, bv, gain, shift)


def head_masks(rows):
    lane = lax.broadcasted_iota(jnp.int32, (rows, LANES), 1)
    return lane < (LANES // 2)


def attend_kernel(tab, q, k, v, segc, segr, mixed_o, lse_o, s_scr):
    own = mixed_o.shape[0]
    first = head_masks(TILE)
    zero = jnp.zeros((), bf16)
    one = jnp.ones((), bf16)
    for i in range(own // TILE):
        start, count = tab[2 * i], tab[2 * i + 1]
        row = HALO + TILE * i
        qt = q[row : row + TILE, :]
        q0 = jnp.where(first, qt, zero)
        q1 = jnp.where(first, zero, qt)
        sq = twice(segc[row : row + TILE, :])

        def scores(t, carry):
            m0, m1 = carry
            at = start + 2 * t
            kt = k[pl.ds(pl.multiple_of(at * LANES, LANES), TILE), :]
            sk = jnp.concatenate([segr[pl.ds(at, 1), :], segr[pl.ds(at + 1, 1), :]], axis=1)
            mask = sq == sk
            s0 = jnp.where(mask, dot_nt(q0, kt), NEG)
            s1 = jnp.where(mask, dot_nt(q1, kt), NEG)
            s_scr[0, t] = s0
            s_scr[1, t] = s1
            m0 = jnp.maximum(m0, jnp.maximum(s0[:, :LANES], s0[:, LANES:]))
            m1 = jnp.maximum(m1, jnp.maximum(s1[:, :LANES], s1[:, LANES:]))
            return m0, m1

        low = jnp.full((TILE, LANES), NEG, f32)
        m0, m1 = lax.fori_loop(0, count, scores, (low, low))
        m0 = jnp.max(m0, axis=1, keepdims=True)
        m1 = jnp.max(m1, axis=1, keepdims=True)

        def weigh(t, carry):
            a0, a1 = carry
            at = start + 2 * t
            vt = v[pl.ds(pl.multiple_of(at * LANES, LANES), TILE), :]
            p0 = jnp.exp(s_scr[0, t] - m0).astype(bf16)
            p1 = jnp.exp(s_scr[1, t] - m1).astype(bf16)
            a0 = a0 + dot_nn(p0, jnp.where(first, vt, one))
            a1 = a1 + dot_nn(p1, jnp.where(first, one, vt))
            return a0, a1

        empty = jnp.zeros((TILE, LANES), f32)
        a0, a1 = lax.fori_loop(0, count, weigh, (empty, empty))
        r0 = pltpu.roll(a0, LANES // 2, 1)
        r1 = pltpu.roll(a1, LANES // 2, 1)
        mixed_o[TILE * i : TILE * (i + 1), :] = jnp.where(first, a0 / r0, a1 / r1).astype(bf16)
        l0 = (m0 + jnp.log(jnp.where(first, r0, a0))).T
        l1 = (m1 + jnp.log(jnp.where(first, a1, r1))).T
        for half in range(2):
            at = 2 * i + half
            lse_o[0, 0, at : at + 1, :] = l0[0:1, half * LANES : (half + 1) * LANES]
            lse_o[0, 1, at : at + 1, :] = l1[0:1, half * LANES : (half + 1) * LANES]


def attend_call(tab, q, k, v, segc, segr, own):
    rows, width = q.shape
    pairs = width // LANES
    col = pl.BlockSpec((rows, LANES), lambda h, *_: (0, h))
    return pl.pallas_call(
        attend_kernel,
        grid_spec=pltpu.PrefetchScalarGridSpec(
            num_scalar_prefetch=1,
            grid=(pairs,),
            in_specs=[col, col, col, whole(segc.shape), whole(segr.shape)],
            out_specs=[
                pl.BlockSpec((own, LANES), lambda h, *_: (0, h)),
                pl.BlockSpec((1, 2, own // LANES, LANES), lambda h, *_: (h, 0, 0, 0)),
            ],
            scratch_shapes=[pltpu.VMEM((2, rows // TILE, TILE, TILE), f32)],
        ),
        out_shape=[
            jax.ShapeDtypeStruct((own, width), bf16),
            jax.ShapeDtypeStruct((pairs, 2, own // LANES, LANES), f32),
        ],
        compiler_params=params(1),
        name="attend",
    )(tab, q, k, v, segc, segr)


def split_pair(x, first):
    zero = jnp.zeros((), bf16)
    return jnp.concatenate([jnp.where(first, x, zero), jnp.where(first, zero, x)], axis=0)


def pair_grads(kt, vt, qcat, dcat, mask, lse0, lse1, dlt0, dlt1):
    half = qcat.shape[0] // 2
    s = dot_nt(kt, qcat)
    dp = dot_nt(vt, dcat)
    p0 = jnp.exp(jnp.where(mask, s[:, :half], NEG) - lse0)
    p1 = jnp.exp(jnp.where(mask, s[:, half:], NEG) - lse1)
    d0 = (p0 * (dp[:, :half] - dlt0)).astype(bf16)
    d1 = (p1 * (dp[:, half:] - dlt1)).astype(bf16)
    probs = jnp.concatenate([p0.astype(bf16), p1.astype(bf16)], axis=1)
    return probs, d0, d1


def attend_back_kernel(tab, q, k, v, dm, lse, dlt, segc, segr, dq_o, dk_o, dv_o, dk_a, dv_a):
    own = dm.shape[0]
    first = head_masks(TILE)
    scale = (LANES // 2) ** -0.5
    dk_a[...] = jnp.zeros_like(dk_a)
    dv_a[...] = jnp.zeros_like(dv_a)
    for i in range(own // TILE):
        start, count = tab[2 * i], tab[2 * i + 1]
        row = HALO + TILE * i
        qcat = split_pair(q[row : row + TILE, :], first)
        dcat = split_pair(dm[TILE * i : TILE * (i + 1), :], first)

        def line(ref, head):
            return jnp.concatenate(
                [ref[0, head, 2 * i : 2 * i + 1, :], ref[0, head, 2 * i + 1 : 2 * i + 2, :]], axis=1
            )

        lse0, lse1, dlt0, dlt1 = line(lse, 0), line(lse, 1), line(dlt, 0), line(dlt, 1)
        at_q = row // LANES
        sq = jnp.concatenate([segr[at_q : at_q + 1, :], segr[at_q + 1 : at_q + 2, :]], axis=1)

        def step(t, carry):
            a0, a1 = carry
            at = pl.multiple_of((start + 2 * t) * LANES, LANES)
            kt = k[pl.ds(at, TILE), :]
            vt = v[pl.ds(at, TILE), :]
            mask = twice(segc[pl.ds(at, TILE), :]) == sq
            probs, d0, d1 = pair_grads(kt, vt, qcat, dcat, mask, lse0, lse1, dlt0, dlt1)
            dv_a[pl.ds(at, TILE), :] += dot_nn(probs, dcat)
            dk_a[pl.ds(at, TILE), :] += dot_nn(jnp.concatenate([d0, d1], axis=1), qcat)
            return a0 + dot_tn(d0, kt), a1 + dot_tn(d1, kt)

        empty = jnp.zeros((TILE, LANES), f32)
        a0, a1 = lax.fori_loop(0, count, step, (empty, empty))
        dq_o[TILE * i : TILE * (i + 1), :] = (jnp.where(first, a0, a1) * scale).astype(bf16)
    dk_o[...] = dk_a[HALO : HALO + own, :]
    dv_o[...] = dv_a[HALO : HALO + own, :]


def attend_back_call(tab, q, k, v, dm, lse, dlt, segc, segr):
    rows, width = q.shape
    own = dm.shape[0]
    pairs = width // LANES
    col = pl.BlockSpec((rows, LANES), lambda h, *_: (0, h))
    own_col = pl.BlockSpec((own, LANES), lambda h, *_: (0, h))
    stat = pl.BlockSpec((1, 2, own // LANES, LANES), lambda h, *_: (h, 0, 0, 0))
    return pl.pallas_call(
        attend_back_kernel,
        grid_spec=pltpu.PrefetchScalarGridSpec(
            num_scalar_prefetch=1,
            grid=(pairs,),
            in_specs=[col, col, col, own_col, stat, stat, whole(segc.shape), whole(segr.shape)],
            out_specs=[own_col] * 3,
            scratch_shapes=[pltpu.VMEM((rows, LANES), f32)] * 2,
        ),
        out_shape=[
            jax.ShapeDtypeStruct((own, width), bf16),
            jax.ShapeDtypeStruct((own, width), f32),
            jax.ShapeDtypeStruct((own, width), f32),
        ],
        compiler_params=params(1),
        name="attend_back",
    )(tab, q, k, v, dm, lse, dlt, segc, segr)


def halo_back_kernel(
    tab, q, k, v, dm_l, dm_r, st_l, st_r, dk_i, dv_i, segc, segr, dk_o, dv_o, dk_a, dv_a
):
    own = dk_o.shape[0]
    first = head_masks(LANES)
    dk_a[...] = dk_i[...]
    dv_a[...] = dv_i[...]
    for side in range(2):
        base = 6 + 3 * side
        count_q, k_first, count_k = tab[base], tab[base + 1], tab[base + 2]
        dm, st = (dm_l, st_l) if side == 0 else (dm_r, st_r)

        def query_tile(t, carry):
            tile = HALO // LANES - 1 - t if side == 0 else t
            tile_w = tile if side == 0 else tile + (HALO + own) // LANES
            at_h = pl.multiple_of(tile * LANES, LANES)
            at_w = pl.multiple_of(tile_w * LANES, LANES)
            qcat = split_pair(q[pl.ds(at_w, LANES), :], first)
            dcat = split_pair(dm[pl.ds(at_h, LANES), :], first)
            lse0, lse1 = st[0, 0, 0, pl.ds(tile, 1), :], st[0, 0, 1, pl.ds(tile, 1), :]
            dlt0, dlt1 = st[1, 0, 0, pl.ds(tile, 1), :], st[1, 0, 1, pl.ds(tile, 1), :]
            sq = segr[pl.ds(tile_w, 1), :]

            def key_tile(u, inner):
                at = pl.multiple_of((k_first + u) * TILE, TILE)
                at_k = pl.multiple_of(HALO + at, LANES)
                kt = k[pl.ds(at_k, TILE), :]
                vt = v[pl.ds(at_k, TILE), :]
                mask = segc[pl.ds(at_k, TILE), :] == sq
                probs, d0, d1 = pair_grads(kt, vt, qcat, dcat, mask, lse0, lse1, dlt0, dlt1)
                dv_a[pl.ds(at, TILE), :] += dot_nn(probs, dcat)
                dk_a[pl.ds(at, TILE), :] += dot_nn(jnp.concatenate([d0, d1], axis=1), qcat)
                return inner

            return lax.fori_loop(0, count_k, key_tile, carry)

        lax.fori_loop(0, count_q, query_tile, 0)
    dk_o[...] = dk_a[...].astype(bf16)
    dv_o[...] = dv_a[...].astype(bf16)


def halo_back_call(tab, q, k, v, dm_l, dm_r, st_l, st_r, dk, dv, segc, segr):
    rows, width = q.shape
    own = dk.shape[0]
    pairs = width // LANES
    col = pl.BlockSpec((rows, LANES), lambda h, *_: (0, h))
    own_col = pl.BlockSpec((own, LANES), lambda h, *_: (0, h))
    halo_col = pl.BlockSpec((HALO, LANES), lambda h, *_: (0, h))
    stat = pl.BlockSpec((2, 1, 2, HALO // LANES, LANES), lambda h, *_: (0, h, 0, 0, 0))
    return pl.pallas_call(
        halo_back_kernel,
        grid_spec=pltpu.PrefetchScalarGridSpec(
            num_scalar_prefetch=1,
            grid=(pairs,),
            in_specs=[
                col,
                col,
                col,
                halo_col,
                halo_col,
                stat,
                stat,
                own_col,
                own_col,
                whole(segc.shape),
                whole(segr.shape),
            ],
            out_specs=[own_col] * 2,
            scratch_shapes=[pltpu.VMEM((own, LANES), f32)] * 2,
        ),
        out_shape=[jax.ShapeDtypeStruct((own, width), bf16)] * 2,
        compiler_params=params(1),
        name="halo_back",
    )(tab, q, k, v, dm_l, dm_r, st_l, st_r, dk, dv, segc, segr)


FF_TILE = 512


def mlp_kernel(
    mixed, tok, dy, sel, w_out, w_up, w_lo, w_dn, b_out, b_up, b_down, gain, shift, heads,
    out_o, dres_o, dmix_o, dlt_o, gui_o, gdo_o, guo_o, gdi_o,
    resid, n2, low_u, dlow_d, low_ut, dlow_dt, acc, acc_low, dn2, dlow_u, gdo_t, gui_t,
):
    j = pl.program_id(0)
    rows, width = mixed.shape
    chunks = [pl.ds(r, TILE) for r in range(0, rows, TILE)]
    up_in = w_lo[:, :LANES]
    down_out = w_lo[:, LANES:]

    @pl.when(j == 0)
    def _():
        for r in chunks:
            x = tok[r, :].astype(f32) + dot_nn(mixed[r, :], w_out[...]) + b_out[...]
            resid[r, :] = x
            normal, _, _ = norm_forward(x, gain[...], shift[...])
            normal = normal.astype(bf16)
            n2[r, :] = normal
            lu = dot_nn(normal, up_in).astype(bf16) * sel[r, :]
            ld = dot_nn(dy[r, :], down_out).astype(bf16) * sel[r, :]
            low_u[r, :] = lu
            dlow_d[r, :] = ld
            low_ut[:, r] = lu.astype(f32).T.astype(bf16)
            dlow_dt[:, r] = ld.astype(f32).T.astype(bf16)
        acc[...] = jnp.zeros_like(acc)
        acc_low[...] = jnp.zeros_like(acc_low)
        dn2[...] = jnp.zeros_like(dn2)
        dlow_u[...] = jnp.zeros_like(dlow_u)
        gdo_t[...] = jnp.zeros_like(gdo_t)
        gui_t[...] = jnp.zeros_like(gui_t)

    down = w_dn[:, :width]
    up_out = w_dn[:, width : width + LANES]
    down_in = w_dn[:, width + LANES :]
    guo_t = jnp.zeros((LANES, FF_TILE), f32)
    gdi_t = jnp.zeros((LANES, FF_TILE), f32)
    for r in chunks:
        pre = dot_nn(n2[r, :], w_up[...]) + b_up[...] + dot_nt(low_u[r, :], up_out)
        d_act = dot_nt(dy[r, :], down) + dot_nt(dlow_d[r, :], down_in)
        gate = 1.0 / (1.0 + jnp.exp(-SLOPE * pre))
        act = pre * gate
        d_pre = (d_act * (gate + SLOPE * act * (1.0 - gate))).astype(bf16)
        act = act.astype(bf16)
        acc[r, :] += dot_nn(act, down)
        acc_low[r, :] += dot_nn(act, down_in)
        dn2[r, :] += dot_nt(d_pre, w_up[...])
        dlow_u[r, :] += dot_nn(d_pre, up_out)
        guo_t += dot_nn(low_ut[:, r], d_pre)
        gdi_t += dot_nn(dlow_dt[:, r], act)
    guo_o[...] = guo_t.T
    gdi_o[...] = gdi_t.T

    @pl.when(j == pl.num_programs(0) - 1)
    def _():
        for r in chunks:
            select = sel[r, :]
            x = resid[r, :]
            low_d = acc_low[r, :].astype(bf16) * select
            out_o[r, :] = (x + acc[r, :] + b_down[...] + dot_nt(low_d, down_out)).astype(bf16)
            lu = dlow_u[r, :].astype(bf16) * select
            _, hat, inv = norm_forward(x, gain[...], shift[...])
            grad = dn2[r, :] + dot_nt(lu, up_in)
            dres = dy[r, :].astype(f32) + norm_backward(grad, hat, inv, gain[...])
            dres_o[r, :] = dres
            dmix = dot_nt(dres.astype(bf16), w_out[...]).astype(bf16)
            dmix_o[r, :] = dmix
            prod = dmix.astype(f32) * mixed[r, :].astype(f32)
            high = prod.astype(bf16)
            rest = (prod - high.astype(f32)).astype(bf16)
            dlt_o[:, r] = dot_nt(heads[...], high) + dot_nt(heads[...], rest)
            gdo_t[...] += dot_nn(low_d.astype(f32).T.astype(bf16), dy[r, :])
            gui_t[...] += dot_nn(lu.astype(f32).T.astype(bf16), n2[r, :])
        gdo_o[...] = gdo_t[...].T
        gui_o[...] = gui_t[...].T


def mlp_call(mixed, tok, dy, sel, w_b, w_c, b_out, b_up, b_down, gain, shift, heads):
    rows, width = mixed.shape
    hidden = w_c.shape[0]
    full = whole((rows, width))
    vec = whole((1, width))
    low = whole((rows, LANES))
    lead = width // FF_TILE
    at_low = (width + hidden) // (2 * LANES)
    grads = jax.ShapeDtypeStruct((width, LANES), f32)
    grads_ff = jax.ShapeDtypeStruct((hidden, LANES), f32)
    const = lambda shape: pl.BlockSpec(shape, lambda j: (0,) * len(shape))
    ff_rows = pl.BlockSpec((FF_TILE, LANES), lambda j: (j, 0))
    return pl.pallas_call(
        mlp_kernel,
        grid=(hidden // FF_TILE,),
        in_specs=[
            full,
            full,
            full,
            low,
            whole((width, width)),
            pl.BlockSpec((width, FF_TILE), lambda j: (0, lead + j)),
            pl.BlockSpec((width, 2 * LANES), lambda j: (0, at_low), pipeline_mode=pl.Buffered(1)),
            pl.BlockSpec((FF_TILE, w_c.shape[1]), lambda j: (j, 0)),
            vec,
            pl.BlockSpec((1, FF_TILE), lambda j: (0, j)),
            vec,
            vec,
            vec,
            whole(heads.shape),
        ],
        out_specs=[
            const((rows, width)),
            const((rows, width)),
            const((rows, width)),
            const((HEADS, rows)),
            const((width, LANES)),
            const((width, LANES)),
            ff_rows,
            ff_rows,
        ],
        out_shape=[
            jax.ShapeDtypeStruct((rows, width), bf16),
            jax.ShapeDtypeStruct((rows, width), f32),
            jax.ShapeDtypeStruct((rows, width), bf16),
            jax.ShapeDtypeStruct((HEADS, rows), f32),
            grads,
            grads,
            grads_ff,
            grads_ff,
        ],
        scratch_shapes=[
            pltpu.VMEM((rows, width), f32),
            pltpu.VMEM((rows, width), bf16),
            pltpu.VMEM((rows, LANES), bf16),
            pltpu.VMEM((rows, LANES), bf16),
            pltpu.VMEM((LANES, rows), bf16),
            pltpu.VMEM((LANES, rows), bf16),
            pltpu.VMEM((rows, width), f32),
            pltpu.VMEM((rows, LANES), f32),
            pltpu.VMEM((rows, width), f32),
            pltpu.VMEM((rows, LANES), f32),
            pltpu.VMEM((LANES, width), f32),
            pltpu.VMEM((LANES, width), f32),
        ],
        compiler_params=params(1),
        name="mlp",
    )(mixed, tok, dy, sel, w_b, w_b, w_b, w_c, b_out, b_up, b_down, gain, shift, heads)


def qkv_back_kernel(dq, dk, dv, tok, dres, sel, w, gain, shift, gin_o, grads_o, acc):
    i = pl.program_id(0)
    width = tok.shape[1]
    normal, hat, inv = norm_forward(tok[...].astype(f32), gain[...], shift[...])
    n1 = normal.astype(bf16)
    select = sel[...]
    q_in = w[:, 3 * width : 3 * width + LANES]
    v_in = w[:, 3 * width + LANES : 3 * width + 2 * LANES]
    q_out = w[:, 3 * width + 2 * LANES : 3 * width + 3 * LANES]
    v_out = w[:, 3 * width + 3 * LANES : 3 * width + 4 * LANES]
    low_q = dot_nn(n1, q_in).astype(bf16) * select
    low_v = dot_nn(n1, v_in).astype(bf16) * select
    dlow_q = dot_nn(dq[...], q_out).astype(bf16) * select
    dlow_v = dot_nn(dv[...], v_out).astype(bf16) * select
    grad = (
        dot_nt(dq[...], w[:, :width])
        + dot_nt(dk[...], w[:, width : 2 * width])
        + dot_nt(dv[...], w[:, 2 * width : 3 * width])
        + dot_nt(dlow_q, q_in)
        + dot_nt(dlow_v, v_in)
    )
    gin_o[...] = (dres[...] + norm_backward(grad, hat, inv, gain[...])).astype(bf16)

    @pl.when(i == 0)
    def _():
        acc[...] = jnp.zeros_like(acc)

    def turned(x):
        return x.astype(f32).T.astype(bf16)

    acc[0] += dot_nn(turned(dlow_q), n1)
    acc[1] += dot_nn(turned(low_q), dq[...])
    acc[2] += dot_nn(turned(dlow_v), n1)
    acc[3] += dot_nn(turned(low_v), dv[...])

    @pl.when(i == pl.num_programs(0) - 1)
    def _():
        for at in range(4):
            grads_o[at] = acc[at].T


def qkv_back_call(dq, dk, dv, tok, dres, sel, w_a, gain, shift):
    rows, width = tok.shape
    tile = pl.BlockSpec((TILE, width), lambda i: (i, 0))
    vec = whole((1, width))
    return pl.pallas_call(
        qkv_back_kernel,
        grid=(rows // TILE,),
        in_specs=[
            tile,
            tile,
            tile,
            tile,
            tile,
            pl.BlockSpec((TILE, LANES), lambda i: (i, 0)),
            whole(w_a.shape),
            vec,
            vec,
        ],
        out_specs=[tile, pl.BlockSpec((4, width, LANES), lambda i: (0, 0, 0))],
        out_shape=[
            jax.ShapeDtypeStruct((rows, width), bf16),
            jax.ShapeDtypeStruct((4, width, LANES), f32),
        ],
        scratch_shapes=[pltpu.VMEM((4, LANES, width), f32)],
        compiler_params=params(1),
        name="qkv_back",
    )(dq, dk, dv, tok, dres, sel, w_a, gain, shift)


def halved(parts, devices, inner):
    me = lax.axis_index(AXES)
    bits = devices.bit_length() - 1
    core = inner.bit_length() - 1
    order = [core] + list(range(core)) + [b for b in range(bits) if b > core]
    left = list(range(bits))[::-1]
    parts = [p.reshape(devices, -1, p.shape[-1]) for p in parts]
    x = parts
    for step, bit in enumerate(order):
        at = left.index(bit)
        outer, rest = 2**at, 2 ** (len(left) - 1 - at)
        mine = (me >> bit) & 1
        pairs = [(p, p ^ (1 << bit)) for p in range(devices)]

        def half(index):
            pieces = [
                lax.dynamic_index_in_dim(
                    p.reshape(outer, 2, rest, p.shape[1], p.shape[2]), index, 1, keepdims=False
                ).reshape(outer * rest, p.shape[1], p.shape[2])
                for p in x
            ]
            return pieces[0] if len(pieces) == 1 else jnp.concatenate(pieces, axis=1)

        send = half(1 - mine)
        if step > 0:
            send = send.astype(bf16)
        got = lax.ppermute(send, AXES, pairs)
        x = [half(mine) + got.astype(f32)]
        left.remove(bit)
    return x[0][0]


def local(
    tokens, cotangent, segments, adapter_ids, ln1_gain, ln1_bias, w_query, b_query, w_key, w_value,
    b_value, w_out, b_out, ln2_gain, ln2_bias, w_up, b_up, w_down, b_down, query_in, query_out,
    value_in, value_out, up_in, up_out, down_in, down_out,
):
    own, width = tokens.shape
    inner = lax.axis_size("dp")
    devices = lax.axis_size("fsdp") * inner
    up = [(i, i + 1) for i in range(devices - 1)]
    down = [(i + 1, i) for i in range(devices - 1)]

    def gather(*pieces):
        return lax.all_gather(jnp.concatenate(pieces, axis=1), AXES, axis=0, tiled=True)

    before = lax.ppermute(tokens[own - HALO :], AXES, up)
    after = lax.ppermute(tokens[:HALO], AXES, down)
    w_a = gather(w_query, w_key, w_value, query_in, value_in, query_out, value_out)
    w_b = gather(w_out, w_up, up_in, down_out)
    w_c = gather(w_down, up_out, down_in)

    position = lax.axis_index(AXES)
    padded = jnp.concatenate(
        [
            jnp.full((HALO,), -1, jnp.int32),
            segments,
            jnp.full((HALO,), 1 << 30, jnp.int32),
        ]
    )
    rows = own + 2 * HALO
    seg_w = lax.dynamic_slice_in_dim(padded, position * own, rows, 0)
    tile_seg = seg_w[HALO : HALO + own].reshape(own // TILE, TILE)
    images = jnp.concatenate([tile_seg[:, 0], tile_seg[:, -1]])
    low = jnp.sum((seg_w[None, :] < images[:, None]).astype(jnp.int32), axis=1)
    high = jnp.sum((seg_w[None, :] <= images[:, None]).astype(jnp.int32), axis=1)
    tiles = own // TILE
    entries = []
    for i in range(tiles):
        start = low[i] // LANES
        count = (high[tiles + i] - start * LANES + TILE - 1) // TILE
        entries += [jnp.minimum(start, rows // LANES - 2 * count), count]
    count_l = (HALO - low[0] + LANES - 1) // LANES
    entries += [
        jnp.maximum(count_l, 0),
        jnp.zeros((), jnp.int32),
        (jnp.minimum(high[0], HALO + own) - HALO + TILE - 1) // TILE,
    ]
    last = 2 * tiles - 1
    first_k = jnp.maximum(low[last] - HALO, 0) // TILE
    entries += [
        jnp.maximum((high[last] - HALO - own + LANES - 1) // LANES, 0),
        first_k,
        tiles - first_k,
    ]
    tab = jnp.stack(entries)
    segr = seg_w.reshape(rows // LANES, LANES)
    segc = jnp.broadcast_to(seg_w[:, None], (rows, LANES))

    image_hot = (seg_w[:, None] == jnp.arange(adapter_ids.shape[0], dtype=jnp.int32)).astype(bf16)
    column = jnp.arange(ADAPTERS * RANK, dtype=jnp.int32) // RANK
    adapter_hot = (adapter_ids[:, None] == column[None, :]).astype(bf16)
    sel_w = dot_nn(image_hot, adapter_hot).astype(bf16)
    sel = sel_w[HALO : HALO + own]
    heads = (
        jnp.arange(width, dtype=jnp.int32)[None, :] // (width // HEADS)
        == jnp.arange(HEADS, dtype=jnp.int32)[:, None]
    ).astype(bf16)

    row = lambda x: x.reshape(1, -1)
    tok_w = jnp.concatenate([before, tokens, after], axis=0)
    q, k, v = qkv_call(
        tok_w, sel_w, w_a, row(b_query), row(b_value), row(ln1_gain), row(ln1_bias)
    )
    mixed, lse = attend_call(tab, q, k, v, segc, segr, own)
    block_out, d_resid, d_mixed, delta, g_ui, g_do, g_uo, g_di = mlp_call(
        mixed, tokens, cotangent, sel, w_b, w_c, row(b_out), row(b_up), row(b_down),
        row(ln2_gain), row(ln2_bias), heads,
    )
    dlt = delta.reshape(lse.shape)
    stats = jnp.stack([lse, dlt])
    cut = (own - HALO) // LANES
    dm_l = lax.ppermute(d_mixed[own - HALO :], AXES, up)
    dm_r = lax.ppermute(d_mixed[:HALO], AXES, down)
    st_l = lax.ppermute(stats[:, :, :, cut:], AXES, up)
    st_r = lax.ppermute(stats[:, :, :, : HALO // LANES], AXES, down)
    mlp_grads = halved([g_ui, g_uo, g_di, g_do], devices, inner)
    dq, dk, dv = attend_back_call(tab, q, k, v, d_mixed, lse, dlt, segc, segr)
    dk, dv = halo_back_call(tab, q, k, v, dm_l, dm_r, st_l, st_r, dk, dv, segc, segr)
    grad_input, g_qv = qkv_back_call(
        dq, dk, dv, tokens, d_resid, sel, w_a, row(ln1_gain), row(ln1_bias)
    )
    qv_grads = halved([g_qv[0], g_qv[1], g_qv[2], g_qv[3]], devices, inner)
    r = width // devices
    r_ff = w_c.shape[0] // devices
    return (
        block_out,
        grad_input,
        qv_grads[:r],
        qv_grads[r : 2 * r],
        qv_grads[2 * r : 3 * r],
        qv_grads[3 * r :],
        mlp_grads[:r],
        mlp_grads[r : r + r_ff],
        mlp_grads[r + r_ff : r + 2 * r_ff],
        mlp_grads[r + 2 * r_ff :],
    )


def solution(mesh):
    split = P(AXES, None)
    return jax.shard_map(
        local,
        mesh=mesh,
        in_specs=(
            split, split, P(), P(), P(), P(), split, P(), split, split, P(), split, P(), P(), P(),
            split, P(), split, P(), split, split, split, split, split, split, split, split,
        ),
        out_specs=(split,) * 10,
        check_vma=False,
    )
```

time: 2060 us -> 555 us (0.27)
  waiting for transfers between devices: 908 us -> 196 us
  blocking collectives: 519 us -> 0 us
  matrix products: 376 us -> 0.47 us
  Pallas kernels: 0 us -> 212 us
  other arithmetic: 140 us -> 16.2 us
  starting transfers between devices: 10.3 us -> 77.9 us
  local copies, waits for them, and re-layouts: 84.7 us -> 26.6 us
    reduce_scatter x7 -> x0, waiting for transfers between devices: 813 us -> none  [the longest x1 138 us: local(): lax.psum_scatter(grad_down_in, ('fsdp', 'dp'), scatter_dimension=0, tiled...]
    all_gather x6 -> x0, blocking collectives: 519 us -> none  [the longest x1 161 us: local(): lax.all_gather(down_out, ('fsdp', 'dp'), axis=0, tiled=True)]
    dot_general x61 -> x1, matrix products: 376 us -> 0.47 us  [dot_nn(): return jnp.dot(a, b, preferred_element_type=f32)]
    pallas_call x0 -> x6, Pallas kernels: none -> 212 us  [the longest x1 58.3 us: mlp_call(): pl.pallas_call(mlp_kernel, grid=(hidden // FF_TILE,), in_specs=[full, ful...]
    all_gather x8 -> x3, waiting for transfers between devices: 0.07 us -> 139 us  [gather(): lax.all_gather(jnp.concatenate(pieces, axis=1), AXES, axis=0, tiled=True)]
    ppermute x4 -> x16, starting transfers between devices: 9.68 us -> 77.8 us  [the longest x10 59 us: halved(): got = lax.ppermute(send, AXES, pairs)]
    convert_element_type x7 -> x1, other arithmetic: 66.2 us -> 0.62 us  [local(): heads = (jnp.arange(width, dtype=jnp.int32)[None, :] // (width // HEADS)...]
    unnamed x17 -> x3, waiting for transfers between devices: 46.4 us -> 0.05 us
  transfers between devices with their start and end apart: 20 -> 19, of which waited for: 9 -> 11; matrix products, arithmetic and copies ran while one was open for 20% -> 5% of each run, Pallas kernels for 0% -> 28%
where the time goes in v1:
time: 555 us; the launch traced here: 557 us
  Pallas kernels  212 us (38%)
  waiting for transfers between devices  196 us (35%)
  starting transfers between devices  77.9 us (14%)
  between operations  26.7 us (5%)
  local copies, waits for them, and re-layouts  26.6 us (5%)
  other arithmetic  16.2 us (3%)
    all_gather x3, waiting for transfers between devices, gather(): lax.all_gather(jnp.concatenate(pieces, axis=1), AXES, axis=0, tiled=True)  139 us
    ppermute x10, starting transfers between devices, halved(): got = lax.ppermute(send, AXES, pairs)  59 us
    pallas_call x1, Pallas kernels, mlp_call(): pl.pallas_call(mlp_kernel, grid=(hidden // FF_TILE,), in_specs=[full, ful...  58.3 us
    pallas_call x1, Pallas kernels, attend_back_call(): pl.pallas_call(attend_back_kernel, grid_spec=pltpu.PrefetchScalarGridSpec...  49.7 us
    pallas_call x1, Pallas kernels, attend_call(): pl.pallas_call(attend_kernel, grid_spec=pltpu.PrefetchScalarGridSpec(num_...  48.3 us
    ppermute x1, waiting for transfers between devices, local(): before = lax.ppermute(tokens[own - HALO:], AXES, up)  29.2 us
    ppermute x10, waiting for transfers between devices, halved(): got = lax.ppermute(send, AXES, pairs)  27 us
    pallas_call x1, Pallas kernels, qkv_call(): pl.pallas_call(qkv_kernel, grid=(rows // TILE,), in_specs=[tile, pl.Block...  24.1 us
  transfers between devices with their start and end apart: 19, of which 11 were waited for; matrix products, arithmetic and copies ran while one was open for 5% of the time, Pallas kernels for 28%

profile of v1, /device:TPU:0, one launch (start us, length us, event | category | flops | bytes accessed | tf_op | source)
XLA Modules:
  0.0 556.6 jit_solution(4224882496614639670)
XLA Ops:
  18.5 6.0 %collective-permute-start = (bf16[640,1024]{1,0:T(8,128)(2,1)}, bf16[640,1024]{1,0:T(8,128)(2,1)}, u32[]{:S(2)}, u32[]{:S(2)}) collective-permute-start(bf16[640,1024]{1,0:T(8,128)(2,1)} %get-tuple-element.64), channel_id=1, source_target_pairs={{0,1},{1,2},{2,3},{3,4},{4,5},{5,6},{6,7},{7,8},{8,9},{9,10},{10,1... | collective-permute-start | bytes 3932168 | tf_op jit(solution)/shard_map/ppermute | solution.py:621
  42.7 29.2 %collective-permute-done = bf16[640,1024]{1,0:T(8,128)(2,1)} collective-permute-done((bf16[640,1024]{1,0:T(8,128)(2,1)}, bf16[640,1024]{1,0:T(8,128)(2,1)}, u32[]{:S(2)}, u32[]{:S(2)}) %collective-permute-start) | collective-permute-done | bytes 1310752 | tf_op jit(solution)/shard_map/ppermute | solution.py:621
  72.3 3.5 pad_maximum_fusion.tok
  75.8 35.4 %all-gather.4.cloned.1.call-done.w = bf16[1024,3584]{1,0:T(8,128)(2,1)} async-done(((bf16[32,3584]{1,0:T(8,128)(2,1)}), bf16[1024,3584]{1,0:T(8,128)(2,1)}) %all-gather.4.cloned.1.call-update) | async-done | bytes 7340048 | tf_op jit(solution)/shard_map/all_gather | solution.py:619
  111.2 24.1 %qkv.1 = (bf16[2048,1024]{1,0:T(8,128)(2,1)}, bf16[2048,1024]{1,0:T(8,128)(2,1)}, bf16[2048,1024]{1,0:T(8,128)(2,1)}) custom-call(bf16[2048,1024]{1,0:T(8,128)(2,1)} %pad_maximum_fusion.tok, bf16[2048,128]{1,0:T(8,128)(2,1)} %copy-done.1, bf16[1024,3584]{1,0:T(8,128)(2,1)} %all-gather.4.cloned.1.call-done.w, f32[1,1024]{1,0:T(1,128)} %bitcast.144, ...), custom_call_target="tpu_custom_call" | custom-call | tf_op jit(solution)/shard_map/qkv/pallas_call | solution.py:93
  136.7 48.3 %attend.1 = (bf16[768,1024]{1,0:T(8,128)(2,1)}, f32[8,2,6,128]{3,2,1,0:T(8,128)}) custom-call(s32[12]{0:T(128)} %stack.53.tab, bf16[2048,1024]{1,0:T(8,128)(2,1)} %get-tuple-element.30.q, bf16[2048,1024]{1,0:T(8,128)(2,1)} %get-tuple-element.31.k, bf16[2048,1024]{1,0:T(8,128)(2,1)} %get-tuple-element.32.v, s32[2048,128]{1,0:T(8,128)} %broadcast_in_dim.8.segc, ...), custom_call_target="tpu_custom_call" | custom-call | tf_op jit(solution)/shard_map/attend/pallas_call | solution.py:176
  185.0 14.2 %all-gather.8.cloned.1.call-done.w_dn = bf16[4096,1280]{1,0:T(8,128)(2,1)} async-done(((bf16[128,1280]{1,0:T(8,128)(2,1)}), bf16[4096,1280]{1,0:T(8,128)(2,1)}) %all-gather.8.cloned.1.call-update) | async-done | bytes 10485776 | tf_op jit(solution)/shard_map/all_gather | solution.py:619
  199.2 89.8 %all-gather.6.cloned.1.call-done.w_out.w_up.w_lo = bf16[1024,5376]{1,0:T(8,128)(2,1)} async-done(((bf16[32,5376]{1,0:T(8,128)(2,1)}), bf16[1024,5376]{1,0:T(8,128)(2,1)}) %all-gather.6.cloned.1.call-update) | async-done | bytes 11010064 | tf_op jit(solution)/shard_map/all_gather | solution.py:619
  289.0 58.3 %mlp.1 = (bf16[768,1024]{1,0:T(8,128)(2,1)}, f32[768,1024]{1,0:T(8,128)}, bf16[768,1024]{1,0:T(8,128)(2,1)}, f32[16,768]{1,0:T(8,128)}, f32[1024,128]{1,0:T(8,12...) custom-call(bf16[768,1024]{1,0:T(8,128)(2,1)} %get-tuple-element.33.mixed, ...), custom_call_target="tpu_custom_call" | custom-call | tf_op jit(solution)/shard_map/mlp/pallas_call | solution.py:447
  347.4 3.6 fusion.17
  350.9 4.5 collective-permute-start.2
  361.4 4.5 collective-permute-start.4
  367.9 49.7 %attend_back.1 = (bf16[768,1024]{1,0:T(8,128)(2,1)}, f32[768,1024]{1,0:T(8,128)}, f32[768,1024]{1,0:T(8,128)}) custom-call(s32[12]{0:T(128)} %stack.53.tab, bf16[2048,1024]{1,0:T(8,128)(2,1)} %get-tuple-element.30.q, bf16[2048,1024]{1,0:T(8,128)(2,1)} %get-tuple-element.31.k, bf16[2048,1024]{1,0:T(8,128)(2,1)} %get-tuple-element.32.v, ...), custom_call_target="tpu_custom_call" | custom-call | tf_op jit(solution)/shard_map/attend_back/pallas_call | solution.py:260
  418.3 14.4 %halo_back.1 = (bf16[768,1024]{1,0:T(8,128)(2,1)}, bf16[768,1024]{1,0:T(8,128)(2,1)}) custom-call(s32[12]{0:T(128)} %stack.53.tab, bf16[2048,1024]{1,0:T(8,128)(2,1)} %get-tuple-element.30.q, bf16[2048,1024]{1,0:T(8,128)(2,1)} %get-tuple-element.31.k, bf16[2048,1024]{1,0:T(8,128)(2,1)} %get-tuple-element.32.v, ...), custom_call_target="tpu_custom_call" | custom-call | tf_op jit(solution)/shard_map/halo_back/pallas_call | solution.py:328
  432.8 17.6 %qkv_back.1 = (bf16[768,1024]{1,0:T(8,128)(2,1)}, f32[4,1024,128]{2,1,0:T(8,128)}) custom-call(bf16[768,1024]{1,0:T(8,128)(2,1)} %get-tuple-element.38.dq, bf16[768,1024]{1,0:T(8,128)(2,1)} %get-tuple-element.41.dk, bf16[768,1024]{1,0:T(8,128)(2,1)} %get-tuple-element.42.dv, bf16[768,1024]{1,0:T(8,128)(2,1)} %tok.3, f32[768,1024]{1,0:T(8,128)} %get-tuple-element.43.dres, ...), custom_call_target="tpu_custom_call" | custom-call | tf_op jit(solution)/shard_map/qkv_back/pallas_call | solution.py:550
  455.4 25.5 %collective-permute-start.6 = (f32[16,128,128]{2,1,0:T(8,128)}, f32[16,128,128]{2,1,0:T(8,128)}, u32[]{:S(2)}, u32[]{:S(2)}) collective-permute-start(f32[16,128,128]{2,1,0:T(8,128)} %pad_maximum_fusion.2), channel_id=1, source_target_pairs={{0,2},{1,3},{2,0},{3,1},{4,6},{5,7},{6,4},{7,5},{8,10},{9,11},{10,... | collective-permute-start | bytes 3145736 | tf_op jit(solution)/shard_map/ppermute | solution.py:601
  485.2 11.4 %collective-permute-start.7 = (bf16[8,128,128]{2,1,0:T(8,128)(2,1)S(1)}, bf16[8,128,128]{2,1,0:T(8,128)(2,1)S(1)}, u32[]{:S(2)}, u32[]{:S(2)}) collective-permute-start(bf16[8,128,128]{2,1,0:T(8,128)(2,1)S(1)} %fusion.3), channel_id=1, source_target_pairs={{0,1},{1,0},{2,3},{3,2},{4,5},{5,4},{6,7},{7,6},{8,9},{9,8},{10,11... | collective-permute-start | bytes 786440 | tf_op jit(solution)/shard_map/ppermute | solution.py:601
  500.2 3.5 collective-permute-done.7
  503.8 11.2 %collective-permute-start.8 = (bf16[4,128,128]{2,1,0:T(8,128)(2,1)S(1)}, bf16[4,128,128]{2,1,0:T(8,128)(2,1)S(1)}, u32[]{:S(2)}, u32[]{:S(2)}) collective-permute-start(bf16[4,128,128]{2,1,0:T(8,128)(2,1)S(1)} %fusion.5), channel_id=1, source_target_pairs={{0,4},{1,5},{2,6},{3,7},{4,0},{5,1},{6,2},{7,3},{8,12},{9,13},{10,... | collective-permute-start | bytes 393224 | tf_op jit(solution)/shard_map/ppermute | solution.py:601
  515.0 3.1 collective-permute-done.8
  519.5 10.4 %collective-permute-start.13 = (bf16[4,320,128]{2,1,0:T(8,128)(2,1)S(1)}, bf16[4,320,128]{2,1,0:T(8,128)(2,1)S(1)}, u32[]{:S(2)}, u32[]{:S(2)}) collective-permute-start(bf16[4,320,128]{2,1,0:T(8,128)(2,1)S(1)} %fusion.2), channel_id=1, source_target_pairs={{0,4},{1,5},{2,6},{3,7},{4,0},{5,1},{6,2},{7,3},{8,12},{9,13},{10,... | collective-permute-start | bytes 983048 | tf_op jit(solution)/shard_map/ppermute | solution.py:601
  530.1 7.3 %collective-permute-done.13 = bf16[4,320,128]{2,1,0:T(8,128)(2,1)S(1)} collective-permute-done((bf16[4,320,128]{2,1,0:T(8,128)(2,1)S(1)}, bf16[4,320,128]{2,1,0:T(8,128)(2,1)S(1)}, u32[]{:S(2)}, u32[]{:S(2)}) %collective-permute-start.13) | collective-permute-done | bytes 327712 | tf_op jit(solution)/shard_map/ppermute | solution.py:601
  537.7 5.3 collective-permute-done.14
  543.7 5.1 collective-permute-done.15
  (113 shorter events, 43.9 us)
Async XLA Ops:
  7.2 9.9 %copy-start = (bf16[768,1024]{1,0:T(8,128)(2,1)S(1)}, bf16[768,1024]{1,0:T(8,128)(2,1)}, u32[]{:S(2)}) copy-start(bf16[768,1024]{1,0:T(8,128)(2,1)} %tok.3) | copy-start | bytes 4718596
  7.2 104.0 %all-gather.4.cloned.1.call-start = ((), (), s32[]{:S(2)}) async-start(), calls=%async_computation | async-start | bytes 7569408 | tf_op jit(solution)/shard_map/all_gather | solution.py:619
  13.4 185.8 %all-gather.8.cloned.1.call-start = ((), (), s32[]{:S(2)}) async-start(), calls=%async_computation.2 | async-start | bytes 10813440 | tf_op jit(solution)/shard_map/all_gather | solution.py:619
  15.3 273.7 %all-gather.6.cloned.1.call-start = ((), (), s32[]{:S(2)}) async-start(), calls=%async_computation.1 | async-start | bytes 11354112 | tf_op jit(solution)/shard_map/all_gather | solution.py:619
  17.1 22.4 %copy-start.12 = (s32[48]{0:T(128)S(1)}, s32[48]{0:T(128)}, u32[]{:S(2)}) copy-start(s32[48]{0:T(128)} %param.30) | copy-start | bytes 580
  18.5 53.3 %collective-permute-start = (bf16[640,1024]{1,0:T(8,128)(2,1)}, bf16[640,1024]{1,0:T(8,128)(2,1)}, u32[]{:S(2)}, u32[]{:S(2)}) collective-permute-start(bf16[640,1024]{1,0:T(8,128)(2,1)} %get-tuple-element.64), channel_id=1, source_target_pairs={{0,1},{1,2},{2,3},{3,4},{4,5},{5,6},{6,7},{7,8},{8,9},{9,10},{10,1... | collective-permute-start | bytes 3932168 | tf_op jit(solution)/shard_map/ppermute | solution.py:621
  24.5 47.9 %collective-permute-start.1 = (bf16[640,1024]{1,0:T(8,128)(2,1)S(1)}, bf16[640,1024]{1,0:T(8,128)(2,1)}, u32[]{:S(2)}, u32[]{:S(2)}) collective-permute-start(bf16[640,1024]{1,0:T(8,128)(2,1)S(1)} %get-tuple-element.65), channel_id=1, source_target_pairs={{1,0},{2,1},{3,2},{4,3},{5,4},{6,5},{7,6},{8,7},{9,8},{10,9},{11,1... | collective-permute-start | bytes 3932168 | tf_op jit(solution)/shard_map/ppermute | solution.py:622
  40.0 35.8 %copy-start.1 = (bf16[2048,128]{1,0:T(8,128)(2,1)}, bf16[2048,128]{1,0:T(8,128)(2,1)S(1)}, u32[]{:S(2)}) copy-start(bf16[2048,128]{1,0:T(8,128)(2,1)S(1)} %convolution_convert_fusion.sel) | copy-start | bytes 1572868
  347.3 9.4 %copy-start.4 = (f32[1024,128]{1,0:T(8,128)S(1)}, f32[1024,128]{1,0:T(8,128)}, u32[]{:S(2)}) copy-start(f32[1024,128]{1,0:T(8,128)} %get-tuple-element.49) | copy-start | bytes 1572868
  347.3 9.5 %copy-start.3 = (f32[4096,128]{1,0:T(8,128)S(1)}, f32[4096,128]{1,0:T(8,128)}, u32[]{:S(2)}) copy-start(f32[4096,128]{1,0:T(8,128)} %get-tuple-element.47) | copy-start | bytes 6291460
  350.9 66.7 %collective-permute-start.2 = (bf16[640,1024]{1,0:T(8,128)(2,1)}, bf16[640,1024]{1,0:T(8,128)(2,1)}, u32[]{:S(2)}, u32[]{:S(2)}) collective-permute-start(bf16[640,1024]{1,0:T(8,128)(2,1)} %get-tuple-element.63), channel_id=1, source_target_pairs={{0,1},{1,2},{2,3},{3,4},{4,5},{5,6},{6,7},{7,8},{8,9},{9,10},{10,1... | collective-permute-start | bytes 3932168 | tf_op jit(solution)/shard_map/ppermute | solution.py:687
  355.4 62.3 %collective-permute-start.3 = (bf16[640,1024]{1,0:T(8,128)(2,1)}, bf16[640,1024]{1,0:T(8,128)(2,1)}, u32[]{:S(2)}, u32[]{:S(2)}) collective-permute-start(bf16[640,1024]{1,0:T(8,128)(2,1)} %get-tuple-element.62), channel_id=1, source_target_pairs={{1,0},{2,1},{3,2},{4,3},{5,4},{6,5},{7,6},{8,7},{9,8},{10,9},{11,1... | collective-permute-start | bytes 3932168 | tf_op jit(solution)/shard_map/ppermute | solution.py:688
  360.1 136.5 %collective-permute-start.11 = (f32[16,320,128]{2,1,0:T(8,128)S(1)}, f32[16,320,128]{2,1,0:T(8,128)}, u32[]{:S(2)}, u32[]{:S(2)}) collective-permute-start(f32[16,320,128]{2,1,0:T(8,128)S(1)} %pad_maximum_fusion.1), channel_id=1, source_target_pairs={{0,2},{1,3},{2,0},{3,1},{4,6},{5,7},{6,4},{7,5},{8,10},{9,11},{10,... | collective-permute-start | bytes 7864328 | tf_op jit(solution)/shard_map/ppermute | solution.py:601
  361.4 56.2 %collective-permute-start.4 = (f32[2,8,2,5,128]{4,3,2,1,0:T(8,128)}, f32[2,8,2,5,128]{4,3,2,1,0:T(8,128)S(1)}, u32[]{:S(2)}, u32[]{:S(2)}) collective-permute-start(f32[2,8,2,5,128]{4,3,2,1,0:T(8,128)} %get-tuple-element.83), channel_id=1, source_target_pairs={{0,1},{1,2},{2,3},{3,4},{4,5},{5,6},{6,7},{7,8},{8,9},{9,10},{10,1... | collective-permute-start | bytes 245768 | tf_op jit(solution)/shard_map/ppermute | solution.py:689
  366.0 51.7 %collective-permute-start.5 = (f32[2,8,2,5,128]{4,3,2,1,0:T(8,128)}, f32[2,8,2,5,128]{4,3,2,1,0:T(8,128)S(1)}, u32[]{:S(2)}, u32[]{:S(2)}) collective-permute-start(f32[2,8,2,5,128]{4,3,2,1,0:T(8,128)} %get-tuple-element.82), channel_id=1, source_target_pairs={{1,0},{2,1},{3,2},{4,3},{5,4},{6,5},{7,6},{8,7},{9,8},{10,9},{11,1... | collective-permute-start | bytes 245768 | tf_op jit(solution)/shard_map/ppermute | solution.py:690
  455.4 28.2 %collective-permute-start.6 = (f32[16,128,128]{2,1,0:T(8,128)}, f32[16,128,128]{2,1,0:T(8,128)}, u32[]{:S(2)}, u32[]{:S(2)}) collective-permute-start(f32[16,128,128]{2,1,0:T(8,128)} %pad_maximum_fusion.2), channel_id=1, source_target_pairs={{0,2},{1,3},{2,0},{3,1},{4,6},{5,7},{6,4},{7,5},{8,10},{9,11},{10,... | collective-permute-start | bytes 3145736 | tf_op jit(solution)/shard_map/ppermute | solution.py:601
  485.2 18.6 %collective-permute-start.7 = (bf16[8,128,128]{2,1,0:T(8,128)(2,1)S(1)}, bf16[8,128,128]{2,1,0:T(8,128)(2,1)S(1)}, u32[]{:S(2)}, u32[]{:S(2)}) collective-permute-start(bf16[8,128,128]{2,1,0:T(8,128)(2,1)S(1)} %fusion.3), channel_id=1, source_target_pairs={{0,1},{1,0},{2,3},{3,2},{4,5},{5,4},{6,7},{7,6},{8,9},{9,8},{10,11... | collective-permute-start | bytes 786440 | tf_op jit(solution)/shard_map/ppermute | solution.py:601
  500.2 18.1 %collective-permute-start.12 = (bf16[8,320,128]{2,1,0:T(8,128)(2,1)}, bf16[8,320,128]{2,1,0:T(8,128)(2,1)}, u32[]{:S(2)}, u32[]{:S(2)}) collective-permute-start(bf16[8,320,128]{2,1,0:T(8,128)(2,1)} %fusion), channel_id=1, source_target_pairs={{0,1},{1,0},{2,3},{3,2},{4,5},{5,4},{6,7},{7,6},{8,9},{9,8},{10,11... | collective-permute-start | bytes 1966088 | tf_op jit(solution)/shard_map/ppermute | solution.py:601
  503.8 14.3 %collective-permute-start.8 = (bf16[4,128,128]{2,1,0:T(8,128)(2,1)S(1)}, bf16[4,128,128]{2,1,0:T(8,128)(2,1)S(1)}, u32[]{:S(2)}, u32[]{:S(2)}) collective-permute-start(bf16[4,128,128]{2,1,0:T(8,128)(2,1)S(1)} %fusion.5), channel_id=1, source_target_pairs={{0,4},{1,5},{2,6},{3,7},{4,0},{5,1},{6,2},{7,3},{8,12},{9,13},{10,... | collective-permute-start | bytes 393224 | tf_op jit(solution)/shard_map/ppermute | solution.py:601
  518.2 11.8 %collective-permute-start.9 = (bf16[2,128,128]{2,1,0:T(8,128)(2,1)S(1)}, bf16[2,128,128]{2,1,0:T(8,128)(2,1)S(1)}, u32[]{:S(2)}, u32[]{:S(2)}) collective-permute-start(bf16[2,128,128]{2,1,0:T(8,128)(2,1)S(1)} %fusion.6), channel_id=1, source_target_pairs={{0,8},{1,9},{2,10},{3,11},{4,12},{5,13},{6,14},{7,15},{8,0},{9,1},... | collective-permute-start | bytes 196616 | tf_op jit(solution)/shard_map/ppermute | solution.py:601
  519.5 17.9 %collective-permute-start.13 = (bf16[4,320,128]{2,1,0:T(8,128)(2,1)S(1)}, bf16[4,320,128]{2,1,0:T(8,128)(2,1)S(1)}, u32[]{:S(2)}, u32[]{:S(2)}) collective-permute-start(bf16[4,320,128]{2,1,0:T(8,128)(2,1)S(1)} %fusion.2), channel_id=1, source_target_pairs={{0,4},{1,5},{2,6},{3,7},{4,0},{5,1},{6,2},{7,3},{8,12},{9,13},{10,... | collective-permute-start | bytes 983048 | tf_op jit(solution)/shard_map/ppermute | solution.py:601
  530.0 7.6 %collective-permute-start.10 = (bf16[1,128,128]{2,1,0:T(8,128)(2,1)S(1)}, bf16[1,128,128]{2,1,0:T(8,128)(2,1)S(1)}, u32[]{:S(2)}, u32[]{:S(2)}) collective-permute-start(bf16[1,128,128]{2,1,0:T(8,128)(2,1)S(1)} %dynamic-slice_convert_fusion.7), channel_id=1, source_target_pairs={{0,16},{1,17},{2,18},{3,19},{4,20},{5,21},{6,22},{7,23},{8,24},{9,... | collective-permute-start | bytes 98312 | tf_op jit(solution)/shard_map/ppermute | solution.py:601
  537.6 5.4 collective-permute-start.14
  543.0 5.8 %collective-permute-start.15 = (bf16[1,320,128]{2,1,0:T(8,128)(2,1)S(1)}, bf16[1,320,128]{2,1,0:T(8,128)(2,1)S(1)}, u32[]{:S(2)}, u32[]{:S(2)}) collective-permute-start(bf16[1,320,128]{2,1,0:T(8,128)(2,1)S(1)} %dynamic-slice_convert_fusion.5), channel_id=1, source_target_pairs={{0,16},{1,17},{2,18},{3,19},{4,20},{5,21},{6,22},{7,23},{8,24},{9,... | collective-permute-start | bytes 245768 | tf_op jit(solution)/shard_map/ppermute | solution.py:601
  (8 other events, 23.8 us)
Sparse Core Ops, SparseCore 0:
  13.5 97.6 all-gather.3
  114.1 85.0 all-gather.7
  202.1 86.8 all-gather.5

commit v2 on v1

v2 whole, which is shorter than its diff:
```python
import jax
import jax.numpy as jnp
from jax import lax
from jax.experimental import pallas as pl
from jax.experimental.pallas import tpu as pltpu
from jax.sharding import PartitionSpec as P


HEADS = 16
RANK = 16
ADAPTERS = 8
EPS = 1e-05
SLOPE = 1.702
NEG = -1000000000.0
AXES = ("fsdp", "dp")
LANES = 128
TILE = 256
HALO = 640
VMEM_LIMIT = 60 * 1024 * 1024
WIDE = 2

f32 = jnp.float32
bf16 = jnp.bfloat16


def dot_nn(a, b):
    return jnp.dot(a, b, preferred_element_type=f32)


def dot_nt(a, b):
    return lax.dot_general(a, b, (((1,), (1,)), ((), ())), preferred_element_type=f32)


def dot_tn(a, b):
    return lax.dot_general(a, b, (((0,), (0,)), ((), ())), preferred_element_type=f32)


def norm_forward(values, gain, shift):
    mean = jnp.mean(values, axis=1, keepdims=True)
    centered = values - mean
    inverse = lax.rsqrt(jnp.mean(centered * centered, axis=1, keepdims=True) + EPS)
    normed = centered * inverse
    return normed * gain + shift, normed, inverse


def norm_backward(grad, normed, inverse, gain):
    scaled = grad * gain
    return inverse * (
        scaled
        - jnp.mean(scaled, axis=1, keepdims=True)
        - normed * jnp.mean(scaled * normed, axis=1, keepdims=True)
    )


def params(grid_dims):
    return pltpu.CompilerParams(
        dimension_semantics=("arbitrary",) * grid_dims, vmem_limit_bytes=VMEM_LIMIT
    )


def whole(shape):
    return pl.BlockSpec(shape, lambda *_: (0,) * len(shape), pipeline_mode=pl.Buffered(1))


def twice(x):
    return jnp.concatenate([x, x], axis=1)


def qkv_kernel(tab, tok, sel, w, bq, bv, gain, shift, q_o, k_o, v_o):
    i = pl.program_id(0)
    needed = (i >= tab[12]) & (i <= tab[13])

    @pl.when(needed)
    def _():
        qkv_tile(tok, sel, w, bq, bv, gain, shift, q_o, k_o, v_o)

    @pl.when(jnp.logical_not(needed))
    def _():
        q_o[...] = jnp.zeros_like(q_o)
        k_o[...] = jnp.zeros_like(k_o)
        v_o[...] = jnp.zeros_like(v_o)


def qkv_tile(tok, sel, w, bq, bv, gain, shift, q_o, k_o, v_o):
    width = tok.shape[1]
    normal, _, _ = norm_forward(tok[...].astype(f32), gain[...], shift[...])
    n1 = normal.astype(bf16)
    select = sel[...]
    low = dot_nn(n1, w[:, 3 * width : 3 * width + 2 * LANES]).astype(bf16)
    low_q = low[:, :LANES] * select
    low_v = low[:, LANES:] * select
    q_out = w[:, 3 * width + 2 * LANES : 3 * width + 3 * LANES]
    v_out = w[:, 3 * width + 3 * LANES : 3 * width + 4 * LANES]
    scale = (width // HEADS) ** -0.5
    q = dot_nn(n1, w[:, :width]) + bq[...] + dot_nt(low_q, q_out)
    q_o[...] = (q * scale).astype(bf16)
    k_o[...] = dot_nn(n1, w[:, width : 2 * width]).astype(bf16)
    v = dot_nn(n1, w[:, 2 * width : 3 * width]) + bv[...] + dot_nt(low_v, v_out)
    v_o[...] = v.astype(bf16)


def qkv_call(tab, tok_w, sel_w, w_a, bq, bv, gain, shift):
    rows, width = tok_w.shape
    tile = pl.BlockSpec((TILE, width), lambda i, *_: (i, 0))
    vec = whole((1, width))
    out = jax.ShapeDtypeStruct((rows, width), bf16)
    return pl.pallas_call(
        qkv_kernel,
        grid_spec=pltpu.PrefetchScalarGridSpec(
            num_scalar_prefetch=1,
            grid=(rows // TILE,),
            in_specs=[
                tile,
                pl.BlockSpec((TILE, LANES), lambda i, *_: (i, 0)),
                whole((width, 3 * width + 4 * LANES)),
                vec,
                vec,
                vec,
                vec,
            ],
            out_specs=[tile] * 3,
        ),
        out_shape=[out] * 3,
        compiler_params=params(1),
        name="qkv",
    )(tab, tok_w, sel_w, w_a, bq, bv, gain, shift)


def head_masks(rows):
    lane = lax.broadcasted_iota(jnp.int32, (rows, LANES), 1)
    return lane < (LANES // 2)


def columns(c):
    return slice(c * LANES, (c + 1) * LANES)


def attend_kernel(tab, q, k, v, segc, segr, mixed_o, lse_o, s_scr):
    own = mixed_o.shape[0]
    wide = q.shape[1] // LANES
    first = head_masks(TILE)
    one = jnp.ones((), bf16)

    @pl.loop(0, own // TILE)
    def _(i):
        start, count = tab[2 * i], tab[2 * i + 1]
        row = pl.ds(pl.multiple_of(HALO + TILE * i, LANES), TILE)
        qs = [split_pair(q[row, columns(c)], first) for c in range(wide)]
        sq = twice(segc[row, :])

        def scores(t, carry):
            at = start + 2 * t
            here = pl.ds(pl.multiple_of(at * LANES, LANES), TILE)
            sk = jnp.concatenate([segr[pl.ds(at, 1), :], segr[pl.ds(at + 1, 1), :]], axis=1)
            mask = sq == sk
            out = []
            for c in range(wide):
                both = dot_nt(qs[c], k[here, columns(c)])
                for head in range(2):
                    x = jnp.where(mask, both[head * TILE : (head + 1) * TILE], NEG)
                    s_scr[2 * c + head, t] = x
                    out.append(
                        jnp.maximum(carry[2 * c + head], jnp.maximum(x[:, :LANES], x[:, LANES:]))
                    )
            return tuple(out)

        low = jnp.full((TILE, LANES), NEG, f32)
        tops = lax.fori_loop(0, count, scores, (low,) * (2 * wide))
        tops = [jnp.max(m, axis=1, keepdims=True) for m in tops]

        def weigh(t, carry):
            at = start + 2 * t
            here = pl.ds(pl.multiple_of(at * LANES, LANES), TILE)
            out = []
            for c in range(wide):
                vt = v[here, columns(c)]
                p0 = jnp.exp(s_scr[2 * c, t] - tops[2 * c]).astype(bf16)
                p1 = jnp.exp(s_scr[2 * c + 1, t] - tops[2 * c + 1]).astype(bf16)
                out.append(carry[2 * c] + dot_nn(p0, jnp.where(first, vt, one)))
                out.append(carry[2 * c + 1] + dot_nn(p1, jnp.where(first, one, vt)))
            return tuple(out)

        empty = jnp.zeros((TILE, LANES), f32)
        sums = lax.fori_loop(0, count, weigh, (empty,) * (2 * wide))
        for c in range(wide):
            a0, a1 = sums[2 * c], sums[2 * c + 1]
            r0 = pltpu.roll(a0, LANES // 2, 1)
            r1 = pltpu.roll(a1, LANES // 2, 1)
            out = jnp.where(first, a0 / r0, a1 / r1).astype(bf16)
            mixed_o[pl.ds(pl.multiple_of(TILE * i, TILE), TILE), columns(c)] = out
            l0 = (tops[2 * c] + jnp.log(jnp.where(first, r0, a0))).T
            l1 = (tops[2 * c + 1] + jnp.log(jnp.where(first, a1, r1))).T
            for half in range(2):
                at = 2 * i + half
                lse_o[c, 0, pl.ds(at, 1), :] = l0[0:1, columns(half)]
                lse_o[c, 1, pl.ds(at, 1), :] = l1[0:1, columns(half)]


def attend_call(tab, q, k, v, segc, segr, own):
    rows, width = q.shape
    pairs = width // LANES
    col = pl.BlockSpec((rows, WIDE * LANES), lambda h, *_: (0, h))
    return pl.pallas_call(
        attend_kernel,
        grid_spec=pltpu.PrefetchScalarGridSpec(
            num_scalar_prefetch=1,
            grid=(pairs // WIDE,),
            in_specs=[col, col, col, whole(segc.shape), whole(segr.shape)],
            out_specs=[
                pl.BlockSpec((own, WIDE * LANES), lambda h, *_: (0, h)),
                pl.BlockSpec((WIDE, 2, own // LANES, LANES), lambda h, *_: (h, 0, 0, 0)),
            ],
            scratch_shapes=[pltpu.VMEM((2 * WIDE, rows // TILE, TILE, TILE), f32)],
        ),
        out_shape=[
            jax.ShapeDtypeStruct((own, width), bf16),
            jax.ShapeDtypeStruct((pairs, 2, own // LANES, LANES), f32),
        ],
        compiler_params=params(1),
        name="attend",
    )(tab, q, k, v, segc, segr)


def split_pair(x, first):
    zero = jnp.zeros((), bf16)
    return jnp.concatenate([jnp.where(first, x, zero), jnp.where(first, zero, x)], axis=0)


def pair_grads(kt, vt, qcat, dcat, mask, lse0, lse1, dlt0, dlt1):
    half = qcat.shape[0] // 2
    s = dot_nt(kt, qcat)
    dp = dot_nt(vt, dcat)
    p0 = jnp.exp(jnp.where(mask, s[:, :half], NEG) - lse0)
    p1 = jnp.exp(jnp.where(mask, s[:, half:], NEG) - lse1)
    d0 = (p0 * (dp[:, :half] - dlt0)).astype(bf16)
    d1 = (p1 * (dp[:, half:] - dlt1)).astype(bf16)
    probs = jnp.concatenate([p0.astype(bf16), p1.astype(bf16)], axis=1)
    return probs, d0, d1


def attend_back_kernel(tab, q, k, v, dm, lse, dlt, segc, segr, dq_o, dk_o, dv_o, dk_a, dv_a):
    own = dm.shape[0]
    wide = q.shape[1] // LANES
    first = head_masks(TILE)
    scale = (LANES // 2) ** -0.5
    dk_a[...] = jnp.zeros_like(dk_a)
    dv_a[...] = jnp.zeros_like(dv_a)

    @pl.loop(0, own // TILE)
    def _(i):
        start, count = tab[2 * i], tab[2 * i + 1]
        row = pl.ds(pl.multiple_of(HALO + TILE * i, LANES), TILE)
        here = pl.ds(pl.multiple_of(TILE * i, TILE), TILE)
        qs = [split_pair(q[row, columns(c)], first) for c in range(wide)]
        ds = [split_pair(dm[here, columns(c)], first) for c in range(wide)]

        def line(ref, c, head):
            return jnp.concatenate(
                [ref[c, head, pl.ds(2 * i, 1), :], ref[c, head, pl.ds(2 * i + 1, 1), :]], axis=1
            )

        stats = [[line(ref, c, head) for ref in (lse, dlt) for head in range(2)] for c in range(wide)]
        at_q = HALO // LANES + 2 * i
        sq = jnp.concatenate([segr[pl.ds(at_q, 1), :], segr[pl.ds(at_q + 1, 1), :]], axis=1)

        def step(t, carry):
            at = pl.ds(pl.multiple_of((start + 2 * t) * LANES, LANES), TILE)
            mask = twice(segc[at, :]) == sq
            out = []
            for c in range(wide):
                kt = k[at, columns(c)]
                vt = v[at, columns(c)]
                probs, d0, d1 = pair_grads(kt, vt, qs[c], ds[c], mask, *stats[c])
                dv_a[at, columns(c)] += dot_nn(probs, ds[c])
                dk_a[at, columns(c)] += dot_nn(jnp.concatenate([d0, d1], axis=1), qs[c])
                out += [carry[2 * c] + dot_tn(d0, kt), carry[2 * c + 1] + dot_tn(d1, kt)]
            return tuple(out)

        empty = jnp.zeros((TILE, LANES), f32)
        sums = lax.fori_loop(0, count, step, (empty,) * (2 * wide))
        for c in range(wide):
            dq_o[here, columns(c)] = (
                jnp.where(first, sums[2 * c], sums[2 * c + 1]) * scale
            ).astype(bf16)

    dk_o[...] = dk_a[HALO : HALO + own, :]
    dv_o[...] = dv_a[HALO : HALO + own, :]


def attend_back_call(tab, q, k, v, dm, lse, dlt, segc, segr):
    rows, width = q.shape
    own = dm.shape[0]
    pairs = width // LANES
    col = pl.BlockSpec((rows, WIDE * LANES), lambda h, *_: (0, h))
    own_col = pl.BlockSpec((own, WIDE * LANES), lambda h, *_: (0, h))
    stat = pl.BlockSpec((WIDE, 2, own // LANES, LANES), lambda h, *_: (h, 0, 0, 0))
    return pl.pallas_call(
        attend_back_kernel,
        grid_spec=pltpu.PrefetchScalarGridSpec(
            num_scalar_prefetch=1,
            grid=(pairs // WIDE,),
            in_specs=[col, col, col, own_col, stat, stat, whole(segc.shape), whole(segr.shape)],
            out_specs=[own_col] * 3,
            scratch_shapes=[pltpu.VMEM((rows, WIDE * LANES), f32)] * 2,
        ),
        out_shape=[
            jax.ShapeDtypeStruct((own, width), bf16),
            jax.ShapeDtypeStruct((own, width), f32),
            jax.ShapeDtypeStruct((own, width), f32),
        ],
        compiler_params=params(1),
        name="attend_back",
    )(tab, q, k, v, dm, lse, dlt, segc, segr)


def halo_back_kernel(
    tab, q, k, v, dm_l, dm_r, st_l, st_r, dk_i, dv_i, segc, segr, dk_o, dv_o, dk_a, dv_a
):
    own = dk_o.shape[0]
    wide = q.shape[1] // LANES
    first = head_masks(LANES)
    dk_a[...] = dk_i[...]
    dv_a[...] = dv_i[...]
    for side in range(2):
        base = 6 + 3 * side
        count_q, k_first, count_k = tab[base], tab[base + 1], tab[base + 2]
        dm, st = (dm_l, st_l) if side == 0 else (dm_r, st_r)

        def query_tile(t, carry):
            tile = HALO // LANES - 1 - t if side == 0 else t
            tile_w = tile if side == 0 else tile + (HALO + own) // LANES
            at_h = pl.ds(pl.multiple_of(tile * LANES, LANES), LANES)
            at_w = pl.ds(pl.multiple_of(tile_w * LANES, LANES), LANES)
            qs = [split_pair(q[at_w, columns(c)], first) for c in range(wide)]
            ds = [split_pair(dm[at_h, columns(c)], first) for c in range(wide)]
            stats = [
                [st[kind, c, head, pl.ds(tile, 1), :] for kind in range(2) for head in range(2)]
                for c in range(wide)
            ]
            sq = segr[pl.ds(tile_w, 1), :]

            def key_tile(u, inner):
                at = pl.ds(pl.multiple_of((k_first + u) * TILE, TILE), TILE)
                at_k = pl.ds(pl.multiple_of(HALO + (k_first + u) * TILE, LANES), TILE)
                mask = segc[at_k, :] == sq
                for c in range(wide):
                    kt = k[at_k, columns(c)]
                    vt = v[at_k, columns(c)]
                    probs, d0, d1 = pair_grads(kt, vt, qs[c], ds[c], mask, *stats[c])
                    dv_a[at, columns(c)] += dot_nn(probs, ds[c])
                    dk_a[at, columns(c)] += dot_nn(jnp.concatenate([d0, d1], axis=1), qs[c])
                return inner

            return lax.fori_loop(0, count_k, key_tile, carry)

        lax.fori_loop(0, count_q, query_tile, 0)
    dk_o[...] = dk_a[...].astype(bf16)
    dv_o[...] = dv_a[...].astype(bf16)


def halo_back_call(tab, q, k, v, dm_l, dm_r, st_l, st_r, dk, dv, segc, segr):
    rows, width = q.shape
    own = dk.shape[0]
    pairs = width // LANES
    col = pl.BlockSpec((rows, WIDE * LANES), lambda h, *_: (0, h))
    own_col = pl.BlockSpec((own, WIDE * LANES), lambda h, *_: (0, h))
    halo_col = pl.BlockSpec((HALO, WIDE * LANES), lambda h, *_: (0, h))
    stat = pl.BlockSpec((2, WIDE, 2, HALO // LANES, LANES), lambda h, *_: (0, h, 0, 0, 0))
    return pl.pallas_call(
        halo_back_kernel,
        grid_spec=pltpu.PrefetchScalarGridSpec(
            num_scalar_prefetch=1,
            grid=(pairs // WIDE,),
            in_specs=[
                col,
                col,
                col,
                halo_col,
                halo_col,
                stat,
                stat,
                own_col,
                own_col,
                whole(segc.shape),
                whole(segr.shape),
            ],
            out_specs=[own_col] * 2,
            scratch_shapes=[pltpu.VMEM((own, WIDE * LANES), f32)] * 2,
        ),
        out_shape=[jax.ShapeDtypeStruct((own, width), bf16)] * 2,
        compiler_params=params(1),
        name="halo_back",
    )(tab, q, k, v, dm_l, dm_r, st_l, st_r, dk, dv, segc, segr)


FF_TILE = 512


def mlp_kernel(
    mixed, tok, dy, sel, w_out, w_up, w_lo, w_dn, w_x, b_out, b_up, b_down, gain, shift, heads,
    out_o, dres_o, dmix_o, head_o, tail_o, dlt_o, gui_o, gdo_o, guo_o, gdi_o,
    resid, n2, low_u, dlow_d, low_ut, dlow_dt, acc, acc_low, dn2, dlow_u, gdo_t, gui_t,
):
    j = pl.program_id(0)
    rows, width = mixed.shape
    chunks = [pl.ds(r, TILE) for r in range(0, rows, TILE)]
    up_in = w_lo[:, :LANES]
    down_out = w_lo[:, LANES:]
    out_w = w_out[...].reshape(width, width)

    @pl.when(j == 0)
    def _():
        for r in chunks:
            x = tok[r, :].astype(f32) + dot_nn(mixed[r, :], out_w) + b_out[...]
            resid[r, :] = x
            normal, _, _ = norm_forward(x, gain[...], shift[...])
            normal = normal.astype(bf16)
            n2[r, :] = normal
            lu = dot_nn(normal, up_in).astype(bf16) * sel[r, :]
            ld = dot_nn(dy[r, :], down_out).astype(bf16) * sel[r, :]
            low_u[r, :] = lu
            dlow_d[r, :] = ld
            low_ut[:, r] = lu.astype(f32).T.astype(bf16)
            dlow_dt[:, r] = ld.astype(f32).T.astype(bf16)
        acc[...] = jnp.zeros_like(acc)
        acc_low[...] = jnp.zeros_like(acc_low)
        dn2[...] = jnp.zeros_like(dn2)
        dlow_u[...] = jnp.zeros_like(dlow_u)
        gdo_t[...] = jnp.zeros_like(gdo_t)
        gui_t[...] = jnp.zeros_like(gui_t)

    down = w_dn[...].reshape(FF_TILE, width)
    up_w = w_up[...].reshape(width, FF_TILE)
    if len(w_x.shape) == 2:
        up_out, down_in = w_x[:, :LANES], w_x[:, LANES:]
    else:
        x = w_x[...]
        columns = [slice(c, c + LANES) for c in range(0, width, LANES)]
        half = len(columns) // 2
        up_out = jnp.concatenate([x[p, :, c] for p in range(x.shape[0]) for c in columns[:half]], axis=0)
        down_in = jnp.concatenate([x[p, :, c] for p in range(x.shape[0]) for c in columns[half:]], axis=0)
    guo_t = jnp.zeros((LANES, FF_TILE), f32)
    gdi_t = jnp.zeros((LANES, FF_TILE), f32)
    for r in chunks:
        pre = dot_nn(n2[r, :], up_w) + b_up[...] + dot_nt(low_u[r, :], up_out)
        d_act = dot_nt(dy[r, :], down) + dot_nt(dlow_d[r, :], down_in)
        gate = 1.0 / (1.0 + jnp.exp(-SLOPE * pre))
        act = pre * gate
        d_pre = (d_act * (gate + SLOPE * act * (1.0 - gate))).astype(bf16)
        act = act.astype(bf16)
        acc[r, :] += dot_nn(act, down)
        acc_low[r, :] += dot_nn(act, down_in)
        dn2[r, :] += dot_nt(d_pre, up_w)
        dlow_u[r, :] += dot_nn(d_pre, up_out)
        guo_t += dot_nn(low_ut[:, r], d_pre)
        gdi_t += dot_nn(dlow_dt[:, r], act)
    guo_o[...] = guo_t.T.astype(bf16)
    gdi_o[...] = gdi_t.T.astype(bf16)

    @pl.when(j == pl.num_programs(0) - 1)
    def _():
        for r in chunks:
            select = sel[r, :]
            x = resid[r, :]
            low_d = acc_low[r, :].astype(bf16) * select
            out_o[r, :] = (x + acc[r, :] + b_down[...] + dot_nt(low_d, down_out)).astype(bf16)
            lu = dlow_u[r, :].astype(bf16) * select
            _, hat, inv = norm_forward(x, gain[...], shift[...])
            grad = dn2[r, :] + dot_nt(lu, up_in)
            dres = dy[r, :].astype(f32) + norm_backward(grad, hat, inv, gain[...])
            dres_o[r, :] = dres
            dmix = dot_nt(dres.astype(bf16), out_w).astype(bf16)
            dmix_o[r, :] = dmix
            at = r.start
            upper = min(HALO - at, TILE)
            head_o[at : at + upper, :] = dmix[:upper]
            skip = max(rows - HALO - at, 0)
            first = at + skip - (rows - HALO)
            tail_o[first : first + TILE - skip, :] = dmix[skip:]
            prod = dmix.astype(f32) * mixed[r, :].astype(f32)
            high = prod.astype(bf16)
            rest = (prod - high.astype(f32)).astype(bf16)
            dlt_o[:, r] = dot_nt(heads[...], high) + dot_nt(heads[...], rest)
            gdo_t[...] += dot_nn(low_d.astype(f32).T.astype(bf16), dy[r, :])
            gui_t[...] += dot_nn(lu.astype(f32).T.astype(bf16), n2[r, :])
        gdo_o[...] = gdo_t[...].T.astype(bf16)
        gui_o[...] = gui_t[...].T.astype(bf16)


def mlp_call(mixed, tok, dy, sel, w_a, w_b, w_c, b_out, b_up, b_down, gain, shift, heads):
    rows, width = mixed.shape
    hidden = b_up.shape[1]
    full = whole((rows, width))
    vec = whole((1, width))
    low = whole((rows, LANES))
    at_low = (3 * width + 4 * LANES) // (2 * LANES)
    grads = jax.ShapeDtypeStruct((width, LANES), bf16)
    grads_ff = jax.ShapeDtypeStruct((hidden, LANES), bf16)
    const = lambda shape: pl.BlockSpec(shape, lambda j: (0,) * len(shape))
    once = pl.Buffered(1)
    ff_rows = pl.BlockSpec((FF_TILE, LANES), lambda j: (j, 0))
    if w_c is None:
        devices = w_b.shape[0]
        r, r_ff = width // devices, hidden // devices
        lead = (r_ff + r) // r
        per = width // FF_TILE
        at_x = lead + hidden // width
        group = FF_TILE // r_ff
        specs = [
            pl.BlockSpec((devices, r, width), lambda j: (0, r_ff // r, 0), pipeline_mode=once),
            pl.BlockSpec((devices, r, FF_TILE), lambda j: (0, lead + j // per, j % per)),
            pl.BlockSpec((group, r_ff, width), lambda j: (j, 0, 0)),
            pl.BlockSpec((group, r, width), lambda j: (j, at_x, 0)),
        ]
        weights = [w_b] * 4
    else:
        lead = width // FF_TILE
        specs = [
            whole((width, width)),
            pl.BlockSpec((width, FF_TILE), lambda j: (0, lead + j)),
            pl.BlockSpec((FF_TILE, width), lambda j: (j, 0)),
            pl.BlockSpec((FF_TILE, 2 * LANES), lambda j: (j, width // (2 * LANES))),
        ]
        weights = [w_b, w_b, w_c, w_c]
    return pl.pallas_call(
        mlp_kernel,
        grid=(hidden // FF_TILE,),
        in_specs=[
            full,
            full,
            full,
            low,
            specs[0],
            specs[1],
            pl.BlockSpec((width, 2 * LANES), lambda j: (0, at_low), pipeline_mode=once),
            specs[2],
            specs[3],
            vec,
            pl.BlockSpec((1, FF_TILE), lambda j: (0, j)),
            vec,
            vec,
            vec,
            whole(heads.shape),
        ],
        out_specs=[
            const((rows, width)),
            const((rows, width)),
            const((rows, width)),
            const((HALO, width)),
            const((HALO, width)),
            const((HEADS, rows)),
            const((width, LANES)),
            const((width, LANES)),
            ff_rows,
            ff_rows,
        ],
        out_shape=[
            jax.ShapeDtypeStruct((rows, width), bf16),
            jax.ShapeDtypeStruct((rows, width), f32),
            jax.ShapeDtypeStruct((rows, width), bf16),
            jax.ShapeDtypeStruct((HALO, width), bf16),
            jax.ShapeDtypeStruct((HALO, width), bf16),
            jax.ShapeDtypeStruct((HEADS, rows), f32),
            grads,
            grads,
            grads_ff,
            grads_ff,
        ],
        scratch_shapes=[
            pltpu.VMEM((rows, width), f32),
            pltpu.VMEM((rows, width), bf16),
            pltpu.VMEM((rows, LANES), bf16),
            pltpu.VMEM((rows, LANES), bf16),
            pltpu.VMEM((LANES, rows), bf16),
            pltpu.VMEM((LANES, rows), bf16),
            pltpu.VMEM((rows, width), f32),
            pltpu.VMEM((rows, LANES), f32),
            pltpu.VMEM((rows, width), f32),
            pltpu.VMEM((rows, LANES), f32),
            pltpu.VMEM((LANES, width), f32),
            pltpu.VMEM((LANES, width), f32),
        ],
        compiler_params=params(1),
        name="mlp",
    )(mixed, tok, dy, sel, weights[0], weights[1], w_a, weights[2], weights[3],
      b_out, b_up, b_down, gain, shift, heads)


def low_back_kernel(dq, dv, tok, sel, w, gain, shift, dlow_o, grads_o, acc):
    i = pl.program_id(0)
    normal, _, _ = norm_forward(tok[...].astype(f32), gain[...], shift[...])
    n1 = normal.astype(bf16)
    select = sel[...]
    low = dot_nn(n1, w[:, : 2 * LANES]).astype(bf16)
    low_q = low[:, :LANES] * select
    low_v = low[:, LANES:] * select
    dlow_q = dot_nn(dq[...], w[:, 2 * LANES : 3 * LANES]).astype(bf16) * select
    dlow_v = dot_nn(dv[...], w[:, 3 * LANES : 4 * LANES]).astype(bf16) * select
    dlow_o[:, :LANES] = dlow_q
    dlow_o[:, LANES:] = dlow_v

    @pl.when(i == 0)
    def _():
        acc[...] = jnp.zeros_like(acc)

    def turned(x):
        return x.astype(f32).T.astype(bf16)

    acc[0] += dot_nn(turned(dlow_q), n1)
    acc[1] += dot_nn(turned(low_q), dq[...])
    acc[2] += dot_nn(turned(dlow_v), n1)
    acc[3] += dot_nn(turned(low_v), dv[...])

    @pl.when(i == pl.num_programs(0) - 1)
    def _():
        for at in range(4):
            grads_o[at] = acc[at].T.astype(bf16)


def low_back_call(dq, dv, tok, sel, w_a, gain, shift):
    rows, width = tok.shape
    tile = pl.BlockSpec((TILE, width), lambda i: (i, 0))
    vec = whole((1, width))
    low = pl.BlockSpec((TILE, LANES), lambda i: (i, 0))
    at_low = 3 * width // (4 * LANES)
    return pl.pallas_call(
        low_back_kernel,
        grid=(rows // TILE,),
        in_specs=[
            tile,
            tile,
            tile,
            low,
            pl.BlockSpec((width, 4 * LANES), lambda i: (0, at_low), pipeline_mode=pl.Buffered(1)),
            vec,
            vec,
        ],
        out_specs=[
            pl.BlockSpec((TILE, 2 * LANES), lambda i: (i, 0)),
            pl.BlockSpec((4, width, LANES), lambda i: (0, 0, 0)),
        ],
        out_shape=[
            jax.ShapeDtypeStruct((rows, 2 * LANES), bf16),
            jax.ShapeDtypeStruct((4, width, LANES), bf16),
        ],
        scratch_shapes=[pltpu.VMEM((4, LANES, width), f32)],
        compiler_params=params(1),
        name="low_back",
    )(dq, dv, tok, sel, w_a, gain, shift)


def qkv_back_kernel(dq, dk, dv, dlow, tok, dres, w, gain, shift, gin_o):
    width = tok.shape[1]
    _, hat, inv = norm_forward(tok[...].astype(f32), gain[...], shift[...])
    grad = (
        dot_nt(dq[...], w[:, :width])
        + dot_nt(dk[...], w[:, width : 2 * width])
        + dot_nt(dv[...], w[:, 2 * width : 3 * width])
        + dot_nt(dlow[...], w[:, 3 * width : 3 * width + 2 * LANES])
    )
    gin_o[...] = (dres[...] + norm_backward(grad, hat, inv, gain[...])).astype(bf16)


def qkv_back_call(dq, dk, dv, dlow, tok, dres, w_a, gain, shift):
    rows, width = tok.shape
    tile = pl.BlockSpec((TILE, width), lambda i: (i, 0))
    vec = whole((1, width))
    return pl.pallas_call(
        qkv_back_kernel,
        grid=(rows // TILE,),
        in_specs=[
            tile,
            tile,
            tile,
            pl.BlockSpec((TILE, 2 * LANES), lambda i: (i, 0)),
            tile,
            tile,
            whole((width, 3 * width + 4 * LANES)),
            vec,
            vec,
        ],
        out_specs=tile,
        out_shape=jax.ShapeDtypeStruct((rows, width), bf16),
        compiler_params=params(1),
        name="qkv_back",
    )(dq, dk, dv, dlow, tok, dres, w_a, gain, shift)


def summed(parts, devices):
    packed = jnp.concatenate([p.reshape(devices, -1, p.shape[-1]) for p in parts], axis=1)
    got = lax.all_to_all(packed, AXES, 0, 0, tiled=True)
    return jnp.sum(got.astype(f32), axis=0)


def local(
    tokens, cotangent, segments, adapter_ids, ln1_gain, ln1_bias, w_query, b_query, w_key, w_value,
    b_value, w_out, b_out, ln2_gain, ln2_bias, w_up, b_up, w_down, b_down, query_in, query_out,
    value_in, value_out, up_in, up_out, down_in, down_out,
):
    own, width = tokens.shape
    inner = lax.axis_size("dp")
    devices = lax.axis_size("fsdp") * inner
    up = [(i, i + 1) for i in range(devices - 1)]
    down = [(i + 1, i) for i in range(devices - 1)]

    def gather(*pieces):
        return lax.all_gather(jnp.concatenate(pieces, axis=1), AXES, axis=0, tiled=True)

    before = lax.ppermute(tokens[own - HALO :], AXES, up)
    after = lax.ppermute(tokens[:HALO], AXES, down)
    w_a = gather(w_query, w_key, w_value, query_in, value_in, query_out, value_out, up_in, down_out)
    r, r_ff = w_out.shape[0], w_down.shape[0]
    if inner == 2 and r % 16 == 0 and 2 * LANES * (r_ff // r) == width:
        chunks = [slice(c, c + r) for c in range(0, r_ff, r)]
        low_maps = jnp.concatenate([m[c] for m in (up_out, down_in) for c in chunks], axis=1)
        up_blocks = [w_up[:, c : c + width] for c in range(0, w_up.shape[1], width)]
        mine = jnp.concatenate([w_down, w_out, *up_blocks, low_maps], axis=0)
        theirs = lax.ppermute(mine, "dp", [(0, 1), (1, 0)])
        is_first = lax.axis_index("dp") == 0
        both = jnp.stack([jnp.where(is_first, mine, theirs), jnp.where(is_first, theirs, mine)])
        w_b = lax.all_gather(both, "fsdp", axis=0, tiled=True)
        w_c = None
    else:
        w_b = gather(w_out, w_up)
        w_c = gather(w_down, up_out, down_in)

    position = lax.axis_index(AXES)
    padded = jnp.concatenate(
        [
            jnp.full((HALO,), -1, jnp.int32),
            segments,
            jnp.full((HALO,), 1 << 30, jnp.int32),
        ]
    )
    rows = own + 2 * HALO
    seg_w = lax.dynamic_slice_in_dim(padded, position * own, rows, 0)
    tile_seg = seg_w[HALO : HALO + own].reshape(own // TILE, TILE)
    images = jnp.concatenate([tile_seg[:, 0], tile_seg[:, -1]])
    low = jnp.sum((seg_w[None, :] < images[:, None]).astype(jnp.int32), axis=1)
    high = jnp.sum((seg_w[None, :] <= images[:, None]).astype(jnp.int32), axis=1)
    tiles = own // TILE
    entries = []
    for i in range(tiles):
        start = low[i] // LANES
        count = (high[tiles + i] - start * LANES + TILE - 1) // TILE
        entries += [jnp.minimum(start, rows // LANES - 2 * count), count]
    count_l = (HALO - low[0] + LANES - 1) // LANES
    entries += [
        jnp.maximum(count_l, 0),
        jnp.zeros((), jnp.int32),
        (jnp.minimum(high[0], HALO + own) - HALO + TILE - 1) // TILE,
    ]
    last = 2 * tiles - 1
    first_k = jnp.maximum(low[last] - HALO, 0) // TILE
    entries += [
        jnp.maximum((high[last] - HALO - own + LANES - 1) // LANES, 0),
        first_k,
        tiles - first_k,
        low[0] // TILE,
        (high[last] - 1) // TILE,
    ]
    tab = jnp.stack(entries)
    segr = seg_w.reshape(rows // LANES, LANES)
    segc = jnp.broadcast_to(seg_w[:, None], (rows, LANES))

    image_hot = (seg_w[:, None] == jnp.arange(adapter_ids.shape[0], dtype=jnp.int32)).astype(bf16)
    column = jnp.arange(ADAPTERS * RANK, dtype=jnp.int32) // RANK
    adapter_hot = (adapter_ids[:, None] == column[None, :]).astype(bf16)
    sel_w = dot_nn(image_hot, adapter_hot).astype(bf16)
    sel = sel_w[HALO : HALO + own]
    heads = (
        jnp.arange(width, dtype=jnp.int32)[None, :] // (width // HEADS)
        == jnp.arange(HEADS, dtype=jnp.int32)[:, None]
    ).astype(bf16)

    row = lambda x: x.reshape(1, -1)
    tok_w = jnp.concatenate([before, tokens, after], axis=0)
    q, k, v = qkv_call(
        tab, tok_w, sel_w, w_a, row(b_query), row(b_value), row(ln1_gain), row(ln1_bias)
    )
    mixed, lse = attend_call(tab, q, k, v, segc, segr, own)
    block_out, d_resid, d_mixed, dm_head, dm_tail, delta, g_ui, g_do, g_uo, g_di = mlp_call(
        mixed, tokens, cotangent, sel, w_a, w_b, w_c, row(b_out), row(b_up), row(b_down),
        row(ln2_gain), row(ln2_bias), heads,
    )
    dlt = delta.reshape(lse.shape)
    stats = jnp.stack([lse, dlt])
    cut = (own - HALO) // LANES
    dm_l = lax.ppermute(dm_tail, AXES, up)
    dm_r = lax.ppermute(dm_head, AXES, down)
    st_l = lax.ppermute(stats[:, :, :, cut:], AXES, up)
    st_r = lax.ppermute(stats[:, :, :, : HALO // LANES], AXES, down)
    mlp_grads = summed([g_ui, g_uo, g_di, g_do], devices)
    dq, dk, dv = attend_back_call(tab, q, k, v, d_mixed, lse, dlt, segc, segr)
    dk, dv = halo_back_call(tab, q, k, v, dm_l, dm_r, st_l, st_r, dk, dv, segc, segr)
    dlow, g_qv = low_back_call(dq, dv, tokens, sel, w_a, row(ln1_gain), row(ln1_bias))
    qv_grads = summed([g_qv[0], g_qv[1], g_qv[2], g_qv[3]], devices)
    grad_input = qkv_back_call(
        dq, dk, dv, dlow, tokens, d_resid, w_a, row(ln1_gain), row(ln1_bias)
    )
    return (
        block_out,
        grad_input,
        qv_grads[:r],
        qv_grads[r : 2 * r],
        qv_grads[2 * r : 3 * r],
        qv_grads[3 * r :],
        mlp_grads[:r],
        mlp_grads[r : r + r_ff],
        mlp_grads[r + r_ff : r + 2 * r_ff],
        mlp_grads[r + 2 * r_ff :],
    )


def solution(mesh):
    split = P(AXES, None)
    return jax.shard_map(
        local,
        mesh=mesh,
        in_specs=(
            split, split, P(), P(), P(), P(), split, P(), split, split, P(), split, P(), P(), P(),
            split, P(), split, P(), split, split, split, split, split, split, split, split,
        ),
        out_specs=(split,) * 10,
        check_vma=False,
    )
```

time: 555 us -> 504 us (0.908)
  starting transfers between devices: 77.9 us -> 46.6 us
  waiting for transfers between devices: 196 us -> 171 us
    all_gather x3 -> x1, waiting for transfers between devices: 139 us -> 0.32 us  [gather(): lax.all_gather(jnp.concatenate(pieces, axis=1), AXES, axis=0, tiled=True)]
    all_to_all x0 -> x2, waiting for transfers between devices: none -> 70.5 us  [summed(): got = lax.all_to_all(packed, AXES, 0, 0, tiled=True)]
    ppermute x12 -> x3, starting transfers between devices: 64.7 us -> 7.75 us  [the longest x1 3.46 us: local(): dm_l = lax.ppermute(dm_tail, AXES, up)]
    all_gather x0 -> x1, waiting for transfers between devices: none -> 44.8 us  [local(): w_b = lax.all_gather(both, 'fsdp', axis=0, tiled=True)]
    all_to_all x0 -> x2, starting transfers between devices: none -> 27.7 us  [summed(): got = lax.all_to_all(packed, AXES, 0, 0, tiled=True)]
    unnamed x32 -> x49, local copies, waits for them, and re-layouts: 7.37 us -> 19.1 us
    ppermute x12 -> x3, waiting for transfers between devices: 27 us -> 16.2 us  [the longest x1 16.2 us: local(): theirs = lax.ppermute(mine, 'dp', [(0, 1), (1, 0)])]
    ppermute x1, waiting for transfers between devices: 29.2 us -> 37.5 us  [local(): before = lax.ppermute(tokens[own - HALO:], AXES, up)]
  transfers between devices with their start and end apart: 19 -> 11, of which waited for: 11 -> 7; matrix products, arithmetic and copies ran while one was open for 5% -> 6% of each run, Pallas kernels for 28% -> 26%
where the time goes in v2:
time: 504 us; the launch traced here: 502 us
  Pallas kernels  215 us (43%)
  waiting for transfers between devices  171 us (34%)
  starting transfers between devices  46.6 us (9%)
  local copies, waits for them, and re-layouts  30.8 us (6%)
  between operations  27.6 us (5%)
  other arithmetic  11 us (2%)
    all_to_all x2, waiting for transfers between devices, summed(): got = lax.all_to_all(packed, AXES, 0, 0, tiled=True)  70.5 us
    pallas_call x1, Pallas kernels, mlp_call(): pl.pallas_call(mlp_kernel, grid=(hidden // FF_TILE,), in_specs=[full, ful...  59.2 us
    pallas_call x1, Pallas kernels, attend_back_call(): pl.pallas_call(attend_back_kernel, grid_spec=pltpu.PrefetchScalarGridSpec...  55.1 us
    all_gather x1, waiting for transfers between devices, local(): w_b = lax.all_gather(both, 'fsdp', axis=0, tiled=True)  44.8 us
    pallas_call x1, Pallas kernels, attend_call(): pl.pallas_call(attend_kernel, grid_spec=pltpu.PrefetchScalarGridSpec(num_...  43.3 us
    ppermute x1, waiting for transfers between devices, local(): before = lax.ppermute(tokens[own - HALO:], AXES, up)  37.5 us
    all_to_all x2, starting transfers between devices, summed(): got = lax.all_to_all(packed, AXES, 0, 0, tiled=True)  27.7 us
    pallas_call x1, Pallas kernels, qkv_call(): pl.pallas_call(qkv_kernel, grid_spec=pltpu.PrefetchScalarGridSpec(num_sca...  21.7 us
  transfers between devices with their start and end apart: 11, of which 7 were waited for; matrix products, arithmetic and copies ran while one was open for 6% of the time, Pallas kernels for 26%

profile of v2, /device:TPU:0, one launch (start us, length us, event | category | flops | bytes accessed | tf_op | source)
XLA Modules:
  0.0 502.0 jit_solution(15487963743253287141)
XLA Ops:
  25.6 3.0 collective-permute-start.2
  28.6 16.2 %collective-permute-done.2 = bf16[320,1024]{1,0:T(8,128)(2,1)S(1)} collective-permute-done((bf16[320,1024]{1,0:T(8,128)(2,1)S(1)}, bf16[320,1024]{1,0:T(8,128)(2,1)S(1)}, u32[]{:S(2)}, u32[]{:S(2)}) %collective-permute-start.2) | collective-permute-done | bytes 655392 | tf_op jit(solution)/shard_map/ppermute | solution.py:718
  48.0 3.3 collective-permute-start
  70.3 37.5 %collective-permute-done = bf16[640,1024]{1,0:T(8,128)(2,1)} collective-permute-done((bf16[640,1024]{1,0:T(8,128)(2,1)}, bf16[640,1024]{1,0:T(8,128)(2,1)}, u32[]{:S(2)}, u32[]{:S(2)}) %collective-permute-start) | collective-permute-done | bytes 1310752 | tf_op jit(solution)/shard_map/ppermute | solution.py:709
  107.8 1.6 collective-permute-done.1
  109.4 3.6 pad_maximum_fusion.tok
  113.3 21.7 %qkv.1 = (bf16[2048,1024]{1,0:T(8,128)(2,1)}, bf16[2048,1024]{1,0:T(8,128)(2,1)}, bf16[2048,1024]{1,0:T(8,128)(2,1)}) custom-call(s32[14]{0:T(128)} %stack.70.tab, bf16[2048,1024]{1,0:T(8,128)(2,1)} %pad_maximum_fusion.tok, bf16[2048,128]{1,0:T(8,128)(2,1)} %copy-done.1, bf16[1024,3840]{1,0:T(8,128)(2,1)} %all-gather.3.cloned.1.call-done.w.w_lo, ...), custom_call_target="tpu_custom_call" | custom-call | tf_op jit(solution)/shard_map/qkv/pallas_call | solution.py:107
  135.1 1.3 broadcast_in_dim.8.segc
  136.4 43.3 %attend.1 = (bf16[768,1024]{1,0:T(8,128)(2,1)}, f32[8,2,6,128]{3,2,1,0:T(8,128)}) custom-call(s32[14]{0:T(128)} %stack.70.tab, bf16[2048,1024]{1,0:T(8,128)(2,1)} %get-tuple-element.32.q, bf16[2048,1024]{1,0:T(8,128)(2,1)} %get-tuple-element.33.k, bf16[2048,1024]{1,0:T(8,128)(2,1)} %get-tuple-element.34.v, s32[2048,128]{1,0:T(8,128)} %broadcast_in_dim.8.segc, ...), custom_call_target="tpu_custom_call" | custom-call | tf_op jit(solution)/shard_map/attend/pallas_call | solution.py:203
  179.7 44.8 %all-gather.5.cloned.1.call-done.w_out.w_up.w_dn.w_x = bf16[32,320,1024]{2,1,0:T(8,128)(2,1)} async-done(((bf16[2,320,1024]{2,1,0:T(8,128)(2,1)}), bf16[32,320,1024]{2,1,0:T(8,128)(2,1)}) %all-gather.5.cloned.1.call-update) | async-done | bytes 20971536 | tf_op jit(solution)/shard_map/all_gather | solution.py:721
  224.5 59.2 %mlp.1 = (bf16[768,1024]{1,0:T(8,128)(2,1)}, f32[768,1024]{1,0:T(8,128)}, bf16[768,1024]{1,0:T(8,128)(2,1)}, bf16[640,1024]{1,0:T(8,128)(2,1)}, bf16[640,1024]{1...) custom-call(bf16[768,1024]{1,0:T(8,128)(2,1)} %get-tuple-element.35., ...), custom_call_target="tpu_custom_call" | custom-call | tf_op jit(solution)/shard_map/mlp/pallas_call | solution.py:525
  283.8 3.5 collective-permute-start.3
  290.7 5.2 %collective-permute-start.5 = (f32[2,8,2,5,128]{4,3,2,1,0:T(8,128)S(1)}, f32[2,8,2,5,128]{4,3,2,1,0:T(8,128)S(1)}, u32[]{:S(2)}, u32[]{:S(2)}) collective-permute-start(f32[2,8,2,5,128]{4,3,2,1,0:T(8,128)S(1)} %get-tuple-element.71), channel_id=1, source_target_pairs={{0,1},{1,2},{2,3},{3,4},{4,5},{5,6},{6,7},{7,8},{8,9},{9,10},{10,1... | collective-permute-start | bytes 245768 | tf_op jit(solution)/shard_map/ppermute | solution.py:791
  295.9 1.4 reshape.154.dlt
  297.3 55.1 %attend_back.1 = (bf16[768,1024]{1,0:T(8,128)(2,1)}, f32[768,1024]{1,0:T(8,128)}, f32[768,1024]{1,0:T(8,128)}) custom-call(s32[14]{0:T(128)} %stack.70.tab, bf16[2048,1024]{1,0:T(8,128)(2,1)} %get-tuple-element.32.q, bf16[2048,1024]{1,0:T(8,128)(2,1)} %get-tuple-element.33.k, bf16[2048,1024]{1,0:T(8,128)(2,1)} %get-tuple-element.34.v, ...), custom_call_target="tpu_custom_call" | custom-call | tf_op jit(solution)/shard_map/attend_back/pallas_call | solution.py:297
  354.0 15.7 %halo_back.1 = (bf16[768,1024]{1,0:T(8,128)(2,1)}, bf16[768,1024]{1,0:T(8,128)(2,1)}) custom-call(s32[14]{0:T(128)} %stack.70.tab, bf16[2048,1024]{1,0:T(8,128)(2,1)} %get-tuple-element.32.q, bf16[2048,1024]{1,0:T(8,128)(2,1)} %get-tuple-element.33.k, bf16[2048,1024]{1,0:T(8,128)(2,1)} %get-tuple-element.34.v, bf16[640,1024]{1,0:T(8,128)(2,1)} %copy-done.2, ...), custom_call_target="tpu_custom_call" | custom-call | tf_op jit(solution)/shard_map/halo_back/pallas_call | solution.py:369
  369.7 7.5 %low_back.1 = (bf16[768,256]{1,0:T(8,128)(2,1)}, bf16[4,1024,128]{2,1,0:T(8,128)(2,1)}) custom-call(bf16[768,1024]{1,0:T(8,128)(2,1)} %get-tuple-element.40.dq, bf16[768,1024]{1,0:T(8,128)(2,1)} %get-tuple-element.46.dv, bf16[768,1024]{1,0:T(8,128)(2,1)} %tok.5, bf16[768,128]{1,0:T(8,128)(2,1)} %slice.167.sel, ...), custom_call_target="tpu_custom_call" | custom-call | tf_op jit(solution)/shard_map/low_back/pallas_call | solution.py:626
  379.6 24.1 %all-to-all-start = ((bf16[32,128,128]{2,1,0:T(8,128)(2,1)}), bf16[32,128,128]{2,1,0:T(8,128)(2,1)}, u32[]{:S(2)}, u32[]{:S(2)}) async-start(bf16[32,128,128]{2,1,0:T(8,128)(2,1)} %pad_maximum_fusion.3), calls=%async_computation | async-start | bytes 2097152 | tf_op jit(solution)/shard_map/all_to_all | solution.py:691
  403.8 1.6 pad_maximum_fusion.1
  405.4 24.5 %all-to-all-done = bf16[32,128,128]{2,1,0:T(8,128)(2,1)} async-done(((bf16[32,128,128]{2,1,0:T(8,128)(2,1)}), bf16[32,128,128]{2,1,0:T(8,128)(2,1)}, u32[]{:S(2)}, u32[]{:S(2)}) %all-to-all-start) | async-done | bytes 1048608 | tf_op jit(solution)/shard_map/all_to_all | solution.py:691
  429.9 3.6 all-to-all-start.1
  433.5 12.0 %qkv_back.1 = bf16[768,1024]{1,0:T(8,128)(2,1)} custom-call(bf16[768,1024]{1,0:T(8,128)(2,1)} %get-tuple-element.40.dq, bf16[768,1024]{1,0:T(8,128)(2,1)} %get-tuple-element.45.dk, bf16[768,1024]{1,0:T(8,128)(2,1)} %get-tuple-element.46.dv, bf16[768,256]{1,0:T(8,128)(2,1)} %get-tuple-element.47.dlow, bf16[768,1024]{1,0:T(8,128)(2,1)} %tok.5, ...), custom_call_target="tpu_custom_call" | custom-call | tf_op jit(solution)/shard_map/qkv_back/pallas_call | solution.py:668
  445.6 1.4 convert_reduce_fusion.1
  447.6 46.0 %all-to-all-done.1 = bf16[32,320,128]{2,1,0:T(8,128)(2,1)S(1)} async-done(((bf16[32,320,128]{2,1,0:T(8,128)(2,1)}), bf16[32,320,128]{2,1,0:T(8,128)(2,1)S(1)}, u32[]{:S(2)}, u32[]{:S(2)}) %all-to-all-start.1) | async-done | bytes 2621472 | tf_op jit(solution)/shard_map/all_to_all | solution.py:691
  (90 shorter events, 37.2 us)
Async XLA Ops:
  7.2 106.2 %all-gather.3.cloned.1.call-start = ((), (), s32[]{:S(2)}) async-start(), calls=%async_computation.2 | async-start | bytes 8110080 | tf_op jit(solution)/shard_map/all_gather | solution.py:707
  14.0 0.7 copy-start.6
  14.7 209.8 %all-gather.5.cloned.1.call-start = ((), (), s32[]{:S(2)}) async-start(), calls=%async_computation.3 | async-start | bytes 22282240 | tf_op jit(solution)/shard_map/all_gather | solution.py:721
  25.6 19.2 %collective-permute-start.2 = (bf16[320,1024]{1,0:T(8,128)(2,1)S(1)}, bf16[320,1024]{1,0:T(8,128)(2,1)S(1)}, u32[]{:S(2)}, u32[]{:S(2)}) collective-permute-start(bf16[320,1024]{1,0:T(8,128)(2,1)S(1)} %constant_dynamic-update-slice_fusion.12), channel_id=1, source_target_pairs={{0,1},{1,0},{2,3},{3,2},{4,5},{5,4},{6,7},{7,6},{8,9},{9,8},{10,11... | collective-permute-start | bytes 1966088 | tf_op jit(solution)/shard_map/ppermute | solution.py:718
  44.8 1.9 copy-start
  46.7 5.9 %copy-start.7 = (s32[24576]{0:T(1024)S(1)}, s32[24576]{0:T(1024)}, u32[]{:S(2)}) copy-start(s32[24576]{0:T(1024)} %param.29) | copy-start | bytes 294916
  46.7 20.4 %copy-start.13 = (s32[48]{0:T(128)S(1)}, s32[48]{0:T(128)}, u32[]{:S(2)}) copy-start(s32[48]{0:T(128)} %param.30) | copy-start | bytes 580
  48.0 59.8 %collective-permute-start = (bf16[640,1024]{1,0:T(8,128)(2,1)}, bf16[640,1024]{1,0:T(8,128)(2,1)}, u32[]{:S(2)}, u32[]{:S(2)}) collective-permute-start(bf16[640,1024]{1,0:T(8,128)(2,1)} %get-tuple-element.58), channel_id=1, source_target_pairs={{0,1},{1,2},{2,3},{3,4},{4,5},{5,6},{6,7},{7,8},{8,9},{9,10},{10,1... | collective-permute-start | bytes 3932168 | tf_op jit(solution)/shard_map/ppermute | solution.py:709
  51.3 58.1 %collective-permute-start.1 = (bf16[640,1024]{1,0:T(8,128)(2,1)S(1)}, bf16[640,1024]{1,0:T(8,128)(2,1)}, u32[]{:S(2)}, u32[]{:S(2)}) collective-permute-start(bf16[640,1024]{1,0:T(8,128)(2,1)S(1)} %get-tuple-element.59), channel_id=1, source_target_pairs={{1,0},{2,1},{3,2},{4,3},{5,4},{6,5},{7,6},{8,7},{9,8},{10,9},{11,1... | collective-permute-start | bytes 3932168 | tf_op jit(solution)/shard_map/ppermute | solution.py:710
  67.6 45.4 %copy-start.1 = (bf16[2048,128]{1,0:T(8,128)(2,1)}, bf16[2048,128]{1,0:T(8,128)(2,1)S(1)}, u32[]{:S(2)}) copy-start(bf16[2048,128]{1,0:T(8,128)(2,1)S(1)} %convolution_convert_fusion.sel) | copy-start | bytes 1572868
  224.5 64.8 %copy-start.8 = (f32[8,2,6,128]{3,2,1,0:T(8,128)S(1)}, f32[8,2,6,128]{3,2,1,0:T(8,128)}, u32[]{:S(2)}) copy-start(f32[8,2,6,128]{3,2,1,0:T(8,128)} %get-tuple-element.38.lse) | copy-start | bytes 147460
  283.8 68.7 %collective-permute-start.3 = (bf16[640,1024]{1,0:T(8,128)(2,1)}, bf16[640,1024]{1,0:T(8,128)(2,1)S(1)}, u32[]{:S(2)}, u32[]{:S(2)}) collective-permute-start(bf16[640,1024]{1,0:T(8,128)(2,1)} %get-tuple-element.41), channel_id=1, source_target_pairs={{0,1},{1,2},{2,3},{3,4},{4,5},{5,6},{6,7},{7,8},{8,9},{9,10},{10,1... | collective-permute-start | bytes 3932168 | tf_op jit(solution)/shard_map/ppermute | solution.py:789
  287.2 65.2 %collective-permute-start.4 = (bf16[640,1024]{1,0:T(8,128)(2,1)}, bf16[640,1024]{1,0:T(8,128)(2,1)S(1)}, u32[]{:S(2)}, u32[]{:S(2)}) collective-permute-start(bf16[640,1024]{1,0:T(8,128)(2,1)} %get-tuple-element.42), channel_id=1, source_target_pairs={{1,0},{2,1},{3,2},{4,3},{5,4},{6,5},{7,6},{8,7},{9,8},{10,9},{11,1... | collective-permute-start | bytes 3932168 | tf_op jit(solution)/shard_map/ppermute | solution.py:790
  289.4 63.0 %collective-permute-start.6 = (f32[2,8,2,5,128]{4,3,2,1,0:T(8,128)S(1)}, f32[2,8,2,5,128]{4,3,2,1,0:T(8,128)S(1)}, u32[]{:S(2)}, u32[]{:S(2)}) collective-permute-start(f32[2,8,2,5,128]{4,3,2,1,0:T(8,128)S(1)} %get-tuple-element.70), channel_id=1, source_target_pairs={{1,0},{2,1},{3,2},{4,3},{5,4},{6,5},{7,6},{8,7},{9,8},{10,9},{11,1... | collective-permute-start | bytes 245768 | tf_op jit(solution)/shard_map/ppermute | solution.py:792
  290.7 61.7 %collective-permute-start.5 = (f32[2,8,2,5,128]{4,3,2,1,0:T(8,128)S(1)}, f32[2,8,2,5,128]{4,3,2,1,0:T(8,128)S(1)}, u32[]{:S(2)}, u32[]{:S(2)}) collective-permute-start(f32[2,8,2,5,128]{4,3,2,1,0:T(8,128)S(1)} %get-tuple-element.71), channel_id=1, source_target_pairs={{0,1},{1,2},{2,3},{3,4},{4,5},{5,6},{6,7},{7,8},{8,9},{9,10},{10,1... | collective-permute-start | bytes 245768 | tf_op jit(solution)/shard_map/ppermute | solution.py:791
  352.4 0.7 copy-start.12
  352.4 1.1 copy-start.2
  352.5 1.5 copy-start.3
  378.5 25.2 %copy-start.4 = (bf16[4096,128]{1,0:T(8,128)(2,1)S(1)}, bf16[4096,128]{1,0:T(8,128)(2,1)}, u32[]{:S(2)}) copy-start(bf16[4096,128]{1,0:T(8,128)(2,1)} %get-tuple-element.51) | copy-start | bytes 3145732
  378.5 25.2 %copy-start.5 = (bf16[4096,128]{1,0:T(8,128)(2,1)S(1)}, bf16[4096,128]{1,0:T(8,128)(2,1)}, u32[]{:S(2)}) copy-start(bf16[4096,128]{1,0:T(8,128)(2,1)} %get-tuple-element.52) | copy-start | bytes 3145732
  378.5 25.2 %copy-start.9 = (bf16[1024,128]{1,0:T(8,128)(2,1)S(1)}, bf16[1024,128]{1,0:T(8,128)(2,1)}, u32[]{:S(2)}) copy-start(bf16[1024,128]{1,0:T(8,128)(2,1)} %get-tuple-element.50) | copy-start | bytes 786436
  378.5 25.2 %copy-start.10 = (bf16[1024,128]{1,0:T(8,128)(2,1)S(1)}, bf16[1024,128]{1,0:T(8,128)(2,1)}, u32[]{:S(2)}) copy-start(bf16[1024,128]{1,0:T(8,128)(2,1)} %get-tuple-element.53) | copy-start | bytes 786436
  379.6 50.3 %all-to-all-start = ((bf16[32,128,128]{2,1,0:T(8,128)(2,1)}), bf16[32,128,128]{2,1,0:T(8,128)(2,1)}, u32[]{:S(2)}, u32[]{:S(2)}) async-start(bf16[32,128,128]{2,1,0:T(8,128)(2,1)} %pad_maximum_fusion.3), calls=%async_computation | async-start | bytes 2097152 | tf_op jit(solution)/shard_map/all_to_all | solution.py:691
  429.9 63.6 %all-to-all-start.1 = ((bf16[32,320,128]{2,1,0:T(8,128)(2,1)}), bf16[32,320,128]{2,1,0:T(8,128)(2,1)S(1)}, u32[]{:S(2)}, u32[]{:S(2)}) async-start(bf16[32,320,128]{2,1,0:T(8,128)(2,1)} %pad_maximum_fusion.1), calls=%async_computation.1 | async-start | bytes 5242880 | tf_op jit(solution)/shard_map/all_to_all | solution.py:691
  (1 other events, 0.6 us)
Sparse Core Ops, SparseCore 0:
  14.8 98.4 all-gather.2
  115.5 108.9 all-gather.4

commit v3 on v2

--- a/solution.py
+++ b/solution.py
@@ -398,7 +398,7 @@
 
 def mlp_kernel(
     mixed, tok, dy, sel, w_out, w_up, w_lo, w_dn, w_x, b_out, b_up, b_down, gain, shift, heads,
-    out_o, dres_o, dmix_o, head_o, tail_o, dlt_o, gui_o, gdo_o, guo_o, gdi_o,
+    out_o, dres_o, dmix_o, head_o, tail_o, dlt_o, grads_o,
     resid, n2, low_u, dlow_d, low_ut, dlow_dt, acc, acc_low, dn2, dlow_u, gdo_t, gui_t,
 ):
     j = pl.program_id(0)
@@ -454,8 +454,13 @@
         dlow_u[r, :] += dot_nn(d_pre, up_out)
         guo_t += dot_nn(low_ut[:, r], d_pre)
         gdi_t += dot_nn(dlow_dt[:, r], act)
-    guo_o[...] = guo_t.T.astype(bf16)
-    gdi_o[...] = gdi_t.T.astype(bf16)
+    owners, packed = grads_o.shape[:2]
+    narrow = width // owners
+    deep = packed // 2 - narrow
+    group = FF_TILE // deep
+    own_j = pl.ds(j * group, group)
+    grads_o[own_j, 2 * narrow : 2 * narrow + deep, :] = guo_t.T.reshape(group, deep, LANES)
+    grads_o[own_j, 2 * narrow + deep :, :] = gdi_t.T.reshape(group, deep, LANES)
 
     @pl.when(j == pl.num_programs(0) - 1)
     def _():
@@ -480,25 +485,25 @@
             prod = dmix.astype(f32) * mixed[r, :].astype(f32)
             high = prod.astype(bf16)
             rest = (prod - high.astype(f32)).astype(bf16)
-            dlt_o[:, r] = dot_nt(heads[...], high) + dot_nt(heads[...], rest)
+            delta = dot_nt(heads[...], high) + dot_nt(heads[...], rest)
+            for part in range(TILE // LANES):
+                dlt_o[:, at // LANES + part, :] = delta[:, part * LANES : (part + 1) * LANES]
             gdo_t[...] += dot_nn(low_d.astype(f32).T.astype(bf16), dy[r, :])
             gui_t[...] += dot_nn(lu.astype(f32).T.astype(bf16), n2[r, :])
-        gdo_o[...] = gdo_t[...].T.astype(bf16)
-        gui_o[...] = gui_t[...].T.astype(bf16)
-
-
-def mlp_call(mixed, tok, dy, sel, w_a, w_b, w_c, b_out, b_up, b_down, gain, shift, heads):
+        grads_o[:, :narrow, :] = gui_t[...].T.reshape(owners, narrow, LANES)
+        grads_o[:, narrow : 2 * narrow, :] = gdo_t[...].T.reshape(owners, narrow, LANES)
+
+
+def mlp_call(mixed, tok, dy, sel, w_a, w_b, w_c, b_out, b_up, b_down, gain, shift, heads, owners):
     rows, width = mixed.shape
     hidden = b_up.shape[1]
     full = whole((rows, width))
     vec = whole((1, width))
     low = whole((rows, LANES))
     at_low = (3 * width + 4 * LANES) // (2 * LANES)
-    grads = jax.ShapeDtypeStruct((width, LANES), bf16)
-    grads_ff = jax.ShapeDtypeStruct((hidden, LANES), bf16)
+    packed = (owners, 2 * (width + hidden) // owners, LANES)
     const = lambda shape: pl.BlockSpec(shape, lambda j: (0,) * len(shape))
     once = pl.Buffered(1)
-    ff_rows = pl.BlockSpec((FF_TILE, LANES), lambda j: (j, 0))
     if w_c is None:
         devices = w_b.shape[0]
         r, r_ff = width // devices, hidden // devices
@@ -548,11 +553,8 @@
             const((rows, width)),
             const((HALO, width)),
             const((HALO, width)),
-            const((HEADS, rows)),
-            const((width, LANES)),
-            const((width, LANES)),
-            ff_rows,
-            ff_rows,
+            const((HEADS, rows // LANES, LANES)),
+            const(packed),
         ],
         out_shape=[
             jax.ShapeDtypeStruct((rows, width), bf16),
@@ -560,11 +562,8 @@
             jax.ShapeDtypeStruct((rows, width), bf16),
             jax.ShapeDtypeStruct((HALO, width), bf16),
             jax.ShapeDtypeStruct((HALO, width), bf16),
-            jax.ShapeDtypeStruct((HEADS, rows), f32),
-            grads,
-            grads,
-            grads_ff,
-            grads_ff,
+            jax.ShapeDtypeStruct((HEADS, rows // LANES, LANES), f32),
+            jax.ShapeDtypeStruct(packed, f32),
         ],
         scratch_shapes=[
             pltpu.VMEM((rows, width), f32),
@@ -708,19 +707,24 @@
 
     before = lax.ppermute(tokens[own - HALO :], AXES, up)
     after = lax.ppermute(tokens[:HALO], AXES, down)
-    w_a = gather(w_query, w_key, w_value, query_in, value_in, query_out, value_out, up_in, down_out)
+    first_maps = (w_query, w_key, w_value, query_in, value_in, query_out, value_out, up_in, down_out)
     r, r_ff = w_out.shape[0], w_down.shape[0]
     if inner == 2 and r % 16 == 0 and 2 * LANES * (r_ff // r) == width:
         chunks = [slice(c, c + r) for c in range(0, r_ff, r)]
         low_maps = jnp.concatenate([m[c] for m in (up_out, down_in) for c in chunks], axis=1)
         up_blocks = [w_up[:, c : c + width] for c in range(0, w_up.shape[1], width)]
-        mine = jnp.concatenate([w_down, w_out, *up_blocks, low_maps], axis=0)
-        theirs = lax.ppermute(mine, "dp", [(0, 1), (1, 0)])
         is_first = lax.axis_index("dp") == 0
-        both = jnp.stack([jnp.where(is_first, mine, theirs), jnp.where(is_first, theirs, mine)])
-        w_b = lax.all_gather(both, "fsdp", axis=0, tiled=True)
+
+        def gather_twice(mine):
+            theirs = lax.ppermute(mine, "dp", [(0, 1), (1, 0)])
+            both = jnp.stack([jnp.where(is_first, mine, theirs), jnp.where(is_first, theirs, mine)])
+            return lax.all_gather(both, "fsdp", axis=0, tiled=True)
+
+        w_a = gather_twice(jnp.concatenate(first_maps, axis=1)).reshape(r * devices, -1)
+        w_b = gather_twice(jnp.concatenate([w_down, w_out, *up_blocks, low_maps], axis=0))
         w_c = None
     else:
+        w_a = gather(*first_maps)
         w_b = gather(w_out, w_up)
         w_c = gather(w_down, up_out, down_in)
 
@@ -779,9 +783,9 @@
         tab, tok_w, sel_w, w_a, row(b_query), row(b_value), row(ln1_gain), row(ln1_bias)
     )
     mixed, lse = attend_call(tab, q, k, v, segc, segr, own)
-    block_out, d_resid, d_mixed, dm_head, dm_tail, delta, g_ui, g_do, g_uo, g_di = mlp_call(
+    block_out, d_resid, d_mixed, dm_head, dm_tail, delta, g_ff = mlp_call(
         mixed, tokens, cotangent, sel, w_a, w_b, w_c, row(b_out), row(b_up), row(b_down),
-        row(ln2_gain), row(ln2_bias), heads,
+        row(ln2_gain), row(ln2_bias), heads, devices // inner,
     )
     dlt = delta.reshape(lse.shape)
     stats = jnp.stack([lse, dlt])
@@ -790,11 +794,21 @@
     dm_r = lax.ppermute(dm_head, AXES, down)
     st_l = lax.ppermute(stats[:, :, :, cut:], AXES, up)
     st_r = lax.ppermute(stats[:, :, :, : HALO // LANES], AXES, down)
-    mlp_grads = summed([g_ui, g_uo, g_di, g_do], devices)
+    g_ff = lax.psum_scatter(g_ff, "fsdp", scatter_dimension=0, tiled=False)
     dq, dk, dv = attend_back_call(tab, q, k, v, d_mixed, lse, dlt, segc, segr)
     dk, dv = halo_back_call(tab, q, k, v, dm_l, dm_r, st_l, st_r, dk, dv, segc, segr)
     dlow, g_qv = low_back_call(dq, dv, tokens, sel, w_a, row(ln1_gain), row(ln1_bias))
     qv_grads = summed([g_qv[0], g_qv[1], g_qv[2], g_qv[3]], devices)
+    narrow, deep = width // (devices // inner), b_up.shape[0] // (devices // inner)
+    cuts = (0, narrow, 2 * narrow, 2 * narrow + deep, 2 * (narrow + deep))
+    pieces = [g_ff[lo:hi].reshape(inner, -1, LANES) for lo, hi in zip(cuts[:-1], cuts[1:])]
+    g_ff = jnp.concatenate(pieces, axis=1)
+    if inner == 2:
+        is_low = lax.axis_index("dp") == 0
+        got = lax.ppermute(jnp.where(is_low, g_ff[1], g_ff[0]), "dp", [(0, 1), (1, 0)])
+        mlp_grads = jnp.where(is_low, g_ff[0], g_ff[1]) + got
+    else:
+        mlp_grads = lax.psum_scatter(g_ff, "dp", scatter_dimension=0, tiled=False)
     grad_input = qkv_back_call(
         dq, dk, dv, dlow, tokens, d_resid, w_a, row(ln1_gain), row(ln1_bias)
     )
@@ -806,9 +820,9 @@
         qv_grads[2 * r : 3 * r],
         qv_grads[3 * r :],
         mlp_grads[:r],
-        mlp_grads[r : r + r_ff],
-        mlp_grads[r + r_ff : r + 2 * r_ff],
-        mlp_grads[r + 2 * r_ff :],
+        mlp_grads[2 * r : 2 * r + r_ff],
+        mlp_grads[2 * r + r_ff :],
+        mlp_grads[r : 2 * r],
     )
 
 

time: 504 us -> 438 us (0.87)
  waiting for transfers between devices: 171 us -> 116 us
  local copies, waits for them, and re-layouts: 30.8 us -> 18.8 us
    all_to_all x2 -> x1, waiting for transfers between devices: 70.5 us -> 14.2 us  [summed(): got = lax.all_to_all(packed, AXES, 0, 0, tiled=True)]
    ppermute x1, waiting for transfers between devices: 37.5 us -> 23.6 us  [local(): before = lax.ppermute(tokens[own - HALO:], AXES, up)]
    unnamed x49 -> x51, local copies, waits for them, and re-layouts: 19.1 us -> 8.43 us
    all_gather x2, waiting for transfers between devices: 45.2 us -> 53.8 us  [gather_twice(): return lax.all_gather(both, 'fsdp', axis=0, tiled=True)]
    ppermute x1 -> x3, waiting for transfers between devices: 16.2 us -> 24.2 us  [the longest x2 20.1 us: gather_twice(): theirs = lax.ppermute(mine, 'dp', [(0, 1), (1, 0)])]
    all_to_all x2 -> x1, starting transfers between devices: 27.7 us -> 23.9 us  [summed(): got = lax.all_to_all(packed, AXES, 0, 0, tiled=True)]
  transfers between devices with their start and end apart: 11 -> 13, of which waited for: 7 -> 8; matrix products, arithmetic and copies ran while one was open for 6% -> 3% of each run, Pallas kernels for 26% -> 36%
where the time goes in v3:
time: 438 us; the launch traced here: 436 us
  Pallas kernels  217 us (50%)
  waiting for transfers between devices  116 us (26%)
  starting transfers between devices  47.5 us (11%)
  between operations  27.4 us (6%)
  local copies, waits for them, and re-layouts  18.8 us (4%)
  other arithmetic  8.66 us (2%)
    pallas_call x1, Pallas kernels, mlp_call(): pl.pallas_call(mlp_kernel, grid=(hidden // FF_TILE,), in_specs=[full, ful...  61.1 us
    pallas_call x1, Pallas kernels, attend_back_call(): pl.pallas_call(attend_back_kernel, grid_spec=pltpu.PrefetchScalarGridSpec...  55.6 us
    all_gather x2, waiting for transfers between devices, gather_twice(): return lax.all_gather(both, 'fsdp', axis=0, tiled=True)  53.8 us
    pallas_call x1, Pallas kernels, attend_call(): pl.pallas_call(attend_kernel, grid_spec=pltpu.PrefetchScalarGridSpec(num_...  43.4 us
    all_to_all x1, starting transfers between devices, summed(): got = lax.all_to_all(packed, AXES, 0, 0, tiled=True)  23.9 us
    ppermute x1, waiting for transfers between devices, local(): before = lax.ppermute(tokens[own - HALO:], AXES, up)  23.6 us
    pallas_call x1, Pallas kernels, qkv_call(): pl.pallas_call(qkv_kernel, grid_spec=pltpu.PrefetchScalarGridSpec(num_sca...  21.8 us
    ppermute x2, waiting for transfers between devices, gather_twice(): theirs = lax.ppermute(mine, 'dp', [(0, 1), (1, 0)])  20.1 us
  transfers between devices with their start and end apart: 13, of which 8 were waited for; matrix products, arithmetic and copies ran while one was open for 3% of the time, Pallas kernels for 36%

profile of v3, /device:TPU:0, one launch (start us, length us, event | category | flops | bytes accessed | tf_op | source)
XLA Modules:
  0.0 436.3 jit_solution(13211802583453916239)
XLA Ops:
  14.1 3.0 collective-permute-start.2
  17.1 6.0 %collective-permute-done.2 = bf16[32,3840]{1,0:T(8,128)(2,1)S(1)} collective-permute-done((bf16[32,3840]{1,0:T(8,128)(2,1)S(1)}, bf16[32,3840]{1,0:T(8,128)(2,1)S(1)}, u32[]{:S(2)}, u32[]{:S(2)}) %collective-permute-start.2) | collective-permute-done | bytes 245792 | tf_op jit(solution)/shard_map/ppermute | solution.py:719
  24.2 1.8 collective-permute-start.3
  26.0 14.2 %collective-permute-done.3 = bf16[320,1024]{1,0:T(8,128)(2,1)S(1)} collective-permute-done((bf16[320,1024]{1,0:T(8,128)(2,1)S(1)}, bf16[320,1024]{1,0:T(8,128)(2,1)S(1)}, u32[]{:S(2)}, u32[]{:S(2)}) %collective-permute-start.3) | collective-permute-done | bytes 655392 | tf_op jit(solution)/shard_map/ppermute | solution.py:719
  42.2 1.3 fusion.10
  43.5 4.4 %collective-permute-start = (bf16[640,1024]{1,0:T(8,128)(2,1)}, bf16[640,1024]{1,0:T(8,128)(2,1)}, u32[]{:S(2)}, u32[]{:S(2)}) collective-permute-start(bf16[640,1024]{1,0:T(8,128)(2,1)} %get-tuple-element.52), channel_id=1, source_target_pairs={{0,1},{1,2},{2,3},{3,4},{4,5},{5,6},{6,7},{7,8},{8,9},{9,10},{10,1... | collective-permute-start | bytes 3932168 | tf_op jit(solution)/shard_map/ppermute | solution.py:708
  66.8 23.6 %collective-permute-done = bf16[640,1024]{1,0:T(8,128)(2,1)} collective-permute-done((bf16[640,1024]{1,0:T(8,128)(2,1)}, bf16[640,1024]{1,0:T(8,128)(2,1)}, u32[]{:S(2)}, u32[]{:S(2)}) %collective-permute-start) | collective-permute-done | bytes 1310752 | tf_op jit(solution)/shard_map/ppermute | solution.py:708
  90.8 3.5 pad_maximum_fusion.tok
  94.3 9.7 %all-gather.3.cloned.1.call-done = bf16[32,32,3840]{2,1,0:T(8,128)(2,1)} async-done(((bf16[2,32,3840]{2,1,0:T(8,128)(2,1)}), bf16[32,32,3840]{2,1,0:T(8,128)(2,1)}) %all-gather.3.cloned.1.call-update) | async-done | bytes 7864336 | tf_op jit(solution)/shard_map/all_gather | solution.py:721
  104.0 21.8 %qkv.1 = (bf16[2048,1024]{1,0:T(8,128)(2,1)}, bf16[2048,1024]{1,0:T(8,128)(2,1)}, bf16[2048,1024]{1,0:T(8,128)(2,1)}) custom-call(s32[14]{0:T(128)} %stack.79.tab, bf16[2048,1024]{1,0:T(8,128)(2,1)} %pad_maximum_fusion.tok, bf16[2048,128]{1,0:T(8,128)(2,1)} %copy-done.1, bf16[1024,3840]{1,0:T(8,128)(2,1)} %bitcast.57, f32[1,1024]{1,0:T(1,128)} %bitcast.79, ...), custom_call_target="tpu_custom_call" | custom-call | tf_op jit(solution)/shard_map/qkv/pallas_call | solution.py:107
  127.0 43.4 %attend.1 = (bf16[768,1024]{1,0:T(8,128)(2,1)}, f32[8,2,6,128]{3,2,1,0:T(8,128)}) custom-call(s32[14]{0:T(128)} %stack.79.tab, bf16[2048,1024]{1,0:T(8,128)(2,1)} %get-tuple-element.29.q, bf16[2048,1024]{1,0:T(8,128)(2,1)} %get-tuple-element.30.k, bf16[2048,1024]{1,0:T(8,128)(2,1)} %get-tuple-element.31.v, s32[2048,128]{1,0:T(8,128)} %broadcast_in_dim.8.segc, ...), custom_call_target="tpu_custom_call" | custom-call | tf_op jit(solution)/shard_map/attend/pallas_call | solution.py:203
  170.4 44.1 %all-gather.5.cloned.1.call-done.w_out.w_up.w_dn.w_x = bf16[32,320,1024]{2,1,0:T(8,128)(2,1)} async-done(((bf16[2,320,1024]{2,1,0:T(8,128)(2,1)}), bf16[32,320,1024]{2,1,0:T(8,128)(2,1)}) %all-gather.5.cloned.1.call-update) | async-done | bytes 20971536 | tf_op jit(solution)/shard_map/all_gather | solution.py:721
  214.5 61.1 %mlp.1 = (bf16[768,1024]{1,0:T(8,128)(2,1)}, f32[768,1024]{1,0:T(8,128)}, bf16[768,1024]{1,0:T(8,128)(2,1)}, bf16[640,1024]{1,0:T(8,128)(2,1)}, bf16[640,1024]{1...) custom-call(bf16[768,1024]{1,0:T(8,128)(2,1)} %get-tuple-element.32.mixed, bf16[768,1024]{1,0:T(8,128)(2,1)} %tok.5, ...), custom_call_target="tpu_custom_call" | custom-call | tf_op jit(solution)/shard_map/mlp/pallas_call | solution.py:530
  275.7 3.6 collective-permute-start.4
  279.3 1.3 collective-permute-start.5
  282.0 5.2 %collective-permute-start.6 = (f32[2,8,2,5,128]{4,3,2,1,0:T(8,128)S(1)}, f32[2,8,2,5,128]{4,3,2,1,0:T(8,128)S(1)}, u32[]{:S(2)}, u32[]{:S(2)}) collective-permute-start(f32[2,8,2,5,128]{4,3,2,1,0:T(8,128)S(1)} %get-tuple-element.71), channel_id=1, source_target_pairs={{0,1},{1,2},{2,3},{3,4},{4,5},{5,6},{6,7},{7,8},{8,9},{9,10},{10,1... | collective-permute-start | bytes 245768 | tf_op jit(solution)/shard_map/ppermute | solution.py:795
  287.2 55.6 %attend_back.1 = (bf16[768,1024]{1,0:T(8,128)(2,1)}, f32[768,1024]{1,0:T(8,128)}, f32[768,1024]{1,0:T(8,128)}) custom-call(s32[14]{0:T(128)} %stack.79.tab, bf16[2048,1024]{1,0:T(8,128)(2,1)} %get-tuple-element.29.q, bf16[2048,1024]{1,0:T(8,128)(2,1)} %get-tuple-element.30.k, bf16[2048,1024]{1,0:T(8,128)(2,1)} %get-tuple-element.31.v, ...), custom_call_target="tpu_custom_call" | custom-call | tf_op jit(solution)/shard_map/attend_back/pallas_call | solution.py:297
  344.3 15.8 %halo_back.1 = (bf16[768,1024]{1,0:T(8,128)(2,1)}, bf16[768,1024]{1,0:T(8,128)(2,1)}) custom-call(s32[14]{0:T(128)} %stack.79.tab, bf16[2048,1024]{1,0:T(8,128)(2,1)} %get-tuple-element.29.q, bf16[2048,1024]{1,0:T(8,128)(2,1)} %get-tuple-element.30.k, bf16[2048,1024]{1,0:T(8,128)(2,1)} %get-tuple-element.31.v, bf16[640,1024]{1,0:T(8,128)(2,1)} %copy-done.2, ...), custom_call_target="tpu_custom_call" | custom-call | tf_op jit(solution)/shard_map/halo_back/pallas_call | solution.py:369
  360.1 7.5 %low_back.1 = (bf16[768,256]{1,0:T(8,128)(2,1)}, bf16[4,1024,128]{2,1,0:T(8,128)(2,1)}) custom-call(bf16[768,1024]{1,0:T(8,128)(2,1)} %get-tuple-element.37.dq, bf16[768,1024]{1,0:T(8,128)(2,1)} %get-tuple-element.43.dv, bf16[768,1024]{1,0:T(8,128)(2,1)} %tok.5, bf16[768,128]{1,0:T(8,128)(2,1)} %slice.197.sel, bf16[1024,3840]{1,0:T(8,128)(2,1)} %bitcast.59, ...), custom_call_target="tpu_custom_call" | custom-call | tf_op jit(solution)/shard_map/low_back/pallas_call | solution.py:625
  370.0 23.9 %all-to-all-start = ((bf16[32,128,128]{2,1,0:T(8,128)(2,1)}), bf16[32,128,128]{2,1,0:T(8,128)(2,1)S(1)}, u32[]{:S(2)}, u32[]{:S(2)}) async-start(bf16[32,128,128]{2,1,0:T(8,128)(2,1)} %pad_maximum_fusion.2), calls=%async_computation | async-start | bytes 2097152 | tf_op jit(solution)/shard_map/all_to_all | solution.py:690
  394.0 12.0 %qkv_back.1 = bf16[768,1024]{1,0:T(8,128)(2,1)} custom-call(bf16[768,1024]{1,0:T(8,128)(2,1)} %get-tuple-element.37.dq, bf16[768,1024]{1,0:T(8,128)(2,1)} %get-tuple-element.42.dk, bf16[768,1024]{1,0:T(8,128)(2,1)} %get-tuple-element.43.dv, bf16[768,256]{1,0:T(8,128)(2,1)} %get-tuple-element.44.dlow, bf16[768,1024]{1,0:T(8,128)(2,1)} %tok.5, ...), custom_call_target="tpu_custom_call" | custom-call | tf_op jit(solution)/shard_map/qkv_back/pallas_call | solution.py:667
  406.0 14.2 %all-to-all-done = bf16[32,128,128]{2,1,0:T(8,128)(2,1)S(1)} async-done(((bf16[32,128,128]{2,1,0:T(8,128)(2,1)}), bf16[32,128,128]{2,1,0:T(8,128)(2,1)S(1)}, u32[]{:S(2)}, u32[]{:S(2)}) %all-to-all-start) | async-done | bytes 1048608 | tf_op jit(solution)/shard_map/all_to_all | solution.py:690
  422.2 1.6 collective-permute-start.8
  424.4 4.1 collective-permute-done.8
  (100 shorter events, 26.4 us)
Async XLA Ops:
  7.2 16.8 %copy-start.7 = (bf16[128,1024]{1,0:T(8,128)(2,1)S(1)}, bf16[128,1024]{1,0:T(8,128)(2,1)}, u32[]{:S(2)}) copy-start(bf16[128,1024]{1,0:T(8,128)(2,1)} %param.44) | copy-start | bytes 786436
  7.2 16.8 %copy-start.11 = (bf16[32,1024]{1,0:T(8,128)(2,1)S(1)}, bf16[32,1024]{1,0:T(8,128)(2,1)}, u32[]{:S(2)}) copy-start(bf16[32,1024]{1,0:T(8,128)(2,1)} %param.38) | copy-start | bytes 196612
  7.2 16.8 %copy-start.8 = (bf16[32,4096]{1,0:T(8,128)(2,1)S(1)}, bf16[32,4096]{1,0:T(8,128)(2,1)}, u32[]{:S(2)}) copy-start(bf16[32,4096]{1,0:T(8,128)(2,1)} %param.42) | copy-start | bytes 786436
  7.2 16.9 %copy-start.12 = (bf16[128,128]{1,0:T(8,128)(2,1)S(1)}, bf16[128,128]{1,0:T(8,128)(2,1)}, u32[]{:S(2)}) copy-start(bf16[128,128]{1,0:T(8,128)(2,1)} %param.51) | copy-start | bytes 98308
  7.2 17.0 %copy-start.13 = (bf16[128,128]{1,0:T(8,128)(2,1)S(1)}, bf16[128,128]{1,0:T(8,128)(2,1)}, u32[]{:S(2)}) copy-start(bf16[128,128]{1,0:T(8,128)(2,1)} %param.52) | copy-start | bytes 98308
  7.2 96.8 %all-gather.3.cloned.1.call-start = ((), (), s32[]{:S(2)}) async-start(), calls=%async_computation.2 | async-start | bytes 8355840 | tf_op jit(solution)/shard_map/all_gather | solution.py:721
  14.1 8.9 %collective-permute-start.2 = (bf16[32,3840]{1,0:T(8,128)(2,1)S(1)}, bf16[32,3840]{1,0:T(8,128)(2,1)S(1)}, u32[]{:S(2)}, u32[]{:S(2)}) collective-permute-start(bf16[32,3840]{1,0:T(8,128)(2,1)S(1)} %constant_dynamic-update-slice_fusion), channel_id=1, source_target_pairs={{0,1},{1,0},{2,3},{3,2},{4,5},{5,4},{6,7},{7,6},{8,9},{9,8},{10,11... | collective-permute-start | bytes 737288 | tf_op jit(solution)/shard_map/ppermute | solution.py:719
  23.9 190.6 %all-gather.5.cloned.1.call-start = ((), (), s32[]{:S(2)}) async-start(), calls=%async_computation.3 | async-start | bytes 22282240 | tf_op jit(solution)/shard_map/all_gather | solution.py:721
  24.2 16.0 %collective-permute-start.3 = (bf16[320,1024]{1,0:T(8,128)(2,1)S(1)}, bf16[320,1024]{1,0:T(8,128)(2,1)S(1)}, u32[]{:S(2)}, u32[]{:S(2)}) collective-permute-start(bf16[320,1024]{1,0:T(8,128)(2,1)S(1)} %constant_dynamic-update-slice_fusion.12), channel_id=1, source_target_pairs={{0,1},{1,0},{2,3},{3,2},{4,5},{5,4},{6,7},{7,6},{8,9},{9,8},{10,11... | collective-permute-start | bytes 1966088 | tf_op jit(solution)/shard_map/ppermute | solution.py:719
  40.3 1.9 copy-start
  41.5 7.7 %copy-start.4 = (s32[24576]{0:T(1024)S(1)}, s32[24576]{0:T(1024)}, u32[]{:S(2)}) copy-start(s32[24576]{0:T(1024)} %param.29) | copy-start | bytes 294916
  41.5 22.1 %copy-start.14 = (s32[48]{0:T(128)S(1)}, s32[48]{0:T(128)}, u32[]{:S(2)}) copy-start(s32[48]{0:T(128)} %param.30) | copy-start | bytes 580
  41.5 378.8 %reduce-scatter.2.cloned.1.call-start = ((), (), s32[]{:S(2)}) async-start(), calls=%async_computation.4 | async-start | bytes 5570560 | tf_op jit(solution)/shard_map/reduce_scatter | solution.py:797
  43.5 46.9 %collective-permute-start = (bf16[640,1024]{1,0:T(8,128)(2,1)}, bf16[640,1024]{1,0:T(8,128)(2,1)}, u32[]{:S(2)}, u32[]{:S(2)}) collective-permute-start(bf16[640,1024]{1,0:T(8,128)(2,1)} %get-tuple-element.52), channel_id=1, source_target_pairs={{0,1},{1,2},{2,3},{3,4},{4,5},{5,6},{6,7},{7,8},{8,9},{9,10},{10,1... | collective-permute-start | bytes 3932168 | tf_op jit(solution)/shard_map/ppermute | solution.py:708
  47.9 42.9 %collective-permute-start.1 = (bf16[640,1024]{1,0:T(8,128)(2,1)S(1)}, bf16[640,1024]{1,0:T(8,128)(2,1)}, u32[]{:S(2)}, u32[]{:S(2)}) collective-permute-start(bf16[640,1024]{1,0:T(8,128)(2,1)S(1)} %get-tuple-element.53), channel_id=1, source_target_pairs={{1,0},{2,1},{3,2},{4,3},{5,4},{6,5},{7,6},{8,7},{9,8},{10,9},{11,1... | collective-permute-start | bytes 3932168 | tf_op jit(solution)/shard_map/ppermute | solution.py:709
  64.1 30.2 %copy-start.1 = (bf16[2048,128]{1,0:T(8,128)(2,1)}, bf16[2048,128]{1,0:T(8,128)(2,1)S(1)}, u32[]{:S(2)}) copy-start(bf16[2048,128]{1,0:T(8,128)(2,1)S(1)} %convolution_convert_fusion.sel) | copy-start | bytes 1572868
  275.7 5.0 %copy-start.5 = (f32[8,2,6,128]{3,2,1,0:T(8,128)S(1)}, f32[8,2,6,128]{3,2,1,0:T(8,128)}, u32[]{:S(2)}) copy-start(f32[8,2,6,128]{3,2,1,0:T(8,128)} %get-tuple-element.35.lse) | copy-start | bytes 147460
  275.7 5.0 %copy-start.6 = (f32[16,6,128]{2,1,0:T(8,128)S(1)}, f32[16,6,128]{2,1,0:T(8,128)}, u32[]{:S(2)}) copy-start(f32[16,6,128]{2,1,0:T(8,128)} %get-tuple-element.36) | copy-start | bytes 147460
  275.7 67.1 %collective-permute-start.4 = (bf16[640,1024]{1,0:T(8,128)(2,1)}, bf16[640,1024]{1,0:T(8,128)(2,1)S(1)}, u32[]{:S(2)}, u32[]{:S(2)}) collective-permute-start(bf16[640,1024]{1,0:T(8,128)(2,1)} %get-tuple-element.38), channel_id=1, source_target_pairs={{0,1},{1,2},{2,3},{3,4},{4,5},{5,6},{6,7},{7,8},{8,9},{9,10},{10,1... | collective-permute-start | bytes 3932168 | tf_op jit(solution)/shard_map/ppermute | solution.py:793
  279.3 63.5 %collective-permute-start.5 = (bf16[640,1024]{1,0:T(8,128)(2,1)}, bf16[640,1024]{1,0:T(8,128)(2,1)S(1)}, u32[]{:S(2)}, u32[]{:S(2)}) collective-permute-start(bf16[640,1024]{1,0:T(8,128)(2,1)} %get-tuple-element.39), channel_id=1, source_target_pairs={{1,0},{2,1},{3,2},{4,3},{5,4},{6,5},{7,6},{8,7},{9,8},{10,9},{11,1... | collective-permute-start | bytes 3932168 | tf_op jit(solution)/shard_map/ppermute | solution.py:794
  280.7 62.1 %collective-permute-start.7 = (f32[2,8,2,5,128]{4,3,2,1,0:T(8,128)S(1)}, f32[2,8,2,5,128]{4,3,2,1,0:T(8,128)S(1)}, u32[]{:S(2)}, u32[]{:S(2)}) collective-permute-start(f32[2,8,2,5,128]{4,3,2,1,0:T(8,128)S(1)} %get-tuple-element.70), channel_id=1, source_target_pairs={{1,0},{2,1},{3,2},{4,3},{5,4},{6,5},{7,6},{8,7},{9,8},{10,9},{11,1... | collective-permute-start | bytes 245768 | tf_op jit(solution)/shard_map/ppermute | solution.py:796
  282.0 60.8 %collective-permute-start.6 = (f32[2,8,2,5,128]{4,3,2,1,0:T(8,128)S(1)}, f32[2,8,2,5,128]{4,3,2,1,0:T(8,128)S(1)}, u32[]{:S(2)}, u32[]{:S(2)}) collective-permute-start(f32[2,8,2,5,128]{4,3,2,1,0:T(8,128)S(1)} %get-tuple-element.71), channel_id=1, source_target_pairs={{0,1},{1,2},{2,3},{3,4},{4,5},{5,6},{6,7},{7,8},{8,9},{9,10},{10,1... | collective-permute-start | bytes 245768 | tf_op jit(solution)/shard_map/ppermute | solution.py:795
  370.0 50.2 %all-to-all-start = ((bf16[32,128,128]{2,1,0:T(8,128)(2,1)}), bf16[32,128,128]{2,1,0:T(8,128)(2,1)S(1)}, u32[]{:S(2)}, u32[]{:S(2)}) async-start(bf16[32,128,128]{2,1,0:T(8,128)(2,1)} %pad_maximum_fusion.2), calls=%async_computation | async-start | bytes 2097152 | tf_op jit(solution)/shard_map/all_to_all | solution.py:690
  422.2 6.3 %collective-permute-start.8 = (f32[320,128]{1,0:T(8,128)S(1)}, f32[320,128]{1,0:T(8,128)S(1)}, u32[]{:S(2)}, u32[]{:S(2)}) collective-permute-start(f32[320,128]{1,0:T(8,128)S(1)} %select_bitcast_fusion.4), channel_id=1, source_target_pairs={{0,1},{1,0},{2,3},{3,2},{4,5},{5,4},{6,7},{7,6},{8,9},{9,8},{10,11... | collective-permute-start | bytes 491528 | tf_op jit(solution)/shard_map/ppermute | solution.py:808
  (4 other events, 4.0 us)
Sparse Core Ops, SparseCore 0:
  24.1 79.8 all-gather.2
  106.2 108.3 all-gather.4
  275.8 78.3 reduce-scatter.1

commit v4 on v3

--- a/solution.py
+++ b/solution.py
@@ -263,8 +263,8 @@
         at_q = HALO // LANES + 2 * i
         sq = jnp.concatenate([segr[pl.ds(at_q, 1), :], segr[pl.ds(at_q + 1, 1), :]], axis=1)
 
-        def step(t, carry):
-            at = pl.ds(pl.multiple_of((start + 2 * t) * LANES, LANES), TILE)
+        def step(t, carry, size=TILE):
+            at = pl.ds(pl.multiple_of((start + 2 * t) * LANES, LANES), size)
             mask = twice(segc[at, :]) == sq
             out = []
             for c in range(wide):
@@ -277,7 +277,10 @@
             return tuple(out)
 
         empty = jnp.zeros((TILE, LANES), f32)
-        sums = lax.fori_loop(0, count, step, (empty,) * (2 * wide))
+        sums = lax.fori_loop(
+            0, count // 2, lambda t, c: step(2 * t, c, 2 * TILE), (empty,) * (2 * wide)
+        )
+        sums = lax.fori_loop(count // 2 * 2, count, step, sums)
         for c in range(wide):
             dq_o[here, columns(c)] = (
                 jnp.where(first, sums[2 * c], sums[2 * c + 1]) * scale
@@ -339,9 +342,9 @@
             ]
             sq = segr[pl.ds(tile_w, 1), :]
 
-            def key_tile(u, inner):
-                at = pl.ds(pl.multiple_of((k_first + u) * TILE, TILE), TILE)
-                at_k = pl.ds(pl.multiple_of(HALO + (k_first + u) * TILE, LANES), TILE)
+            def key_tile(u, inner, size=TILE):
+                at = pl.ds(pl.multiple_of((k_first + u) * TILE, TILE), size)
+                at_k = pl.ds(pl.multiple_of(HALO + (k_first + u) * TILE, LANES), size)
                 mask = segc[at_k, :] == sq
                 for c in range(wide):
                     kt = k[at_k, columns(c)]
@@ -351,7 +354,10 @@
                     dk_a[at, columns(c)] += dot_nn(jnp.concatenate([d0, d1], axis=1), qs[c])
                 return inner
 
-            return lax.fori_loop(0, count_k, key_tile, carry)
+            carry = lax.fori_loop(
+                0, count_k // 2, lambda u, c: key_tile(2 * u, c, 2 * TILE), carry
+            )
+            return lax.fori_loop(count_k // 2 * 2, count_k, key_tile, carry)
 
         lax.fori_loop(0, count_q, query_tile, 0)
     dk_o[...] = dk_a[...].astype(bf16)

time: 438 us -> 431 us (0.984)
  transfers between devices with their start and end apart: 13 -> 13, of which waited for: 8 -> 8; matrix products, arithmetic and copies ran while one was open for 3% -> 3% of each run, Pallas kernels for 36% -> 35%
where the time goes in v4:
time: 431 us; the launch traced here: 430 us
  Pallas kernels  213 us (49%)
  waiting for transfers between devices  116 us (27%)
  starting transfers between devices  45.6 us (11%)
  between operations  27.4 us (6%)
  local copies, waits for them, and re-layouts  18.8 us (4%)
  other arithmetic  8.66 us (2%)
    pallas_call x1, Pallas kernels, mlp_call(): pl.pallas_call(mlp_kernel, grid=(hidden // FF_TILE,), in_specs=[full, ful...  61.1 us
    all_gather x2, waiting for transfers between devices, gather_twice(): return lax.all_gather(both, 'fsdp', axis=0, tiled=True)  53.8 us
    pallas_call x1, Pallas kernels, attend_back_call(): pl.pallas_call(attend_back_kernel, grid_spec=pltpu.PrefetchScalarGridSpec...  51.2 us
    pallas_call x1, Pallas kernels, attend_call(): pl.pallas_call(attend_kernel, grid_spec=pltpu.PrefetchScalarGridSpec(num_...  43.4 us
    ppermute x1, waiting for transfers between devices, local(): before = lax.ppermute(tokens[own - HALO:], AXES, up)  23.6 us
    all_to_all x1, starting transfers between devices, summed(): got = lax.all_to_all(packed, AXES, 0, 0, tiled=True)  22.1 us
    pallas_call x1, Pallas kernels, qkv_call(): pl.pallas_call(qkv_kernel, grid_spec=pltpu.PrefetchScalarGridSpec(num_sca...  21.8 us
    ppermute x2, waiting for transfers between devices, gather_twice(): theirs = lax.ppermute(mine, 'dp', [(0, 1), (1, 0)])  20.1 us
  transfers between devices with their start and end apart: 13, of which 8 were waited for; matrix products, arithmetic and copies ran while one was open for 3% of the time, Pallas kernels for 35%

profile of v4, /device:TPU:0, one launch (start us, length us, event | category | flops | bytes accessed | tf_op | source)
XLA Modules:
  0.0 430.1 jit_solution(15286219811057876552)
XLA Ops:
  14.1 3.0 collective-permute-start.2
  17.1 6.0 %collective-permute-done.2 = bf16[32,3840]{1,0:T(8,128)(2,1)S(1)} collective-permute-done((bf16[32,3840]{1,0:T(8,128)(2,1)S(1)}, bf16[32,3840]{1,0:T(8,128)(2,1)S(1)}, u32[]{:S(2)}, u32[]{:S(2)}) %collective-permute-start.2) | collective-permute-done | bytes 245792 | tf_op jit(solution)/shard_map/ppermute | solution.py:725
  24.2 1.8 collective-permute-start.3
  26.0 14.2 %collective-permute-done.3 = bf16[320,1024]{1,0:T(8,128)(2,1)S(1)} collective-permute-done((bf16[320,1024]{1,0:T(8,128)(2,1)S(1)}, bf16[320,1024]{1,0:T(8,128)(2,1)S(1)}, u32[]{:S(2)}, u32[]{:S(2)}) %collective-permute-start.3) | collective-permute-done | bytes 655392 | tf_op jit(solution)/shard_map/ppermute | solution.py:725
  42.2 1.3 fusion.10
  43.5 4.4 %collective-permute-start = (bf16[640,1024]{1,0:T(8,128)(2,1)}, bf16[640,1024]{1,0:T(8,128)(2,1)}, u32[]{:S(2)}, u32[]{:S(2)}) collective-permute-start(bf16[640,1024]{1,0:T(8,128)(2,1)} %get-tuple-element.52), channel_id=1, source_target_pairs={{0,1},{1,2},{2,3},{3,4},{4,5},{5,6},{6,7},{7,8},{8,9},{9,10},{10,1... | collective-permute-start | bytes 3932168 | tf_op jit(solution)/shard_map/ppermute | solution.py:714
  66.8 23.6 %collective-permute-done = bf16[640,1024]{1,0:T(8,128)(2,1)} collective-permute-done((bf16[640,1024]{1,0:T(8,128)(2,1)}, bf16[640,1024]{1,0:T(8,128)(2,1)}, u32[]{:S(2)}, u32[]{:S(2)}) %collective-permute-start) | collective-permute-done | bytes 1310752 | tf_op jit(solution)/shard_map/ppermute | solution.py:714
  90.8 3.5 pad_maximum_fusion.tok
  94.3 9.7 %all-gather.3.cloned.1.call-done = bf16[32,32,3840]{2,1,0:T(8,128)(2,1)} async-done(((bf16[2,32,3840]{2,1,0:T(8,128)(2,1)}), bf16[32,32,3840]{2,1,0:T(8,128)(2,1)}) %all-gather.3.cloned.1.call-update) | async-done | bytes 7864336 | tf_op jit(solution)/shard_map/all_gather | solution.py:727
  104.0 21.8 %qkv.1 = (bf16[2048,1024]{1,0:T(8,128)(2,1)}, bf16[2048,1024]{1,0:T(8,128)(2,1)}, bf16[2048,1024]{1,0:T(8,128)(2,1)}) custom-call(s32[14]{0:T(128)} %stack.79.tab, bf16[2048,1024]{1,0:T(8,128)(2,1)} %pad_maximum_fusion.tok, bf16[2048,128]{1,0:T(8,128)(2,1)} %copy-done.1, bf16[1024,3840]{1,0:T(8,128)(2,1)} %bitcast.57, f32[1,1024]{1,0:T(1,128)} %bitcast.79, ...), custom_call_target="tpu_custom_call" | custom-call | tf_op jit(solution)/shard_map/qkv/pallas_call | solution.py:107
  127.0 43.4 %attend.1 = (bf16[768,1024]{1,0:T(8,128)(2,1)}, f32[8,2,6,128]{3,2,1,0:T(8,128)}) custom-call(s32[14]{0:T(128)} %stack.79.tab, bf16[2048,1024]{1,0:T(8,128)(2,1)} %get-tuple-element.29.q, bf16[2048,1024]{1,0:T(8,128)(2,1)} %get-tuple-element.30.k, bf16[2048,1024]{1,0:T(8,128)(2,1)} %get-tuple-element.31.v, s32[2048,128]{1,0:T(8,128)} %broadcast_in_dim.8.segc, ...), custom_call_target="tpu_custom_call" | custom-call | tf_op jit(solution)/shard_map/attend/pallas_call | solution.py:203
  170.4 44.1 %all-gather.5.cloned.1.call-done.w_out.w_up.w_dn.w_x = bf16[32,320,1024]{2,1,0:T(8,128)(2,1)} async-done(((bf16[2,320,1024]{2,1,0:T(8,128)(2,1)}), bf16[32,320,1024]{2,1,0:T(8,128)(2,1)}) %all-gather.5.cloned.1.call-update) | async-done | bytes 20971536 | tf_op jit(solution)/shard_map/all_gather | solution.py:727
  214.5 61.1 %mlp.1 = (bf16[768,1024]{1,0:T(8,128)(2,1)}, f32[768,1024]{1,0:T(8,128)}, bf16[768,1024]{1,0:T(8,128)(2,1)}, bf16[640,1024]{1,0:T(8,128)(2,1)}, bf16[640,1024]{1...) custom-call(bf16[768,1024]{1,0:T(8,128)(2,1)} %get-tuple-element.32.mixed, bf16[768,1024]{1,0:T(8,128)(2,1)} %tok.5, ...), custom_call_target="tpu_custom_call" | custom-call | tf_op jit(solution)/shard_map/mlp/pallas_call | solution.py:536
  275.7 3.6 collective-permute-start.4
  279.3 1.3 collective-permute-start.5
  282.0 5.2 %collective-permute-start.6 = (f32[2,8,2,5,128]{4,3,2,1,0:T(8,128)S(1)}, f32[2,8,2,5,128]{4,3,2,1,0:T(8,128)S(1)}, u32[]{:S(2)}, u32[]{:S(2)}) collective-permute-start(f32[2,8,2,5,128]{4,3,2,1,0:T(8,128)S(1)} %get-tuple-element.71), channel_id=1, source_target_pairs={{0,1},{1,2},{2,3},{3,4},{4,5},{5,6},{6,7},{7,8},{8,9},{9,10},{10,1... | collective-permute-start | bytes 245768 | tf_op jit(solution)/shard_map/ppermute | solution.py:801
  287.2 51.2 %attend_back.1 = (bf16[768,1024]{1,0:T(8,128)(2,1)}, f32[768,1024]{1,0:T(8,128)}, f32[768,1024]{1,0:T(8,128)}) custom-call(s32[14]{0:T(128)} %stack.79.tab, bf16[2048,1024]{1,0:T(8,128)(2,1)} %get-tuple-element.29.q, bf16[2048,1024]{1,0:T(8,128)(2,1)} %get-tuple-element.30.k, bf16[2048,1024]{1,0:T(8,128)(2,1)} %get-tuple-element.31.v, ...), custom_call_target="tpu_custom_call" | custom-call | tf_op jit(solution)/shard_map/attend_back/pallas_call | solution.py:300
  340.0 15.8 %halo_back.1 = (bf16[768,1024]{1,0:T(8,128)(2,1)}, bf16[768,1024]{1,0:T(8,128)(2,1)}) custom-call(s32[14]{0:T(128)} %stack.79.tab, bf16[2048,1024]{1,0:T(8,128)(2,1)} %get-tuple-element.29.q, bf16[2048,1024]{1,0:T(8,128)(2,1)} %get-tuple-element.30.k, bf16[2048,1024]{1,0:T(8,128)(2,1)} %get-tuple-element.31.v, bf16[640,1024]{1,0:T(8,128)(2,1)} %copy-done.2, ...), custom_call_target="tpu_custom_call" | custom-call | tf_op jit(solution)/shard_map/halo_back/pallas_call | solution.py:375
  355.8 7.5 %low_back.1 = (bf16[768,256]{1,0:T(8,128)(2,1)}, bf16[4,1024,128]{2,1,0:T(8,128)(2,1)}) custom-call(bf16[768,1024]{1,0:T(8,128)(2,1)} %get-tuple-element.37.dq, bf16[768,1024]{1,0:T(8,128)(2,1)} %get-tuple-element.43.dv, bf16[768,1024]{1,0:T(8,128)(2,1)} %tok.5, bf16[768,128]{1,0:T(8,128)(2,1)} %slice.197.sel, bf16[1024,3840]{1,0:T(8,128)(2,1)} %bitcast.59, ...), custom_call_target="tpu_custom_call" | custom-call | tf_op jit(solution)/shard_map/low_back/pallas_call | solution.py:631
  365.7 22.1 %all-to-all-start = ((bf16[32,128,128]{2,1,0:T(8,128)(2,1)}), bf16[32,128,128]{2,1,0:T(8,128)(2,1)S(1)}, u32[]{:S(2)}, u32[]{:S(2)}) async-start(bf16[32,128,128]{2,1,0:T(8,128)(2,1)} %pad_maximum_fusion.2), calls=%async_computation | async-start | bytes 2097152 | tf_op jit(solution)/shard_map/all_to_all | solution.py:696
  387.8 12.0 %qkv_back.1 = bf16[768,1024]{1,0:T(8,128)(2,1)} custom-call(bf16[768,1024]{1,0:T(8,128)(2,1)} %get-tuple-element.37.dq, bf16[768,1024]{1,0:T(8,128)(2,1)} %get-tuple-element.42.dk, bf16[768,1024]{1,0:T(8,128)(2,1)} %get-tuple-element.43.dv, bf16[768,256]{1,0:T(8,128)(2,1)} %get-tuple-element.44.dlow, bf16[768,1024]{1,0:T(8,128)(2,1)} %tok.5, ...), custom_call_target="tpu_custom_call" | custom-call | tf_op jit(solution)/shard_map/qkv_back/pallas_call | solution.py:673
  399.9 14.2 %all-to-all-done = bf16[32,128,128]{2,1,0:T(8,128)(2,1)S(1)} async-done(((bf16[32,128,128]{2,1,0:T(8,128)(2,1)}), bf16[32,128,128]{2,1,0:T(8,128)(2,1)S(1)}, u32[]{:S(2)}, u32[]{:S(2)}) %all-to-all-start) | async-done | bytes 1048608 | tf_op jit(solution)/shard_map/all_to_all | solution.py:696
  416.0 1.6 collective-permute-start.8
  418.2 4.1 collective-permute-done.8
  (100 shorter events, 26.4 us)
Async XLA Ops:
  7.2 16.8 %copy-start.7 = (bf16[128,1024]{1,0:T(8,128)(2,1)S(1)}, bf16[128,1024]{1,0:T(8,128)(2,1)}, u32[]{:S(2)}) copy-start(bf16[128,1024]{1,0:T(8,128)(2,1)} %param.44) | copy-start | bytes 786436
  7.2 16.8 %copy-start.11 = (bf16[32,1024]{1,0:T(8,128)(2,1)S(1)}, bf16[32,1024]{1,0:T(8,128)(2,1)}, u32[]{:S(2)}) copy-start(bf16[32,1024]{1,0:T(8,128)(2,1)} %param.38) | copy-start | bytes 196612
  7.2 16.8 %copy-start.8 = (bf16[32,4096]{1,0:T(8,128)(2,1)S(1)}, bf16[32,4096]{1,0:T(8,128)(2,1)}, u32[]{:S(2)}) copy-start(bf16[32,4096]{1,0:T(8,128)(2,1)} %param.42) | copy-start | bytes 786436
  7.2 16.9 %copy-start.12 = (bf16[128,128]{1,0:T(8,128)(2,1)S(1)}, bf16[128,128]{1,0:T(8,128)(2,1)}, u32[]{:S(2)}) copy-start(bf16[128,128]{1,0:T(8,128)(2,1)} %param.51) | copy-start | bytes 98308
  7.2 17.0 %copy-start.13 = (bf16[128,128]{1,0:T(8,128)(2,1)S(1)}, bf16[128,128]{1,0:T(8,128)(2,1)}, u32[]{:S(2)}) copy-start(bf16[128,128]{1,0:T(8,128)(2,1)} %param.52) | copy-start | bytes 98308
  7.2 96.8 %all-gather.3.cloned.1.call-start = ((), (), s32[]{:S(2)}) async-start(), calls=%async_computation.2 | async-start | bytes 8355840 | tf_op jit(solution)/shard_map/all_gather | solution.py:727
  14.1 8.9 %collective-permute-start.2 = (bf16[32,3840]{1,0:T(8,128)(2,1)S(1)}, bf16[32,3840]{1,0:T(8,128)(2,1)S(1)}, u32[]{:S(2)}, u32[]{:S(2)}) collective-permute-start(bf16[32,3840]{1,0:T(8,128)(2,1)S(1)} %constant_dynamic-update-slice_fusion), channel_id=1, source_target_pairs={{0,1},{1,0},{2,3},{3,2},{4,5},{5,4},{6,7},{7,6},{8,9},{9,8},{10,11... | collective-permute-start | bytes 737288 | tf_op jit(solution)/shard_map/ppermute | solution.py:725
  23.9 190.6 %all-gather.5.cloned.1.call-start = ((), (), s32[]{:S(2)}) async-start(), calls=%async_computation.3 | async-start | bytes 22282240 | tf_op jit(solution)/shard_map/all_gather | solution.py:727
  24.2 16.0 %collective-permute-start.3 = (bf16[320,1024]{1,0:T(8,128)(2,1)S(1)}, bf16[320,1024]{1,0:T(8,128)(2,1)S(1)}, u32[]{:S(2)}, u32[]{:S(2)}) collective-permute-start(bf16[320,1024]{1,0:T(8,128)(2,1)S(1)} %constant_dynamic-update-slice_fusion.12), channel_id=1, source_target_pairs={{0,1},{1,0},{2,3},{3,2},{4,5},{5,4},{6,7},{7,6},{8,9},{9,8},{10,11... | collective-permute-start | bytes 1966088 | tf_op jit(solution)/shard_map/ppermute | solution.py:725
  40.3 1.9 copy-start
  41.5 7.7 %copy-start.4 = (s32[24576]{0:T(1024)S(1)}, s32[24576]{0:T(1024)}, u32[]{:S(2)}) copy-start(s32[24576]{0:T(1024)} %param.29) | copy-start | bytes 294916
  41.5 22.1 %copy-start.14 = (s32[48]{0:T(128)S(1)}, s32[48]{0:T(128)}, u32[]{:S(2)}) copy-start(s32[48]{0:T(128)} %param.30) | copy-start | bytes 580
  41.5 372.7 %reduce-scatter.2.cloned.1.call-start = ((), (), s32[]{:S(2)}) async-start(), calls=%async_computation.4 | async-start | bytes 5570560 | tf_op jit(solution)/shard_map/reduce_scatter | solution.py:803
  43.5 46.9 %collective-permute-start = (bf16[640,1024]{1,0:T(8,128)(2,1)}, bf16[640,1024]{1,0:T(8,128)(2,1)}, u32[]{:S(2)}, u32[]{:S(2)}) collective-permute-start(bf16[640,1024]{1,0:T(8,128)(2,1)} %get-tuple-element.52), channel_id=1, source_target_pairs={{0,1},{1,2},{2,3},{3,4},{4,5},{5,6},{6,7},{7,8},{8,9},{9,10},{10,1... | collective-permute-start | bytes 3932168 | tf_op jit(solution)/shard_map/ppermute | solution.py:714
  47.9 42.9 %collective-permute-start.1 = (bf16[640,1024]{1,0:T(8,128)(2,1)S(1)}, bf16[640,1024]{1,0:T(8,128)(2,1)}, u32[]{:S(2)}, u32[]{:S(2)}) collective-permute-start(bf16[640,1024]{1,0:T(8,128)(2,1)S(1)} %get-tuple-element.53), channel_id=1, source_target_pairs={{1,0},{2,1},{3,2},{4,3},{5,4},{6,5},{7,6},{8,7},{9,8},{10,9},{11,1... | collective-permute-start | bytes 3932168 | tf_op jit(solution)/shard_map/ppermute | solution.py:715
  64.1 30.2 %copy-start.1 = (bf16[2048,128]{1,0:T(8,128)(2,1)}, bf16[2048,128]{1,0:T(8,128)(2,1)S(1)}, u32[]{:S(2)}) copy-start(bf16[2048,128]{1,0:T(8,128)(2,1)S(1)} %convolution_convert_fusion.sel) | copy-start | bytes 1572868
  275.7 5.0 %copy-start.5 = (f32[8,2,6,128]{3,2,1,0:T(8,128)S(1)}, f32[8,2,6,128]{3,2,1,0:T(8,128)}, u32[]{:S(2)}) copy-start(f32[8,2,6,128]{3,2,1,0:T(8,128)} %get-tuple-element.35.lse) | copy-start | bytes 147460
  275.7 5.0 %copy-start.6 = (f32[16,6,128]{2,1,0:T(8,128)S(1)}, f32[16,6,128]{2,1,0:T(8,128)}, u32[]{:S(2)}) copy-start(f32[16,6,128]{2,1,0:T(8,128)} %get-tuple-element.36) | copy-start | bytes 147460
  275.7 62.7 %collective-permute-start.4 = (bf16[640,1024]{1,0:T(8,128)(2,1)}, bf16[640,1024]{1,0:T(8,128)(2,1)S(1)}, u32[]{:S(2)}, u32[]{:S(2)}) collective-permute-start(bf16[640,1024]{1,0:T(8,128)(2,1)} %get-tuple-element.38), channel_id=1, source_target_pairs={{0,1},{1,2},{2,3},{3,4},{4,5},{5,6},{6,7},{7,8},{8,9},{9,10},{10,1... | collective-permute-start | bytes 3932168 | tf_op jit(solution)/shard_map/ppermute | solution.py:799
  279.3 59.1 %collective-permute-start.5 = (bf16[640,1024]{1,0:T(8,128)(2,1)}, bf16[640,1024]{1,0:T(8,128)(2,1)S(1)}, u32[]{:S(2)}, u32[]{:S(2)}) collective-permute-start(bf16[640,1024]{1,0:T(8,128)(2,1)} %get-tuple-element.39), channel_id=1, source_target_pairs={{1,0},{2,1},{3,2},{4,3},{5,4},{6,5},{7,6},{8,7},{9,8},{10,9},{11,1... | collective-permute-start | bytes 3932168 | tf_op jit(solution)/shard_map/ppermute | solution.py:800
  280.7 57.7 %collective-permute-start.7 = (f32[2,8,2,5,128]{4,3,2,1,0:T(8,128)S(1)}, f32[2,8,2,5,128]{4,3,2,1,0:T(8,128)S(1)}, u32[]{:S(2)}, u32[]{:S(2)}) collective-permute-start(f32[2,8,2,5,128]{4,3,2,1,0:T(8,128)S(1)} %get-tuple-element.70), channel_id=1, source_target_pairs={{1,0},{2,1},{3,2},{4,3},{5,4},{6,5},{7,6},{8,7},{9,8},{10,9},{11,1... | collective-permute-start | bytes 245768 | tf_op jit(solution)/shard_map/ppermute | solution.py:802
  282.0 56.4 %collective-permute-start.6 = (f32[2,8,2,5,128]{4,3,2,1,0:T(8,128)S(1)}, f32[2,8,2,5,128]{4,3,2,1,0:T(8,128)S(1)}, u32[]{:S(2)}, u32[]{:S(2)}) collective-permute-start(f32[2,8,2,5,128]{4,3,2,1,0:T(8,128)S(1)} %get-tuple-element.71), channel_id=1, source_target_pairs={{0,1},{1,2},{2,3},{3,4},{4,5},{5,6},{6,7},{7,8},{8,9},{9,10},{10,1... | collective-permute-start | bytes 245768 | tf_op jit(solution)/shard_map/ppermute | solution.py:801
  365.7 48.3 %all-to-all-start = ((bf16[32,128,128]{2,1,0:T(8,128)(2,1)}), bf16[32,128,128]{2,1,0:T(8,128)(2,1)S(1)}, u32[]{:S(2)}, u32[]{:S(2)}) async-start(bf16[32,128,128]{2,1,0:T(8,128)(2,1)} %pad_maximum_fusion.2), calls=%async_computation | async-start | bytes 2097152 | tf_op jit(solution)/shard_map/all_to_all | solution.py:696
  416.0 6.3 %collective-permute-start.8 = (f32[320,128]{1,0:T(8,128)S(1)}, f32[320,128]{1,0:T(8,128)S(1)}, u32[]{:S(2)}, u32[]{:S(2)}) collective-permute-start(f32[320,128]{1,0:T(8,128)S(1)} %select_bitcast_fusion.4), channel_id=1, source_target_pairs={{0,1},{1,0},{2,3},{3,2},{4,5},{5,4},{6,7},{7,6},{8,9},{9,8},{10,11... | collective-permute-start | bytes 491528 | tf_op jit(solution)/shard_map/ppermute | solution.py:814
  (4 other events, 4.0 us)
Sparse Core Ops, SparseCore 0:
  24.1 79.8 all-gather.2
  106.2 108.3 all-gather.4
  275.8 78.3 reduce-scatter.1

commit v5 on v4

--- a/solution.py
+++ b/solution.py
@@ -400,6 +400,7 @@
 
 
 FF_TILE = 512
+FF_ROWS = 768
 
 
 def mlp_kernel(
@@ -409,7 +410,7 @@
 ):
     j = pl.program_id(0)
     rows, width = mixed.shape
-    chunks = [pl.ds(r, TILE) for r in range(0, rows, TILE)]
+    chunks = [pl.ds(r, FF_ROWS) for r in range(0, rows, FF_ROWS)]
     up_in = w_lo[:, :LANES]
     down_out = w_lo[:, LANES:]
     out_w = w_out[...].reshape(width, width)
@@ -483,16 +484,16 @@
             dmix = dot_nt(dres.astype(bf16), out_w).astype(bf16)
             dmix_o[r, :] = dmix
             at = r.start
-            upper = min(HALO - at, TILE)
+            upper = min(HALO - at, FF_ROWS)
             head_o[at : at + upper, :] = dmix[:upper]
             skip = max(rows - HALO - at, 0)
             first = at + skip - (rows - HALO)
-            tail_o[first : first + TILE - skip, :] = dmix[skip:]
+            tail_o[first : first + FF_ROWS - skip, :] = dmix[skip:]
             prod = dmix.astype(f32) * mixed[r, :].astype(f32)
             high = prod.astype(bf16)
             rest = (prod - high.astype(f32)).astype(bf16)
             delta = dot_nt(heads[...], high) + dot_nt(heads[...], rest)
-            for part in range(TILE // LANES):
+            for part in range(FF_ROWS // LANES):
                 dlt_o[:, at // LANES + part, :] = delta[:, part * LANES : (part + 1) * LANES]
             gdo_t[...] += dot_nn(low_d.astype(f32).T.astype(bf16), dy[r, :])
             gui_t[...] += dot_nn(lu.astype(f32).T.astype(bf16), n2[r, :])

time: 431 us -> 429 us (level)
  no operation moved by 1% of the time
where the time goes in v5:
time: 429 us; the launch traced here: 428 us
  Pallas kernels  211 us (49%)
  waiting for transfers between devices  116 us (27%)
  starting transfers between devices  45.6 us (11%)
  between operations  27.4 us (6%)
  local copies, waits for them, and re-layouts  18.8 us (4%)
  other arithmetic  8.66 us (2%)
    pallas_call x1, Pallas kernels, mlp_call(): pl.pallas_call(mlp_kernel, grid=(hidden // FF_TILE,), in_specs=[full, ful...  58.9 us
    all_gather x2, waiting for transfers between devices, gather_twice(): return lax.all_gather(both, 'fsdp', axis=0, tiled=True)  53.8 us
    pallas_call x1, Pallas kernels, attend_back_call(): pl.pallas_call(attend_back_kernel, grid_spec=pltpu.PrefetchScalarGridSpec...  51.2 us
    pallas_call x1, Pallas kernels, attend_call(): pl.pallas_call(attend_kernel, grid_spec=pltpu.PrefetchScalarGridSpec(num_...  43.4 us
    ppermute x1, waiting for transfers between devices, local(): before = lax.ppermute(tokens[own - HALO:], AXES, up)  23.6 us
    all_to_all x1, starting transfers between devices, summed(): got = lax.all_to_all(packed, AXES, 0, 0, tiled=True)  22.1 us
    pallas_call x1, Pallas kernels, qkv_call(): pl.pallas_call(qkv_kernel, grid_spec=pltpu.PrefetchScalarGridSpec(num_sca...  21.8 us
    ppermute x2, waiting for transfers between devices, gather_twice(): theirs = lax.ppermute(mine, 'dp', [(0, 1), (1, 0)])  20.1 us
  transfers between devices with their start and end apart: 13, of which 8 were waited for; matrix products, arithmetic and copies ran while one was open for 3% of the time, Pallas kernels for 35%

profile of v5, /device:TPU:0, one launch (start us, length us, event | category | flops | bytes accessed | tf_op | source)
XLA Modules:
  0.0 427.9 jit_solution(11360077337062514671)
XLA Ops:
  14.1 3.0 collective-permute-start.2
  17.1 6.0 %collective-permute-done.2 = bf16[32,3840]{1,0:T(8,128)(2,1)S(1)} collective-permute-done((bf16[32,3840]{1,0:T(8,128)(2,1)S(1)}, bf16[32,3840]{1,0:T(8,128)(2,1)S(1)}, u32[]{:S(2)}, u32[]{:S(2)}) %collective-permute-start.2) | collective-permute-done | bytes 245792 | tf_op jit(solution)/shard_map/ppermute | solution.py:726
  24.2 1.8 collective-permute-start.3
  26.0 14.2 %collective-permute-done.3 = bf16[320,1024]{1,0:T(8,128)(2,1)S(1)} collective-permute-done((bf16[320,1024]{1,0:T(8,128)(2,1)S(1)}, bf16[320,1024]{1,0:T(8,128)(2,1)S(1)}, u32[]{:S(2)}, u32[]{:S(2)}) %collective-permute-start.3) | collective-permute-done | bytes 655392 | tf_op jit(solution)/shard_map/ppermute | solution.py:726
  42.2 1.3 fusion.10
  43.5 4.4 %collective-permute-start = (bf16[640,1024]{1,0:T(8,128)(2,1)}, bf16[640,1024]{1,0:T(8,128)(2,1)}, u32[]{:S(2)}, u32[]{:S(2)}) collective-permute-start(bf16[640,1024]{1,0:T(8,128)(2,1)} %get-tuple-element.52), channel_id=1, source_target_pairs={{0,1},{1,2},{2,3},{3,4},{4,5},{5,6},{6,7},{7,8},{8,9},{9,10},{10,1... | collective-permute-start | bytes 3932168 | tf_op jit(solution)/shard_map/ppermute | solution.py:715
  66.8 23.6 %collective-permute-done = bf16[640,1024]{1,0:T(8,128)(2,1)} collective-permute-done((bf16[640,1024]{1,0:T(8,128)(2,1)}, bf16[640,1024]{1,0:T(8,128)(2,1)}, u32[]{:S(2)}, u32[]{:S(2)}) %collective-permute-start) | collective-permute-done | bytes 1310752 | tf_op jit(solution)/shard_map/ppermute | solution.py:715
  90.8 3.5 pad_maximum_fusion.tok
  94.3 9.7 %all-gather.3.cloned.1.call-done = bf16[32,32,3840]{2,1,0:T(8,128)(2,1)} async-done(((bf16[2,32,3840]{2,1,0:T(8,128)(2,1)}), bf16[32,32,3840]{2,1,0:T(8,128)(2,1)}) %all-gather.3.cloned.1.call-update) | async-done | bytes 7864336 | tf_op jit(solution)/shard_map/all_gather | solution.py:728
  104.0 21.8 %qkv.1 = (bf16[2048,1024]{1,0:T(8,128)(2,1)}, bf16[2048,1024]{1,0:T(8,128)(2,1)}, bf16[2048,1024]{1,0:T(8,128)(2,1)}) custom-call(s32[14]{0:T(128)} %stack.79.tab, bf16[2048,1024]{1,0:T(8,128)(2,1)} %pad_maximum_fusion.tok, bf16[2048,128]{1,0:T(8,128)(2,1)} %copy-done.1, bf16[1024,3840]{1,0:T(8,128)(2,1)} %bitcast.57, f32[1,1024]{1,0:T(1,128)} %bitcast.79, ...), custom_call_target="tpu_custom_call" | custom-call | tf_op jit(solution)/shard_map/qkv/pallas_call | solution.py:107
  127.0 43.4 %attend.1 = (bf16[768,1024]{1,0:T(8,128)(2,1)}, f32[8,2,6,128]{3,2,1,0:T(8,128)}) custom-call(s32[14]{0:T(128)} %stack.79.tab, bf16[2048,1024]{1,0:T(8,128)(2,1)} %get-tuple-element.29.q, bf16[2048,1024]{1,0:T(8,128)(2,1)} %get-tuple-element.30.k, bf16[2048,1024]{1,0:T(8,128)(2,1)} %get-tuple-element.31.v, s32[2048,128]{1,0:T(8,128)} %broadcast_in_dim.8.segc, ...), custom_call_target="tpu_custom_call" | custom-call | tf_op jit(solution)/shard_map/attend/pallas_call | solution.py:203
  170.4 44.1 %all-gather.5.cloned.1.call-done.w_out.w_up.w_dn.w_x = bf16[32,320,1024]{2,1,0:T(8,128)(2,1)} async-done(((bf16[2,320,1024]{2,1,0:T(8,128)(2,1)}), bf16[32,320,1024]{2,1,0:T(8,128)(2,1)}) %all-gather.5.cloned.1.call-update) | async-done | bytes 20971536 | tf_op jit(solution)/shard_map/all_gather | solution.py:728
  214.5 58.9 %mlp.1 = (bf16[768,1024]{1,0:T(8,128)(2,1)}, f32[768,1024]{1,0:T(8,128)}, bf16[768,1024]{1,0:T(8,128)(2,1)}, bf16[640,1024]{1,0:T(8,128)(2,1)}, bf16[640,1024]{1...) custom-call(bf16[768,1024]{1,0:T(8,128)(2,1)} %get-tuple-element.32.mixed, bf16[768,1024]{1,0:T(8,128)(2,1)} %tok.5, ...), custom_call_target="tpu_custom_call" | custom-call | tf_op jit(solution)/shard_map/mlp/pallas_call | solution.py:537
  273.5 3.6 collective-permute-start.4
  277.1 1.3 collective-permute-start.5
  279.8 5.2 %collective-permute-start.6 = (f32[2,8,2,5,128]{4,3,2,1,0:T(8,128)S(1)}, f32[2,8,2,5,128]{4,3,2,1,0:T(8,128)S(1)}, u32[]{:S(2)}, u32[]{:S(2)}) collective-permute-start(f32[2,8,2,5,128]{4,3,2,1,0:T(8,128)S(1)} %get-tuple-element.71), channel_id=1, source_target_pairs={{0,1},{1,2},{2,3},{3,4},{4,5},{5,6},{6,7},{7,8},{8,9},{9,10},{10,1... | collective-permute-start | bytes 245768 | tf_op jit(solution)/shard_map/ppermute | solution.py:802
  285.0 51.2 %attend_back.1 = (bf16[768,1024]{1,0:T(8,128)(2,1)}, f32[768,1024]{1,0:T(8,128)}, f32[768,1024]{1,0:T(8,128)}) custom-call(s32[14]{0:T(128)} %stack.79.tab, bf16[2048,1024]{1,0:T(8,128)(2,1)} %get-tuple-element.29.q, bf16[2048,1024]{1,0:T(8,128)(2,1)} %get-tuple-element.30.k, bf16[2048,1024]{1,0:T(8,128)(2,1)} %get-tuple-element.31.v, ...), custom_call_target="tpu_custom_call" | custom-call | tf_op jit(solution)/shard_map/attend_back/pallas_call | solution.py:300
  337.8 15.8 %halo_back.1 = (bf16[768,1024]{1,0:T(8,128)(2,1)}, bf16[768,1024]{1,0:T(8,128)(2,1)}) custom-call(s32[14]{0:T(128)} %stack.79.tab, bf16[2048,1024]{1,0:T(8,128)(2,1)} %get-tuple-element.29.q, bf16[2048,1024]{1,0:T(8,128)(2,1)} %get-tuple-element.30.k, bf16[2048,1024]{1,0:T(8,128)(2,1)} %get-tuple-element.31.v, bf16[640,1024]{1,0:T(8,128)(2,1)} %copy-done.2, ...), custom_call_target="tpu_custom_call" | custom-call | tf_op jit(solution)/shard_map/halo_back/pallas_call | solution.py:375
  353.6 7.5 %low_back.1 = (bf16[768,256]{1,0:T(8,128)(2,1)}, bf16[4,1024,128]{2,1,0:T(8,128)(2,1)}) custom-call(bf16[768,1024]{1,0:T(8,128)(2,1)} %get-tuple-element.37.dq, bf16[768,1024]{1,0:T(8,128)(2,1)} %get-tuple-element.43.dv, bf16[768,1024]{1,0:T(8,128)(2,1)} %tok.5, bf16[768,128]{1,0:T(8,128)(2,1)} %slice.197.sel, bf16[1024,3840]{1,0:T(8,128)(2,1)} %bitcast.59, ...), custom_call_target="tpu_custom_call" | custom-call | tf_op jit(solution)/shard_map/low_back/pallas_call | solution.py:632
  363.5 22.1 %all-to-all-start = ((bf16[32,128,128]{2,1,0:T(8,128)(2,1)}), bf16[32,128,128]{2,1,0:T(8,128)(2,1)S(1)}, u32[]{:S(2)}, u32[]{:S(2)}) async-start(bf16[32,128,128]{2,1,0:T(8,128)(2,1)} %pad_maximum_fusion.2), calls=%async_computation | async-start | bytes 2097152 | tf_op jit(solution)/shard_map/all_to_all | solution.py:697
  385.6 12.0 %qkv_back.1 = bf16[768,1024]{1,0:T(8,128)(2,1)} custom-call(bf16[768,1024]{1,0:T(8,128)(2,1)} %get-tuple-element.37.dq, bf16[768,1024]{1,0:T(8,128)(2,1)} %get-tuple-element.42.dk, bf16[768,1024]{1,0:T(8,128)(2,1)} %get-tuple-element.43.dv, bf16[768,256]{1,0:T(8,128)(2,1)} %get-tuple-element.44.dlow, bf16[768,1024]{1,0:T(8,128)(2,1)} %tok.5, ...), custom_call_target="tpu_custom_call" | custom-call | tf_op jit(solution)/shard_map/qkv_back/pallas_call | solution.py:674
  397.7 14.2 %all-to-all-done = bf16[32,128,128]{2,1,0:T(8,128)(2,1)S(1)} async-done(((bf16[32,128,128]{2,1,0:T(8,128)(2,1)}), bf16[32,128,128]{2,1,0:T(8,128)(2,1)S(1)}, u32[]{:S(2)}, u32[]{:S(2)}) %all-to-all-start) | async-done | bytes 1048608 | tf_op jit(solution)/shard_map/all_to_all | solution.py:697
  413.8 1.6 collective-permute-start.8
  416.0 4.1 collective-permute-done.8
  (100 shorter events, 26.4 us)
Async XLA Ops:
  7.2 16.8 %copy-start.7 = (bf16[128,1024]{1,0:T(8,128)(2,1)S(1)}, bf16[128,1024]{1,0:T(8,128)(2,1)}, u32[]{:S(2)}) copy-start(bf16[128,1024]{1,0:T(8,128)(2,1)} %param.44) | copy-start | bytes 786436
  7.2 16.8 %copy-start.11 = (bf16[32,1024]{1,0:T(8,128)(2,1)S(1)}, bf16[32,1024]{1,0:T(8,128)(2,1)}, u32[]{:S(2)}) copy-start(bf16[32,1024]{1,0:T(8,128)(2,1)} %param.38) | copy-start | bytes 196612
  7.2 16.8 %copy-start.8 = (bf16[32,4096]{1,0:T(8,128)(2,1)S(1)}, bf16[32,4096]{1,0:T(8,128)(2,1)}, u32[]{:S(2)}) copy-start(bf16[32,4096]{1,0:T(8,128)(2,1)} %param.42) | copy-start | bytes 786436
  7.2 16.9 %copy-start.12 = (bf16[128,128]{1,0:T(8,128)(2,1)S(1)}, bf16[128,128]{1,0:T(8,128)(2,1)}, u32[]{:S(2)}) copy-start(bf16[128,128]{1,0:T(8,128)(2,1)} %param.51) | copy-start | bytes 98308
  7.2 17.0 %copy-start.13 = (bf16[128,128]{1,0:T(8,128)(2,1)S(1)}, bf16[128,128]{1,0:T(8,128)(2,1)}, u32[]{:S(2)}) copy-start(bf16[128,128]{1,0:T(8,128)(2,1)} %param.52) | copy-start | bytes 98308
  7.2 96.8 %all-gather.3.cloned.1.call-start = ((), (), s32[]{:S(2)}) async-start(), calls=%async_computation.2 | async-start | bytes 8355840 | tf_op jit(solution)/shard_map/all_gather | solution.py:728
  14.1 8.9 %collective-permute-start.2 = (bf16[32,3840]{1,0:T(8,128)(2,1)S(1)}, bf16[32,3840]{1,0:T(8,128)(2,1)S(1)}, u32[]{:S(2)}, u32[]{:S(2)}) collective-permute-start(bf16[32,3840]{1,0:T(8,128)(2,1)S(1)} %constant_dynamic-update-slice_fusion), channel_id=1, source_target_pairs={{0,1},{1,0},{2,3},{3,2},{4,5},{5,4},{6,7},{7,6},{8,9},{9,8},{10,11... | collective-permute-start | bytes 737288 | tf_op jit(solution)/shard_map/ppermute | solution.py:726
  23.9 190.6 %all-gather.5.cloned.1.call-start = ((), (), s32[]{:S(2)}) async-start(), calls=%async_computation.3 | async-start | bytes 22282240 | tf_op jit(solution)/shard_map/all_gather | solution.py:728
  24.2 16.0 %collective-permute-start.3 = (bf16[320,1024]{1,0:T(8,128)(2,1)S(1)}, bf16[320,1024]{1,0:T(8,128)(2,1)S(1)}, u32[]{:S(2)}, u32[]{:S(2)}) collective-permute-start(bf16[320,1024]{1,0:T(8,128)(2,1)S(1)} %constant_dynamic-update-slice_fusion.12), channel_id=1, source_target_pairs={{0,1},{1,0},{2,3},{3,2},{4,5},{5,4},{6,7},{7,6},{8,9},{9,8},{10,11... | collective-permute-start | bytes 1966088 | tf_op jit(solution)/shard_map/ppermute | solution.py:726
  40.3 1.9 copy-start
  41.5 7.7 %copy-start.4 = (s32[24576]{0:T(1024)S(1)}, s32[24576]{0:T(1024)}, u32[]{:S(2)}) copy-start(s32[24576]{0:T(1024)} %param.29) | copy-start | bytes 294916
  41.5 22.1 %copy-start.14 = (s32[48]{0:T(128)S(1)}, s32[48]{0:T(128)}, u32[]{:S(2)}) copy-start(s32[48]{0:T(128)} %param.30) | copy-start | bytes 580
  41.5 370.5 %reduce-scatter.2.cloned.1.call-start = ((), (), s32[]{:S(2)}) async-start(), calls=%async_computation.4 | async-start | bytes 5570560 | tf_op jit(solution)/shard_map/reduce_scatter | solution.py:804
  43.5 46.9 %collective-permute-start = (bf16[640,1024]{1,0:T(8,128)(2,1)}, bf16[640,1024]{1,0:T(8,128)(2,1)}, u32[]{:S(2)}, u32[]{:S(2)}) collective-permute-start(bf16[640,1024]{1,0:T(8,128)(2,1)} %get-tuple-element.52), channel_id=1, source_target_pairs={{0,1},{1,2},{2,3},{3,4},{4,5},{5,6},{6,7},{7,8},{8,9},{9,10},{10,1... | collective-permute-start | bytes 3932168 | tf_op jit(solution)/shard_map/ppermute | solution.py:715
  47.9 42.9 %collective-permute-start.1 = (bf16[640,1024]{1,0:T(8,128)(2,1)S(1)}, bf16[640,1024]{1,0:T(8,128)(2,1)}, u32[]{:S(2)}, u32[]{:S(2)}) collective-permute-start(bf16[640,1024]{1,0:T(8,128)(2,1)S(1)} %get-tuple-element.53), channel_id=1, source_target_pairs={{1,0},{2,1},{3,2},{4,3},{5,4},{6,5},{7,6},{8,7},{9,8},{10,9},{11,1... | collective-permute-start | bytes 3932168 | tf_op jit(solution)/shard_map/ppermute | solution.py:716
  64.1 30.2 %copy-start.1 = (bf16[2048,128]{1,0:T(8,128)(2,1)}, bf16[2048,128]{1,0:T(8,128)(2,1)S(1)}, u32[]{:S(2)}) copy-start(bf16[2048,128]{1,0:T(8,128)(2,1)S(1)} %convolution_convert_fusion.sel) | copy-start | bytes 1572868
  273.5 4.9 %copy-start.5 = (f32[8,2,6,128]{3,2,1,0:T(8,128)S(1)}, f32[8,2,6,128]{3,2,1,0:T(8,128)}, u32[]{:S(2)}) copy-start(f32[8,2,6,128]{3,2,1,0:T(8,128)} %get-tuple-element.35.lse) | copy-start | bytes 147460
  273.5 4.9 %copy-start.6 = (f32[16,6,128]{2,1,0:T(8,128)S(1)}, f32[16,6,128]{2,1,0:T(8,128)}, u32[]{:S(2)}) copy-start(f32[16,6,128]{2,1,0:T(8,128)} %get-tuple-element.36) | copy-start | bytes 147460
  273.5 62.7 %collective-permute-start.4 = (bf16[640,1024]{1,0:T(8,128)(2,1)}, bf16[640,1024]{1,0:T(8,128)(2,1)S(1)}, u32[]{:S(2)}, u32[]{:S(2)}) collective-permute-start(bf16[640,1024]{1,0:T(8,128)(2,1)} %get-tuple-element.38), channel_id=1, source_target_pairs={{0,1},{1,2},{2,3},{3,4},{4,5},{5,6},{6,7},{7,8},{8,9},{9,10},{10,1... | collective-permute-start | bytes 3932168 | tf_op jit(solution)/shard_map/ppermute | solution.py:800
  277.1 59.1 %collective-permute-start.5 = (bf16[640,1024]{1,0:T(8,128)(2,1)}, bf16[640,1024]{1,0:T(8,128)(2,1)S(1)}, u32[]{:S(2)}, u32[]{:S(2)}) collective-permute-start(bf16[640,1024]{1,0:T(8,128)(2,1)} %get-tuple-element.39), channel_id=1, source_target_pairs={{1,0},{2,1},{3,2},{4,3},{5,4},{6,5},{7,6},{8,7},{9,8},{10,9},{11,1... | collective-permute-start | bytes 3932168 | tf_op jit(solution)/shard_map/ppermute | solution.py:801
  278.5 57.7 %collective-permute-start.7 = (f32[2,8,2,5,128]{4,3,2,1,0:T(8,128)S(1)}, f32[2,8,2,5,128]{4,3,2,1,0:T(8,128)S(1)}, u32[]{:S(2)}, u32[]{:S(2)}) collective-permute-start(f32[2,8,2,5,128]{4,3,2,1,0:T(8,128)S(1)} %get-tuple-element.70), channel_id=1, source_target_pairs={{1,0},{2,1},{3,2},{4,3},{5,4},{6,5},{7,6},{8,7},{9,8},{10,9},{11,1... | collective-permute-start | bytes 245768 | tf_op jit(solution)/shard_map/ppermute | solution.py:803
  279.8 56.4 %collective-permute-start.6 = (f32[2,8,2,5,128]{4,3,2,1,0:T(8,128)S(1)}, f32[2,8,2,5,128]{4,3,2,1,0:T(8,128)S(1)}, u32[]{:S(2)}, u32[]{:S(2)}) collective-permute-start(f32[2,8,2,5,128]{4,3,2,1,0:T(8,128)S(1)} %get-tuple-element.71), channel_id=1, source_target_pairs={{0,1},{1,2},{2,3},{3,4},{4,5},{5,6},{6,7},{7,8},{8,9},{9,10},{10,1... | collective-permute-start | bytes 245768 | tf_op jit(solution)/shard_map/ppermute | solution.py:802
  363.5 48.3 %all-to-all-start = ((bf16[32,128,128]{2,1,0:T(8,128)(2,1)}), bf16[32,128,128]{2,1,0:T(8,128)(2,1)S(1)}, u32[]{:S(2)}, u32[]{:S(2)}) async-start(bf16[32,128,128]{2,1,0:T(8,128)(2,1)} %pad_maximum_fusion.2), calls=%async_computation | async-start | bytes 2097152 | tf_op jit(solution)/shard_map/all_to_all | solution.py:697
  413.8 6.3 %collective-permute-start.8 = (f32[320,128]{1,0:T(8,128)S(1)}, f32[320,128]{1,0:T(8,128)S(1)}, u32[]{:S(2)}, u32[]{:S(2)}) collective-permute-start(f32[320,128]{1,0:T(8,128)S(1)} %select_bitcast_fusion.4), channel_id=1, source_target_pairs={{0,1},{1,0},{2,3},{3,2},{4,5},{5,4},{6,7},{7,6},{8,9},{9,8},{10,11... | collective-permute-start | bytes 491528 | tf_op jit(solution)/shard_map/ppermute | solution.py:815
  (4 other events, 4.0 us)
Sparse Core Ops, SparseCore 0:
  24.1 79.8 all-gather.2
  106.2 108.3 all-gather.4
  273.6 78.3 reduce-scatter.1
